TPU v7x, 32 devices: a whole 2x2x4 slice. The times are simulated.
32 devices in a mesh: expert: 8 (over y, x, core), tensor: 4 (over z).
Axes of the slice: x: 2, y: 2, z: 4, core: 2. Of those that a mesh axis runs over, the one named last changes fastest.
Arguments:
- inputs: float32 [7880, 512], P('expert'), may hold values from -6 to 6
- cotangent: float32 [7880, 512], P('expert'), may hold values from -6 to 6
- routes: int32 [2, 7880, 2], P(None, 'expert'), may hold values from 0 to 7, all different within a row
- priority: int32 [2, 7880], P(None, 'expert'), may hold values from 0 to 984, as said below
- attend_in: float32 [2, 3, 512, 512], P(None, None, 'expert', 'tensor'), may hold values from -0.375 to 0.375
- attend_out: float32 [2, 512, 512], P(None, 'tensor', 'expert'), may hold values from -1.5 to 1.5
- router: float32 [2, 512, 8], P(None, None, 'expert'), may hold values from -0.1875 to 0.1875
- norm_gains: float32 [2, 2, 512], P(None, None, 'expert'), may hold values from 0.25 to 1.75
- expert_in: float32 [2, 8, 512, 2048], P(None, 'expert', None, 'tensor'), may hold values from -0.25 to 0.25
- expert_out: float32 [2, 8, 2048, 512], P(None, 'expert', 'tensor'), may hold values from -0.5 to 0.5
Outputs:
- outputs: float32 [7880, 512], P('expert')
- input_grad: float32 [7880, 512], P('expert')
- attend_in_grad: float32 [2, 3, 512, 512], P(None, None, 'expert', 'tensor')
- attend_out_grad: float32 [2, 512, 512], P(None, 'tensor', 'expert')
- router_grad: float32 [2, 512, 8], P(None, None, 'expert')
- gains_grad: float32 [2, 2, 512], P(None, None, 'expert')
- expert_in_grad: float32 [2, 8, 512, 2048], P(None, 'expert', None, 'tensor')
- expert_out_grad: float32 [2, 8, 2048, 512], P(None, 'expert', 'tensor')
Inputs may be any that keep to these rules, and one draw needn't show every extreme that they name: `routes`: in each block each token names two different experts, and every expert is named by some token. `priority`: in each block, the values within each device's 985 tokens are a permutation.
All inputs are finite; a program needn't handle non-finite values.
Results may differ from a plain program's by a relative error of at most 0.025.
The roundings to bfloat16 on the way count: a program that leaves them out, or rounds other values in their place, can miss the bound.
Values may be sent and summed in bfloat16 or wider, within the bound.
A program may use at most 192 MiB of HBM per device.

v0:
```python
import jax
import jax.numpy as jnp
from jax import lax
from jax.sharding import PartitionSpec as P

HEAD_DIM = 64
SEQ = 197


def norm_rows(rows_in, gain_row):
    centred = rows_in - jnp.mean(rows_in, axis=-1, keepdims=True)
    spread = jnp.mean(centred * centred, axis=-1, keepdims=True)
    return centred * lax.rsqrt(spread + 1e-06) * gain_row


def gelu_exact(rows_in):
    return 0.5 * rows_in * (1.0 + lax.erf(rows_in * 0.7071067811865476))


def contract_rows(left_side, right_side):
    return lax.dot_general(
        left_side, right_side, (((0,), (0,)), ((), ())), preferred_element_type=jnp.float32
    )


def contract_last(left_side, right_side):
    return lax.dot_general(
        left_side, right_side, (((1,), (1,)), ((), ())), preferred_element_type=jnp.float32
    )


def heads_total(partial_sum):
    return lax.psum(partial_sum, "tensor")


def to_experts(make_rows, model_width):
    return lax.all_to_all(
        make_rows(0, model_width), "expert", split_axis=0, concat_axis=0, tiled=True
    )


def to_sources(partial_rows):
    shares = lax.psum_scatter(partial_rows, "tensor", scatter_dimension=2, tiled=True)
    moved = lax.all_to_all(
        shares.astype(jnp.bfloat16), "expert", split_axis=0, concat_axis=0, tiled=True
    )
    return lax.all_gather(moved, "tensor", axis=2, tiled=True)


def slot_plan(chosen, rank_rows, experts, capacity):
    columns = lax.broadcasted_iota(jnp.int32, (1, experts), 1)
    first_hot = (chosen[:, 0:1] == columns).astype(jnp.bfloat16)
    second = (chosen[:, 1:2] == columns).astype(jnp.bfloat16)
    earlier = (rank_rows[None, :] < rank_rows[:, None]).astype(jnp.bfloat16)
    count_first = jnp.dot(earlier, first_hot, preferred_element_type=jnp.float32)
    count_second = jnp.dot(earlier, second, preferred_element_type=jnp.float32)
    first_f = first_hot.astype(jnp.float32)
    second_f = second.astype(jnp.float32)
    filled = jnp.sum(first_f, axis=0, keepdims=True)
    slot_first = jnp.sum(count_first * first_f, axis=1)
    slot_second = jnp.sum((filled + count_second) * second_f, axis=1)
    slot_nums = jnp.stack([slot_first, slot_second], axis=1).astype(jnp.int32)
    target = jnp.where(slot_nums < capacity, chosen * capacity + slot_nums, experts * capacity)
    return (target, first_f, second_f)


def local(
    inputs,
    cotangent,
    routes,
    priority,
    attend_in,
    attend_out,
    router,
    norm_gains,
    expert_in,
    expert_out,
):
    experts = lax.axis_size("expert")
    tokens = inputs.shape[0]
    model_width = inputs.shape[1]
    images = tokens // SEQ
    local_heads = attend_in.shape[3] // HEAD_DIM
    layers = attend_in.shape[0]
    capacity = max(2, (10 * tokens + 4 * experts - 1) // (4 * experts))
    slots_all = experts * capacity
    score_scale = HEAD_DIM ** (-0.5)
    in_full, out_full, router_full, gains_full = (
        lax.all_gather(attend_in.astype(jnp.bfloat16), "expert", axis=2, tiled=True),
        lax.all_gather(attend_out.astype(jnp.bfloat16), "expert", axis=2, tiled=True),
        lax.all_gather(router.astype(jnp.bfloat16), "expert", axis=2, tiled=True),
        lax.all_gather(norm_gains.astype(jnp.bfloat16), "expert", axis=2, tiled=True),
    )
    slot_ids = lax.broadcasted_iota(jnp.int32, (1, slots_all), 1)
    stream = inputs
    stash_list = []
    for layer_index in range(layers):
        gains_now = gains_full[layer_index].astype(jnp.float32)
        normed = norm_rows(stream, gains_now[0]).astype(jnp.bfloat16)
        project = in_full[layer_index]
        triple = jnp.einsum(
            "td,jdh->jth", normed, project, preferred_element_type=jnp.float32
        ).astype(jnp.bfloat16)
        shaped = triple.reshape(3, images, SEQ, local_heads, HEAD_DIM)
        scores = (
            jnp.einsum("iqhd,ikhd->ihqk", shaped[0], shaped[1], preferred_element_type=jnp.float32)
            * score_scale
        )
        log_total = jax.nn.logsumexp(scores, axis=-1, keepdims=True)
        attention = jnp.exp(scores - log_total).astype(jnp.bfloat16)
        mixed_heads = (
            jnp.einsum("ihqk,ikhd->iqhd", attention, shaped[2], preferred_element_type=jnp.float32)
            .astype(jnp.bfloat16)
            .reshape(tokens, -1)
        )
        middle = stream + heads_total(
            jnp.dot(mixed_heads, out_full[layer_index], preferred_element_type=jnp.float32)
        )
        normed_two = norm_rows(middle, gains_now[1]).astype(jnp.bfloat16)
        logits = jnp.dot(normed_two, router_full[layer_index], preferred_element_type=jnp.float32)
        probs_all = jax.nn.softmax(logits, axis=-1)
        chosen = routes[layer_index]
        gate_values = jnp.take_along_axis(probs_all, chosen, axis=1)
        target, first_f, second_f = slot_plan(chosen, priority[layer_index], experts, capacity)
        pick_first = (target[:, 0:1] == slot_ids).astype(jnp.bfloat16)
        pick_second = (target[:, 1:2] == slot_ids).astype(jnp.bfloat16)
        pick_both = pick_first + pick_second

        def dispatch_rows(first_col, col_count, normed_two=normed_two, pick_both=pick_both):
            return (
                contract_rows(pick_both, normed_two)
                .astype(jnp.bfloat16)
                .reshape(experts, capacity, col_count)
            )

        arrived = to_experts(dispatch_rows, model_width).reshape(slots_all, model_width)
        win_now = expert_in[layer_index, 0].astype(jnp.bfloat16)
        wout_now = expert_out[layer_index, 0].astype(jnp.bfloat16)
        before = jnp.dot(arrived, win_now, preferred_element_type=jnp.float32)
        hidden = gelu_exact(before).astype(jnp.bfloat16)
        expert_rows = jnp.dot(hidden, wout_now, preferred_element_type=jnp.float32).reshape(
            experts, capacity, model_width
        )
        returned = to_sources(expert_rows).reshape(slots_all, model_width)
        rows_first = jnp.dot(pick_first, returned, preferred_element_type=jnp.float32)
        rows_second = jnp.dot(pick_second, returned, preferred_element_type=jnp.float32)
        output = middle + gate_values[:, 0:1] * rows_first + gate_values[:, 1:2] * rows_second
        kept_pre = None
        stash_list.append(
            (
                stream,
                gains_now,
                normed,
                shaped,
                log_total,
                mixed_heads,
                middle,
                normed_two,
                probs_all,
                gate_values,
                target,
                first_f,
                second_f,
                pick_first,
                pick_second,
                pick_both,
                arrived,
                rows_first,
                rows_second,
                kept_pre,
            )
        )
        stream = output
    upstream = cotangent
    grads_in, grads_out, grads_router, grads_gain, grads_win, grads_wout = ([], [], [], [], [], [])
    for layer_index in reversed(range(layers)):
        (
            stream_in,
            gains_now,
            normed,
            shaped,
            log_total,
            mixed_heads,
            middle,
            normed_two,
            probs_all,
            gate_values,
            target,
            first_f,
            second_f,
            pick_first,
            pick_second,
            pick_both,
            arrived,
            rows_first,
            rows_second,
            kept_pre,
        ) = stash_list[layer_index]
        win_now = expert_in[layer_index, 0].astype(jnp.bfloat16)
        wout_now = expert_out[layer_index, 0].astype(jnp.bfloat16)
        gate_first = jnp.sum(upstream * rows_first, axis=1)
        gate_second = jnp.sum(upstream * rows_second, axis=1)
        scaled = jnp.concatenate(
            [
                gate_values[:, 0:1] * upstream,
                gate_values[:, 1:2] * upstream,
                jnp.zeros((1, model_width), jnp.float32),
            ],
            axis=0,
        )
        owners = (
            jnp.full((slots_all + 1,), 2 * tokens, jnp.int32)
            .at[jnp.concatenate([target[:, 0], target[:, 1]])]
            .set(jnp.arange(2 * tokens, dtype=jnp.int32))[:slots_all]
        )

        def gradient_rows(first_col, col_count, scaled=scaled, owners=owners):
            return (
                jnp.take(scaled, owners, axis=0)
                .astype(jnp.bfloat16)
                .reshape(experts, capacity, col_count)
            )

        grad_arrived = to_experts(gradient_rows, model_width).reshape(slots_all, model_width)
        before = jnp.dot(arrived, win_now, preferred_element_type=jnp.float32)
        hidden = gelu_exact(before).astype(jnp.bfloat16)
        grads_wout.append(contract_rows(hidden, grad_arrived))
        grad_hidden = contract_last(grad_arrived, wout_now)
        grad_before = jax.vjp(gelu_exact, before)[1](grad_hidden)[0].astype(jnp.bfloat16)
        grads_win.append(contract_rows(arrived, grad_before))
        grad_rows = contract_last(grad_before, win_now).reshape(experts, capacity, model_width)
        grad_dispatched = to_sources(grad_rows).reshape(slots_all, model_width)
        grad_normed = jnp.dot(pick_both, grad_dispatched, preferred_element_type=jnp.float32)
        grad_probs = first_f * gate_first[:, None] + second_f * gate_second[:, None]
        grad_logits = (
            probs_all * (grad_probs - jnp.sum(probs_all * grad_probs, axis=1, keepdims=True))
        ).astype(jnp.bfloat16)
        grads_router.append(contract_rows(normed_two, grad_logits))
        grad_normed = grad_normed + contract_last(grad_logits, router_full[layer_index])
        norm_back = jax.vjp(norm_rows, middle, gains_now[1])[1](grad_normed)
        grad_middle = upstream + norm_back[0]
        grad_branch = grad_middle.astype(jnp.bfloat16)
        grads_out.append(contract_rows(mixed_heads, grad_branch))
        grad_mixed = (
            contract_last(grad_branch, out_full[layer_index])
            .astype(jnp.bfloat16)
            .reshape(images, SEQ, local_heads, HEAD_DIM)
        )
        scores = (
            jnp.einsum("iqhd,ikhd->ihqk", shaped[0], shaped[1], preferred_element_type=jnp.float32)
            * score_scale
        )
        attention_f = jnp.exp(scores - log_total)
        attention = attention_f.astype(jnp.bfloat16)
        grad_value = jnp.einsum(
            "ihqk,iqhd->ikhd", attention, grad_mixed, preferred_element_type=jnp.float32
        ).astype(jnp.bfloat16)
        grad_attention = jnp.einsum(
            "iqhd,ikhd->ihqk", grad_mixed, shaped[2], preferred_element_type=jnp.float32
        )
        grad_scores = (
            attention_f
            * (grad_attention - jnp.sum(attention_f * grad_attention, axis=-1, keepdims=True))
        ).astype(jnp.bfloat16)
        grad_query = (
            jnp.einsum(
                "ihqk,ikhd->iqhd", grad_scores, shaped[1], preferred_element_type=jnp.float32
            )
            * score_scale
        ).astype(jnp.bfloat16)
        grad_key = (
            jnp.einsum(
                "ihqk,iqhd->ikhd", grad_scores, shaped[0], preferred_element_type=jnp.float32
            )
            * score_scale
        ).astype(jnp.bfloat16)
        grad_triple = jnp.stack([grad_query, grad_key, grad_value]).reshape(3, tokens, -1)
        grads_in.append(
            jnp.einsum("td,jth->jdh", normed, grad_triple, preferred_element_type=jnp.float32)
        )
        project = in_full[layer_index]
        grad_normed_one = heads_total(
            jnp.einsum("jth,jdh->td", grad_triple, project, preferred_element_type=jnp.float32)
        )
        norm_back_one = jax.vjp(norm_rows, stream_in, gains_now[0])[1](grad_normed_one)
        grads_gain.append(jnp.stack([norm_back_one[1], norm_back[1]]))
        upstream = grad_middle + norm_back_one[0]
    in_grad_all = jnp.stack(grads_in[::-1])
    out_grad_all = jnp.stack(grads_out[::-1])
    router_grad_all = jnp.stack(grads_router[::-1])
    gain_grad_all = jnp.stack(grads_gain[::-1])
    reduced = (
        lax.psum_scatter(in_grad_all, "expert", scatter_dimension=2, tiled=True),
        lax.psum_scatter(out_grad_all, "expert", scatter_dimension=2, tiled=True),
        lax.psum_scatter(router_grad_all, "expert", scatter_dimension=2, tiled=True),
        lax.psum_scatter(gain_grad_all, "expert", scatter_dimension=2, tiled=True),
    )
    win_grad_all = jnp.stack(grads_win[::-1])[:, None]
    wout_grad_all = jnp.stack(grads_wout[::-1])[:, None]
    return (
        stream,
        upstream,
        reduced[0],
        reduced[1],
        reduced[2],
        reduced[3],
        win_grad_all,
        wout_grad_all,
    )


def solution(mesh):
    placed = (
        P("expert", None),
        P("expert", None),
        P(None, "expert", None),
        P(None, "expert"),
        P(None, None, "expert", "tensor"),
        P(None, "tensor", "expert"),
        P(None, None, "expert"),
        P(None, None, "expert"),
        P(None, "expert", None, "tensor"),
        P(None, "expert", "tensor", None),
    )
    return jax.shard_map(
        local,
        mesh=mesh,
        in_specs=placed,
        out_specs=(
            P("expert", None),
            P("expert", None),
            P(None, None, "expert", "tensor"),
            P(None, "tensor", "expert"),
            P(None, None, "expert"),
            P(None, None, "expert"),
            P(None, "expert", None, "tensor"),
            P(None, "expert", "tensor", None),
        ),
        check_vma=False,
    )
```

profile of v0, /device:TPU:1, one launch (start us, length us, event | category | flops | bytes accessed | tf_op | source)
XLA Modules:
  0.0 1555.7 jit_solution(12436539425469895753)
XLA Ops:
  68.7 78.0 %all-reduce.10.cloned.1.call-done = f32[985,512]{1,0:T(8,128)} async-done(((f32[985,512]{1,0:T(8,128)}), f32[985,512]{1,0:T(8,128)}) %all-reduce.10.cloned.1.call-update) | async-done | bytes 2017296 | tf_op jit(solution)/shard_map/psum | solution.py:33
  166.3 24.6 %all-to-all-done = bf16[8,308,512]{2,1,0:T(8,128)(2,1)} async-done(((bf16[8,308,512]{2,1,0:T(8,128)(2,1)}), bf16[8,308,512]{2,1,0:T(8,128)(2,1)}, u32[]{:S(2)}, u32[]{:S(2)}) %all-to-all-start) | async-done | bytes 2523168 | tf_op jit(solution)/shard_map/all_to_all | solution.py:37
  208.4 92.0 %reduce-scatter.8.cloned.1.call-done = f32[8,308,128]{2,1,0:T(8,128)} async-done(((f32[8,308,512]{2,1,0:T(8,128)}), f32[8,308,128]{2,1,0:T(8,128)}) %reduce-scatter.8.cloned.1.call-update) | async-done | bytes 1261584 | tf_op jit(solution)/shard_map/reduce_scatter | solution.py:43
  301.8 14.4 all_to_all.40
  327.8 18.5 %gather_fusion = f32[1970]{0:T(1024)S(1)} fusion(f32[985,8]{0,1:T(8,128)S(1)} %fusion.144, s32[1970]{0:T(1024)S(1)} %reshape.507), kind=kCustom, calls=%fused_computation.clone | custom fusion | bytes 31520 | tf_op jit(solution)/shard_map/jit(take_along_axis)/gather | solution.py:123
  347.4 20.3 %all-gather.5.cloned.1.call-done = bf16[8,308,512]{2,1,0:T(8,128)(2,1)} async-done(((bf16[8,308,128]{2,1,0:T(8,128)(2,1)}), bf16[8,308,512]{2,1,0:T(8,128)(2,1)}) %all-gather.5.cloned.1.call-update) | async-done | bytes 2523152 | tf_op jit(solution)/shard_map/all_gather | solution.py:47
  400.9 79.1 %all-reduce.12.cloned.1.call-done = f32[985,512]{1,0:T(8,128)} async-done(((f32[985,512]{1,0:T(8,128)}), f32[985,512]{1,0:T(8,128)}) %all-reduce.12.cloned.1.call-update) | async-done | bytes 2017296 | tf_op jit(solution)/shard_map/psum | solution.py:33
  492.6 35.6 %all_to_all.41 = bf16[8,308,512]{2,1,0:T(8,128)(2,1)} all-to-all(bf16[8,308,512]{2,1,0:T(8,128)(2,1)S(1)} %reshape.434), channel_id=1, replica_groups=mesh['expert'=8,'tensor'=4] {'expert'}, dimensions={0} | all-to-all | bytes 5046272 | tf_op jit(solution)/shard_map/all_to_all | solution.py:37
  545.5 89.2 %reduce-scatter.10.cloned.1.call-done = f32[8,308,128]{2,1,0:T(8,128)} async-done(((f32[8,308,512]{2,1,0:T(8,128)}), f32[8,308,128]{2,1,0:T(8,128)}) %reduce-scatter.10.cloned.1.call-update) | async-done | bytes 1261584 | tf_op jit(solution)/shard_map/reduce_scatter | solution.py:43
  636.1 14.4 all_to_all.42
  675.4 26.5 %all-gather.7.cloned.1.call-done = bf16[8,308,512]{2,1,0:T(8,128)(2,1)} async-done(((bf16[8,308,128]{2,1,0:T(8,128)(2,1)}), bf16[8,308,512]{2,1,0:T(8,128)(2,1)}) %all-gather.7.cloned.1.call-update) | async-done | bytes 2523152 | tf_op jit(solution)/shard_map/all_gather | solution.py:47
  716.0 18.5 %gather_fusion.1 = f32[1970]{0:T(1024)S(1)} fusion(f32[985,8]{0,1:T(8,128)S(1)} %get-tuple-element.98, s32[1970]{0:T(1024)S(1)} %reshape.512), kind=kCustom, calls=%fused_computation.2.clone | custom fusion | bytes 31520 | tf_op jit(solution)/shard_map/jit(take_along_axis)/gather | solution.py:123
  760.7 36.3 %all_to_all.43 = bf16[8,308,512]{2,1,0:T(8,128)(2,1)} all-to-all(bf16[8,308,512]{2,1,0:T(8,128)(2,1)S(1)} %reshape.437), channel_id=1, replica_groups=mesh['expert'=8,'tensor'=4] {'expert'}, dimensions={0} | all-to-all | bytes 5046272 | tf_op jit(solution)/shard_map/all_to_all | solution.py:37
  815.3 89.5 %reduce-scatter.12.cloned.1.call-done = f32[8,308,128]{2,1,0:T(8,128)} async-done(((f32[8,308,512]{2,1,0:T(8,128)}), f32[8,308,128]{2,1,0:T(8,128)}) %reduce-scatter.12.cloned.1.call-update) | async-done | bytes 1261584 | tf_op jit(solution)/shard_map/reduce_scatter | solution.py:43
  920.5 51.3 %all-gather.9.cloned.1.call-done = bf16[8,308,512]{2,1,0:T(8,128)(2,1)} async-done(((bf16[8,308,128]{2,1,0:T(8,128)(2,1)}), bf16[8,308,512]{2,1,0:T(8,128)(2,1)}) %all-gather.9.cloned.1.call-update) | async-done | bytes 2523152 | tf_op jit(solution)/shard_map/all_gather | solution.py:47
  997.5 83.0 %all-reduce.14.cloned.1.call-done = f32[985,512]{1,0:T(8,128)} async-done(((f32[985,512]{1,0:T(8,128)}), f32[985,512]{1,0:T(8,128)}) %all-reduce.14.cloned.1.call-update) | async-done | bytes 2017296 | tf_op jit(solution)/shard_map/psum | solution.py:33
  1111.3 35.1 %all_to_all.45 = bf16[8,308,512]{2,1,0:T(8,128)(2,1)} all-to-all(bf16[8,308,512]{2,1,0:T(8,128)(2,1)S(1)} %reshape.441), channel_id=1, replica_groups=mesh['expert'=8,'tensor'=4] {'expert'}, dimensions={0} | all-to-all | bytes 5046272 | tf_op jit(solution)/shard_map/all_to_all | solution.py:37
  1164.8 89.2 %reduce-scatter.14.cloned.1.call-done = f32[8,308,128]{2,1,0:T(8,128)} async-done(((f32[8,308,512]{2,1,0:T(8,128)}), f32[8,308,128]{2,1,0:T(8,128)}) %reduce-scatter.14.cloned.1.call-update) | async-done | bytes 1261584 | tf_op jit(solution)/shard_map/reduce_scatter | solution.py:43
  1255.3 14.3 all_to_all.46
  1274.8 46.2 %all-gather.11.cloned.1.call-done = bf16[8,308,512]{2,1,0:T(8,128)(2,1)} async-done(((bf16[8,308,128]{2,1,0:T(8,128)(2,1)}), bf16[8,308,512]{2,1,0:T(8,128)(2,1)}) %all-gather.11.cloned.1.call-update) | async-done | bytes 2523152 | tf_op jit(solution)/shard_map/all_gather | solution.py:47
  1372.1 23.2 %all-reduce.2 = f32[2,512,8]{1,0,2:T(2,128)S(1)} all-reduce(f32[2,512,8]{1,0,2:T(2,128)S(1)} %copy.356), channel_id=8, replica_groups=mesh['expert'=8,'tensor'=4] {'expert'}, use_global_device_ids=true, to_apply=%region_50.53.clone | all-reduce | flops 8192 | bytes 65536
  1406.4 16.2 %all-reduce.18.cloned.1.call-done = (f32[2,3,512,128]{3,0,1,2:T(2,128)}, f32[2,128,512]{1,0,2:T(2,128)}) async-done(((f32[2,3,512,128]{3,0,1,2:T(2,128)}, f32[2,128,512]{1,0,2:T(2,128)}), (f32[2,3,512,128]{3,0,1,2:T(2,128)}, f32[2,128,512]{1,0,2:T(2,128)})) %all-reduce.18.cloned.1.call-update) | async-done | bytes 2097168
  1425.7 83.1 %all-reduce.16.cloned.1.call-done = f32[985,512]{1,0:T(8,128)} async-done(((f32[985,512]{1,0:T(8,128)}), f32[985,512]{1,0:T(8,128)}) %all-reduce.16.cloned.1.call-update) | async-done | bytes 2017296 | tf_op jit(solution)/shard_map/psum | solution.py:33
  1518.4 29.0 %reduce-scatter.16.cloned.1.call-done = f32[64,4]{1,0:T(8,128)} async-done(((f32[512,4]{1,0:T(8,128)}), f32[64,4]{1,0:T(8,128)}) %reduce-scatter.16.cloned.1.call-update) | async-done | bytes 1040
  (630 shorter events, 430.9 us)
Async XLA Ops:
  7.2 139.5 %all-reduce.10.cloned.1.call-start = ((), (), s32[]{:S(2)}) async-start(), calls=%async_computation.13 | async-start | bytes 4063232 | tf_op jit(solution)/shard_map/psum | solution.py:33
  157.4 33.5 %all-to-all-start = ((bf16[8,308,512]{2,1,0:T(8,128)(2,1)}), bf16[8,308,512]{2,1,0:T(8,128)(2,1)}, u32[]{:S(2)}, u32[]{:S(2)}) async-start(bf16[8,308,512]{2,1,0:T(8,128)(2,1)} %reshape.430), calls=%async_computation | async-start | bytes 5111808 | tf_op jit(solution)/shard_map/all_to_all | solution.py:37
  162.9 137.5 %reduce-scatter.8.cloned.1.call-start = ((), (), s32[]{:S(2)}) async-start(), calls=%async_computation.14 | async-start | bytes 6389760 | tf_op jit(solution)/shard_map/reduce_scatter | solution.py:43
  208.3 108.0 %copy-start.170 = (f32[2,512,1]{1,2,0:T(1,128)S(1)}, f32[2,512,1]{1,2,0:T(1,128)}, u32[]{:S(2)}) copy-start(f32[2,512,1]{1,2,0:T(1,128)} %param.20) | copy-start | bytes 12292
  208.3 159.3 %all-gather.5.cloned.1.call-start = ((), (), s32[]{:S(2)}) async-start(), calls=%async_computation.15 | async-start | bytes 3194880 | tf_op jit(solution)/shard_map/all_gather | solution.py:47
  316.2 163.7 %all-reduce.12.cloned.1.call-start = ((), (), s32[]{:S(2)}) async-start(), calls=%async_computation.16 | async-start | bytes 4063232 | tf_op jit(solution)/shard_map/psum | solution.py:33
  396.4 238.3 %reduce-scatter.10.cloned.1.call-start = ((), (), s32[]{:S(2)}) async-start(), calls=%async_computation.17 | async-start | bytes 6389760 | tf_op jit(solution)/shard_map/reduce_scatter | solution.py:43
  396.7 254.0 %copy-start.17 = (s32[1,985,2]{2,1,0:T(8,128)}, s32[1,985,2]{2,1,0:T(8,128)S(1)}, u32[]{:S(2)}) copy-start(s32[1,985,2]{2,1,0:T(8,128)S(1)} %copy.402) | copy-start | bytes 23644
  545.5 156.5 %all-gather.7.cloned.1.call-start = ((), (), s32[]{:S(2)}) async-start(), calls=%async_computation.18 | async-start | bytes 3194880 | tf_op jit(solution)/shard_map/all_gather | solution.py:47
  650.6 254.1 %reduce-scatter.12.cloned.1.call-start = ((), (), s32[]{:S(2)}) async-start(), calls=%async_computation.19 | async-start | bytes 6389760 | tf_op jit(solution)/shard_map/reduce_scatter | solution.py:43
  815.2 105.3 %copy-start.110 = (s32[985]{0:T(1024)S(1)}, s32[985]{0:T(1024)}, u32[]{:S(2)}) copy-start(s32[985]{0:T(1024)} %copy-done.108) | copy-start | bytes 11824
  815.2 105.3 %copy-start.126 = (s32[985]{0:T(1024)S(1)}, s32[985]{0:T(1024)}, u32[]{:S(2)}) copy-start(s32[985]{0:T(1024)} %copy-done.124) | copy-start | bytes 11824
  815.2 105.3 %copy-start.147 = (f32[985]{0:T(1024)S(1)}, f32[985]{0:T(1024)}, u32[]{:S(2)}) copy-start(f32[985]{0:T(1024)} %copy-done.146) | copy-start | bytes 11824
  815.2 105.3 %copy-start.149 = (f32[985]{0:T(1024)S(1)}, f32[985]{0:T(1024)}, u32[]{:S(2)}) copy-start(f32[985]{0:T(1024)} %copy-done.148) | copy-start | bytes 11824
  815.2 105.3 %copy-start.150 = (f32[985]{0:T(1024)S(1)}, f32[985]{0:T(1024)}, u32[]{:S(2)}) copy-start(f32[985]{0:T(1024)} %get-tuple-element.97) | copy-start | bytes 11824
  815.2 156.6 %all-gather.9.cloned.1.call-start = ((), (), s32[]{:S(2)}) async-start(), calls=%async_computation.20 | async-start | bytes 3194880 | tf_op jit(solution)/shard_map/all_gather | solution.py:47
  920.4 160.0 %all-reduce.14.cloned.1.call-start = ((), (), s32[]{:S(2)}) async-start(), calls=%async_computation.21 | async-start | bytes 4063232 | tf_op jit(solution)/shard_map/psum | solution.py:33
  997.0 257.0 %reduce-scatter.14.cloned.1.call-start = ((), (), s32[]{:S(2)}) async-start(), calls=%async_computation.22 | async-start | bytes 6389760 | tf_op jit(solution)/shard_map/reduce_scatter | solution.py:43
  1164.7 106.3 %copy-start.26 = (bf16[985,512]{1,0:T(8,128)(2,1)S(1)}, bf16[985,512]{1,0:T(8,128)(2,1)}, u32[]{:S(2)}) copy-start(bf16[985,512]{1,0:T(8,128)(2,1)} %copy-done.24) | copy-start | bytes 3025924
  1164.7 106.5 %copy-start.64 = (bf16[985,128]{0,1:T(8,128)(2,1)S(1)}, bf16[985,128]{0,1:T(8,128)(2,1)}, u32[]{:S(2)}) copy-start(bf16[985,128]{0,1:T(8,128)(2,1)} %copy-done.63) | copy-start | bytes 756484
  1164.7 156.3 %all-gather.11.cloned.1.call-start = ((), (), s32[]{:S(2)}) async-start(), calls=%async_computation.23 | async-start | bytes 3194880 | tf_op jit(solution)/shard_map/all_gather | solution.py:47
  1269.6 153.0 %all-reduce.18.cloned.1.call-start = ((), (), s32[]{:S(2)}) async-start(), calls=%async_computation.26 | async-start | bytes 4194304
  1361.8 147.0 %all-reduce.16.cloned.1.call-start = ((), (), s32[]{:S(2)}) async-start(), calls=%async_computation.24 | async-start | bytes 4063232 | tf_op jit(solution)/shard_map/psum | solution.py:33
  1371.7 175.7 %reduce-scatter.16.cloned.1.call-start = ((), (), s32[]{:S(2)}) async-start(), calls=%async_computation.25 | async-start | bytes 294912
  (164 other events, 2143.6 us)
Sparse Core Ops, SparseCore 0:
  63.2 83.4 all-reduce.9
  208.4 91.9 reduce-scatter.7
  316.4 51.2 all-gather.4
  396.5 83.3 all-reduce.11
  545.6 89.0 reduce-scatter.9
  650.7 51.2 all-gather.6
  815.3 89.4 reduce-scatter.11
  920.5 51.2 all-gather.8
  997.1 83.3 all-reduce.13
  1164.8 89.1 reduce-scatter.13
  1269.8 51.2 all-gather.10
  1362.0 60.6 all-reduce.17
  1425.0 83.8 all-reduce.15
  1514.8 32.5 reduce-scatter.15
where the time goes:
time: 1570 us; the launch traced here: 1560 us
  waiting for transfers between devices  897 us (57%)
  local copies, waits for them, and re-layouts  233 us (15%)
  blocking collectives  226 us (14%)
  matrix products  122 us (8%)
  other arithmetic  53.5 us (3%)
  between operations  17.5 us (1%)
    reduce_scatter x4, waiting for transfers between devices, to_sources(): lax.psum_scatter(partial_rows, 'tensor', scatter_dimension=2, tiled=True)  360 us
    psum x4, waiting for transfers between devices, heads_total(): return lax.psum(partial_sum, 'tensor')  323 us
    all_gather x4, waiting for transfers between devices, to_sources(): return lax.all_gather(moved, 'tensor', axis=2, tiled=True)  144 us
    all_to_all x3, blocking collectives, to_experts(): lax.all_to_all(make_rows(0, model_width), 'expert', split_axis=0, concat_...  107 us
    all_to_all x4, blocking collectives, to_sources(): lax.all_to_all(shares.astype(jnp.bfloat16), 'expert', split_axis=0, conca...  57.3 us
    unnamed x16, waiting for transfers between devices  45.4 us
    gather x6, local copies, waits for them, and re-layouts, local(): gate_values = jnp.take_along_axis(probs_all, chosen, axis=1)  38.4 us
  transfers between devices with their start and end apart: 15, of which 15 were waited for; matrix products, arithmetic and copies ran while one was open for 6% of the time, Pallas kernels for 0%

commit v1 on v0

--- a/solution.py
+++ b/solution.py
@@ -29,22 +29,12 @@
     )
 
 
-def heads_total(partial_sum):
-    return lax.psum(partial_sum, "tensor")
-
-
-def to_experts(make_rows, model_width):
-    return lax.all_to_all(
-        make_rows(0, model_width), "expert", split_axis=0, concat_axis=0, tiled=True
-    )
-
-
-def to_sources(partial_rows):
-    shares = lax.psum_scatter(partial_rows, "tensor", scatter_dimension=2, tiled=True)
-    moved = lax.all_to_all(
-        shares.astype(jnp.bfloat16), "expert", split_axis=0, concat_axis=0, tiled=True
-    )
-    return lax.all_gather(moved, "tensor", axis=2, tiled=True)
+def exchange(rows):
+    return lax.all_to_all(rows, "expert", split_axis=0, concat_axis=0, tiled=True)
+
+
+def own_part(rows, width, axis=1):
+    return lax.dynamic_slice_in_dim(rows, lax.axis_index("tensor") * width, width, axis=axis)
 
 
 def slot_plan(chosen, rank_rows, experts, capacity):
@@ -80,17 +70,39 @@
     tokens = inputs.shape[0]
     model_width = inputs.shape[1]
     images = tokens // SEQ
-    local_heads = attend_in.shape[3] // HEAD_DIM
+    head_cols = attend_in.shape[3]
+    hidden_cols = expert_in.shape[3]
+    local_heads = head_cols * lax.axis_size("tensor") // HEAD_DIM
     layers = attend_in.shape[0]
     capacity = max(2, (10 * tokens + 4 * experts - 1) // (4 * experts))
     slots_all = experts * capacity
     score_scale = HEAD_DIM ** (-0.5)
-    in_full, out_full, router_full, gains_full = (
-        lax.all_gather(attend_in.astype(jnp.bfloat16), "expert", axis=2, tiled=True),
-        lax.all_gather(attend_out.astype(jnp.bfloat16), "expert", axis=2, tiled=True),
-        lax.all_gather(router.astype(jnp.bfloat16), "expert", axis=2, tiled=True),
-        lax.all_gather(norm_gains.astype(jnp.bfloat16), "expert", axis=2, tiled=True),
-    )
+    layer_ids = range(layers)
+    gains_full = lax.all_gather(norm_gains.astype(jnp.bfloat16), "expert", axis=2, tiled=True)
+    router_full = lax.all_gather(router.astype(jnp.bfloat16), "expert", axis=2, tiled=True)
+    in_full = []
+    out_full = []
+    win_full = []
+    wout_full = []
+    for layer_index in layer_ids:
+        in_part = lax.all_gather(
+            attend_in[layer_index].astype(jnp.bfloat16), "tensor", axis=2, tiled=True
+        )
+        in_full.append(lax.all_gather(in_part, "expert", axis=1, tiled=True))
+        out_part = lax.all_gather(
+            attend_out[layer_index].astype(jnp.bfloat16), "tensor", axis=0, tiled=True
+        )
+        out_full.append(lax.all_gather(out_part, "expert", axis=1, tiled=True))
+        win_full.append(
+            lax.all_gather(
+                expert_in[layer_index, 0].astype(jnp.bfloat16), "tensor", axis=1, tiled=True
+            )
+        )
+        wout_full.append(
+            lax.all_gather(
+                expert_out[layer_index, 0].astype(jnp.bfloat16), "tensor", axis=0, tiled=True
+            )
+        )
     slot_ids = lax.broadcasted_iota(jnp.int32, (1, slots_all), 1)
     stream = inputs
     stash_list = []
@@ -113,39 +125,36 @@
             .astype(jnp.bfloat16)
             .reshape(tokens, -1)
         )
-        middle = stream + heads_total(
-            jnp.dot(mixed_heads, out_full[layer_index], preferred_element_type=jnp.float32)
+        middle = stream + jnp.dot(
+            mixed_heads, out_full[layer_index], preferred_element_type=jnp.float32
         )
         normed_two = norm_rows(middle, gains_now[1]).astype(jnp.bfloat16)
         logits = jnp.dot(normed_two, router_full[layer_index], preferred_element_type=jnp.float32)
         probs_all = jax.nn.softmax(logits, axis=-1)
         chosen = routes[layer_index]
-        gate_values = jnp.take_along_axis(probs_all, chosen, axis=1)
         target, first_f, second_f = slot_plan(chosen, priority[layer_index], experts, capacity)
+        gate_values = jnp.stack(
+            [jnp.sum(probs_all * first_f, axis=1), jnp.sum(probs_all * second_f, axis=1)], axis=1
+        )
         pick_first = (target[:, 0:1] == slot_ids).astype(jnp.bfloat16)
         pick_second = (target[:, 1:2] == slot_ids).astype(jnp.bfloat16)
         pick_both = pick_first + pick_second
 
-        def dispatch_rows(first_col, col_count, normed_two=normed_two, pick_both=pick_both):
-            return (
-                contract_rows(pick_both, normed_two)
-                .astype(jnp.bfloat16)
-                .reshape(experts, capacity, col_count)
-            )
-
-        arrived = to_experts(dispatch_rows, model_width).reshape(slots_all, model_width)
-        win_now = expert_in[layer_index, 0].astype(jnp.bfloat16)
-        wout_now = expert_out[layer_index, 0].astype(jnp.bfloat16)
-        before = jnp.dot(arrived, win_now, preferred_element_type=jnp.float32)
+        dispatched = contract_rows(pick_both, normed_two).astype(jnp.bfloat16)
+        arrived = exchange(dispatched.reshape(experts, capacity, model_width)).reshape(
+            slots_all, model_width
+        )
+        before = jnp.dot(arrived, win_full[layer_index], preferred_element_type=jnp.float32)
         hidden = gelu_exact(before).astype(jnp.bfloat16)
-        expert_rows = jnp.dot(hidden, wout_now, preferred_element_type=jnp.float32).reshape(
-            experts, capacity, model_width
-        )
-        returned = to_sources(expert_rows).reshape(slots_all, model_width)
+        expert_rows = jnp.dot(
+            hidden, wout_full[layer_index], preferred_element_type=jnp.float32
+        ).astype(jnp.bfloat16)
+        returned = exchange(expert_rows.reshape(experts, capacity, model_width)).reshape(
+            slots_all, model_width
+        )
         rows_first = jnp.dot(pick_first, returned, preferred_element_type=jnp.float32)
         rows_second = jnp.dot(pick_second, returned, preferred_element_type=jnp.float32)
         output = middle + gate_values[:, 0:1] * rows_first + gate_values[:, 1:2] * rows_second
-        kept_pre = None
         stash_list.append(
             (
                 stream,
@@ -167,7 +176,6 @@
                 arrived,
                 rows_first,
                 rows_second,
-                kept_pre,
             )
         )
         stream = output
@@ -194,42 +202,27 @@
             arrived,
             rows_first,
             rows_second,
-            kept_pre,
         ) = stash_list[layer_index]
-        win_now = expert_in[layer_index, 0].astype(jnp.bfloat16)
-        wout_now = expert_out[layer_index, 0].astype(jnp.bfloat16)
         gate_first = jnp.sum(upstream * rows_first, axis=1)
         gate_second = jnp.sum(upstream * rows_second, axis=1)
-        scaled = jnp.concatenate(
-            [
-                gate_values[:, 0:1] * upstream,
-                gate_values[:, 1:2] * upstream,
-                jnp.zeros((1, model_width), jnp.float32),
-            ],
-            axis=0,
-        )
-        owners = (
-            jnp.full((slots_all + 1,), 2 * tokens, jnp.int32)
-            .at[jnp.concatenate([target[:, 0], target[:, 1]])]
-            .set(jnp.arange(2 * tokens, dtype=jnp.int32))[:slots_all]
-        )
-
-        def gradient_rows(first_col, col_count, scaled=scaled, owners=owners):
-            return (
-                jnp.take(scaled, owners, axis=0)
-                .astype(jnp.bfloat16)
-                .reshape(experts, capacity, col_count)
-            )
-
-        grad_arrived = to_experts(gradient_rows, model_width).reshape(slots_all, model_width)
-        before = jnp.dot(arrived, win_now, preferred_element_type=jnp.float32)
+        scaled_first = (gate_values[:, 0:1] * upstream).astype(jnp.bfloat16)
+        scaled_second = (gate_values[:, 1:2] * upstream).astype(jnp.bfloat16)
+        grad_slots = (
+            contract_rows(pick_first, scaled_first) + contract_rows(pick_second, scaled_second)
+        ).astype(jnp.bfloat16)
+        grad_arrived = exchange(grad_slots.reshape(experts, capacity, model_width)).reshape(
+            slots_all, model_width
+        )
+        before = jnp.dot(arrived, win_full[layer_index], preferred_element_type=jnp.float32)
         hidden = gelu_exact(before).astype(jnp.bfloat16)
-        grads_wout.append(contract_rows(hidden, grad_arrived))
-        grad_hidden = contract_last(grad_arrived, wout_now)
+        grads_wout.append(contract_rows(own_part(hidden, hidden_cols), grad_arrived))
+        grad_hidden = contract_last(grad_arrived, wout_full[layer_index])
         grad_before = jax.vjp(gelu_exact, before)[1](grad_hidden)[0].astype(jnp.bfloat16)
-        grads_win.append(contract_rows(arrived, grad_before))
-        grad_rows = contract_last(grad_before, win_now).reshape(experts, capacity, model_width)
-        grad_dispatched = to_sources(grad_rows).reshape(slots_all, model_width)
+        grads_win.append(contract_rows(arrived, own_part(grad_before, hidden_cols)))
+        grad_rows = contract_last(grad_before, win_full[layer_index]).astype(jnp.bfloat16)
+        grad_dispatched = exchange(grad_rows.reshape(experts, capacity, model_width)).reshape(
+            slots_all, model_width
+        )
         grad_normed = jnp.dot(pick_both, grad_dispatched, preferred_element_type=jnp.float32)
         grad_probs = first_f * gate_first[:, None] + second_f * gate_second[:, None]
         grad_logits = (
@@ -240,7 +233,7 @@
         norm_back = jax.vjp(norm_rows, middle, gains_now[1])[1](grad_normed)
         grad_middle = upstream + norm_back[0]
         grad_branch = grad_middle.astype(jnp.bfloat16)
-        grads_out.append(contract_rows(mixed_heads, grad_branch))
+        grads_out.append(contract_rows(own_part(mixed_heads, head_cols), grad_branch))
         grad_mixed = (
             contract_last(grad_branch, out_full[layer_index])
             .astype(jnp.bfloat16)
@@ -276,11 +269,16 @@
         ).astype(jnp.bfloat16)
         grad_triple = jnp.stack([grad_query, grad_key, grad_value]).reshape(3, tokens, -1)
         grads_in.append(
-            jnp.einsum("td,jth->jdh", normed, grad_triple, preferred_element_type=jnp.float32)
+            jnp.einsum(
+                "td,jth->jdh",
+                normed,
+                own_part(grad_triple, head_cols, 2),
+                preferred_element_type=jnp.float32,
+            )
         )
         project = in_full[layer_index]
-        grad_normed_one = heads_total(
-            jnp.einsum("jth,jdh->td", grad_triple, project, preferred_element_type=jnp.float32)
+        grad_normed_one = jnp.einsum(
+            "jth,jdh->td", grad_triple, project, preferred_element_type=jnp.float32
         )
         norm_back_one = jax.vjp(norm_rows, stream_in, gains_now[0])[1](grad_normed_one)
         grads_gain.append(jnp.stack([norm_back_one[1], norm_back[1]]))

time: 1570 us -> 937 us (0.60)
  waiting for transfers between devices: 897 us -> 205 us
  matrix products: 122 us -> 244 us
  blocking collectives: 226 us -> 187 us
  starting transfers between devices: 6.43 us -> 44.1 us
  local copies, waits for them, and re-layouts: 233 us -> 196 us
  other arithmetic: 53.5 us -> 31.7 us
    reduce_scatter x4 -> x0, waiting for transfers between devices: 360 us -> none  [to_sources(): lax.psum_scatter(partial_rows, 'tensor', scatter_dimension=2, tiled=True)]
    psum x4 -> x0, waiting for transfers between devices: 323 us -> none  [heads_total(): return lax.psum(partial_sum, 'tensor')]
    all_gather x4 -> x6, waiting for transfers between devices: 144 us -> 0.89 us  [the longest x2 0.84 us: local(): lax.all_gather(expert_out[layer_index, 0].astype(jnp.bfloat16), 'tensor',...]
    all_to_all x7 -> x1, blocking collectives: 164 us -> 38.6 us  [exchange(): lax.all_to_all(rows, 'expert', split_axis=0, concat_axis=0, tiled=True)]
    all_to_all x1 -> x7, waiting for transfers between devices: 24.6 us -> 117 us  [exchange(): lax.all_to_all(rows, 'expert', split_axis=0, concat_axis=0, tiled=True)]
    all_gather x2 -> x6, blocking collectives: 20.1 us -> 83.1 us  [the longest x2 39.2 us: local(): out_full.append(lax.all_gather(out_part, 'expert', axis=1, tiled=True))]
    gather x8 -> x0, local copies, waits for them, and re-layouts: 54.8 us -> none  [the longest x6 38.4 us: local(): gate_values = jnp.take_along_axis(probs_all, chosen, axis=1)]
    unnamed x16 -> x10, waiting for transfers between devices: 45.4 us -> 87.1 us
  transfers between devices with their start and end apart: 15 -> 15, of which waited for: 15 -> 8; matrix products, arithmetic and copies ran while one was open for 6% -> 23% of each run, Pallas kernels for 0% -> 0%
where the time goes in v1:
time: 937 us; the launch traced here: 925 us
  matrix products  244 us (26%)
  waiting for transfers between devices  205 us (22%)
  local copies, waits for them, and re-layouts  196 us (21%)
  blocking collectives  187 us (20%)
  starting transfers between devices  44.1 us (5%)
  other arithmetic  31.7 us (3%)
  between operations  17.1 us (2%)
    all_to_all x7, waiting for transfers between devices, exchange(): lax.all_to_all(rows, 'expert', split_axis=0, concat_axis=0, tiled=True)  117 us
    unnamed x10, waiting for transfers between devices  87.1 us
    dot_general x14, matrix products, contract_rows(): lax.dot_general(left_side, right_side, (((0,), (0,)), ((), ())), preferre...  49.9 us
    dot_general x8, matrix products, contract_last(): lax.dot_general(left_side, right_side, (((1,), (1,)), ((), ())), preferre...  47.8 us
    unnamed x1, blocking collectives  44.9 us
    all_to_all x7, starting transfers between devices, exchange(): lax.all_to_all(rows, 'expert', split_axis=0, concat_axis=0, tiled=True)  43.9 us
    all_gather x2, blocking collectives, local(): out_full.append(lax.all_gather(out_part, 'expert', axis=1, tiled=True))  39.2 us
    all_to_all x1, blocking collectives, exchange(): lax.all_to_all(rows, 'expert', split_axis=0, concat_axis=0, tiled=True)  38.6 us
  transfers between devices with their start and end apart: 15, of which 8 were waited for; matrix products, arithmetic and copies ran while one was open for 23% of the time, Pallas kernels for 0%

profile of v1, /device:TPU:1, one launch (start us, length us, event | category | flops | bytes accessed | tf_op | source)
XLA Modules:
  0.0 924.8 jit_solution(8189973012302681919)
XLA Ops:
  8.2 12.5 %all-gather = bf16[1,3,64,512]{3,2,1,0:T(8,128)(2,1)} all-gather(bf16[1,3,64,128]{3,2,1,0:T(8,128)(2,1)S(1)} %get-tuple-element.97), channel_id=2, replica_groups=mesh['expert'=8,'tensor'=4] {'tensor'}, dimensions={3}, use_global_device_ids=true | all-gather | bytes 245760 | tf_op jit(solution)/shard_map/all_gather | solution.py:88
  28.0 11.8 %all_gather.42 = bf16[2,2,512]{1,0,2:T(2,128)(2,1)S(1)} all-gather(bf16[2,2,64]{1,0,2:T(2,128)(2,1)S(1)} %copy.168), channel_id=1, replica_groups=mesh['expert'=8,'tensor'=4] {'expert'}, dimensions={2}, use_global_device_ids=true | all-gather | bytes 4608 | tf_op jit(solution)/shard_map/all_gather | solution.py:81
  43.7 9.5 %all-gather.2 = bf16[1,512,64]{1,2,0:T(8,128)(2,1)S(1)} all-gather(bf16[1,128,64]{1,2,0:T(8,128)(2,1)S(1)} %get-tuple-element.99), channel_id=4, replica_groups=mesh['expert'=8,'tensor'=4] {'tensor'}, dimensions={1}, use_global_device_ids=true | all-gather | bytes 81920 | tf_op jit(solution)/shard_map/all_gather | solution.py:92
  53.2 13.0 %all-gather.3 = bf16[1,512,512]{1,2,0:T(8,128)(2,1)} all-gather(bf16[1,512,64]{1,2,0:T(8,128)(2,1)S(1)} %all-gather.2), channel_id=5, replica_groups=mesh['expert'=8,'tensor'=4] {'expert'}, dimensions={2}, use_global_device_ids=true | all-gather | bytes 589824 | tf_op jit(solution)/shard_map/all_gather | solution.py:95
  66.2 8.2 all_gather.47
  137.1 12.2 %all-gather.6 = bf16[1,3,64,512]{3,2,1,0:T(8,128)(2,1)} all-gather(bf16[1,3,64,128]{3,2,1,0:T(8,128)(2,1)S(1)} %get-tuple-element.96), channel_id=8, replica_groups=mesh['expert'=8,'tensor'=4] {'tensor'}, dimensions={3}, use_global_device_ids=true | all-gather | bytes 245760 | tf_op jit(solution)/shard_map/all_gather | solution.py:88
  149.3 18.0 %all-to-all-done = bf16[8,308,512]{2,1,0:T(8,128)(2,1)S(1)} async-done(((bf16[8,308,512]{2,1,0:T(8,128)(2,1)}), bf16[8,308,512]{2,1,0:T(8,128)(2,1)S(1)}, u32[]{:S(2)}, u32[]{:S(2)}) %all-to-all-start) | async-done | bytes 2523168 | tf_op jit(solution)/shard_map/all_to_all | solution.py:33
  169.4 13.5 %multiply_convert_fusion.1 = (bf16[2464,2048]{1,0:T(8,128)(2,1)}, f32[2464,2048]{1,0:T(8,128)}) fusion(bf16[2464,512]{1,0:T(8,128)(2,1)} %reshape.292, bf16[1,1,512,2048]{3,2,1,0:T(8,128)(2,1)} %all-gather.21.cloned.1.call-done), kind=kOutput, calls=%fused_computation.4 | convolution fusion | flops 5192613888 | bytes 34897920 | tf_op jit(solution)/shard_map/dot_general | solution.py:147
  182.9 9.8 %convolution_convert_fusion.3 = bf16[2464,512]{1,0:T(8,128)(2,1)S(1)} fusion(bf16[2464,2048]{1,0:T(8,128)(2,1)} %get-tuple-element.122, bf16[1,1,2048,512]{3,2,1,0:T(8,128)(2,1)} %all-gather.23.cloned.1.call-done), kind=kOutput, calls=%fused_computation.71 | convolution fusion | flops 5168644096 | bytes 14712832 | tf_op jit(solution)/shard_map/dot_general | solution.py:149
  202.6 9.7 %all-gather.8 = bf16[1,512,64]{1,2,0:T(8,128)(2,1)S(1)} all-gather(bf16[1,128,64]{1,2,0:T(8,128)(2,1)S(1)} %get-tuple-element.98), channel_id=10, replica_groups=mesh['expert'=8,'tensor'=4] {'tensor'}, dimensions={1}, use_global_device_ids=true | all-gather | bytes 81920 | tf_op jit(solution)/shard_map/all_gather | solution.py:92
  212.3 26.3 %all-gather.9 = bf16[1,512,512]{1,2,0:T(8,128)(2,1)} all-gather(bf16[1,512,64]{1,2,0:T(8,128)(2,1)S(1)} %all-gather.8), channel_id=11, replica_groups=mesh['expert'=8,'tensor'=4] {'expert'}, dimensions={2}, use_global_device_ids=true | all-gather | bytes 589824 | tf_op jit(solution)/shard_map/all_gather | solution.py:95
  308.7 27.5 %all-to-all-done.2 = bf16[8,308,512]{2,1,0:T(8,128)(2,1)} async-done(((bf16[8,308,512]{2,1,0:T(8,128)(2,1)}), bf16[8,308,512]{2,1,0:T(8,128)(2,1)}, u32[]{:S(2)}, u32[]{:S(2)}) %all-to-all-start.2) | async-done | bytes 2523168 | tf_op jit(solution)/shard_map/all_to_all | solution.py:33
  340.4 13.6 %multiply_convert_fusion = (bf16[2464,2048]{1,0:T(8,128)(2,1)}, f32[2464,2048]{1,0:T(8,128)}) fusion(bf16[2464,512]{1,0:T(8,128)(2,1)} %reshape.297, bf16[1,1,512,2048]{3,2,1,0:T(8,128)(2,1)} %all-gather.27.cloned.1.call-done), kind=kOutput, calls=%fused_computation.2 | convolution fusion | flops 5192613888 | bytes 34897920 | tf_op jit(solution)/shard_map/dot_general | solution.py:147
  354.8 10.9 %convolution_convert_fusion.2 = bf16[2464,512]{1,0:T(8,128)(2,1)} fusion(bf16[2464,2048]{1,0:T(8,128)(2,1)} %get-tuple-element.129, bf16[1,1,2048,512]{3,2,1,0:T(8,128)(2,1)} %all-gather.29.cloned.1.call-done), kind=kOutput, calls=%fused_computation.70 | convolution fusion | flops 5168644096 | bytes 14712832 | tf_op jit(solution)/shard_map/dot_general | solution.py:149
  378.6 26.4 %all-to-all-done.3 = bf16[8,308,512]{2,1,0:T(8,128)(2,1)} async-done(((bf16[8,308,512]{2,1,0:T(8,128)(2,1)}), bf16[8,308,512]{2,1,0:T(8,128)(2,1)}, u32[]{:S(2)}, u32[]{:S(2)}) %all-to-all-start.3) | async-done | bytes 2523168 | tf_op jit(solution)/shard_map/all_to_all | solution.py:33
  432.2 38.6 %all_to_all.40 = bf16[8,308,512]{2,1,0:T(8,128)(2,1)} all-to-all(bf16[8,308,512]{2,1,0:T(8,128)(2,1)} %reshape.300), channel_id=1, replica_groups=mesh['expert'=8,'tensor'=4] {'expert'}, dimensions={0} | all-to-all | bytes 5046272 | tf_op jit(solution)/shard_map/all_to_all | solution.py:33
  474.9 15.1 %add_convert_fusion.1 = bf16[2464,2048]{1,0:T(8,128)(2,1)S(1)} fusion(f32[2464,2048]{1,0:T(8,128)} %get-tuple-element.130, bf16[2464,512]{1,0:T(8,128)(2,1)} %reshape.301, bf16[1,1,2048,512]{3,2,1,0:T(8,128)(2,1)} %all-gather.29.cloned.1.call-done), kind=kOutput, calls=%fused_computation.1 | convolution fusion | flops 5232984064 | bytes 34897920 | tf_op jit(solution)/shard_map/dot_general | solution.py:27
  510.9 28.0 %all-to-all-done.5 = bf16[8,308,512]{2,1,0:T(8,128)(2,1)} async-done(((bf16[8,308,512]{2,1,0:T(8,128)(2,1)}), bf16[8,308,512]{2,1,0:T(8,128)(2,1)}, u32[]{:S(2)}, u32[]{:S(2)}) %all-to-all-start.5) | async-done | bytes 2523168 | tf_op jit(solution)/shard_map/all_to_all | solution.py:33
  633.7 17.1 %all-to-all-done.6 = bf16[8,308,512]{2,1,0:T(8,128)(2,1)} async-done(((bf16[8,308,512]{2,1,0:T(8,128)(2,1)}), bf16[8,308,512]{2,1,0:T(8,128)(2,1)}, u32[]{:S(2)}, u32[]{:S(2)}) %all-to-all-start.6) | async-done | bytes 2523168 | tf_op jit(solution)/shard_map/all_to_all | solution.py:33
  654.9 15.1 %add_convert_fusion = bf16[2464,2048]{1,0:T(8,128)(2,1)S(1)} fusion(f32[2464,2048]{1,0:T(8,128)} %get-tuple-element.123, bf16[2464,512]{1,0:T(8,128)(2,1)} %reshape.306, bf16[1,1,2048,512]{3,2,1,0:T(8,128)(2,1)} %all-gather.23.cloned.1.call-done), kind=kOutput, calls=%fused_computation | convolution fusion | flops 5232984064 | bytes 34897920 | tf_op jit(solution)/shard_map/dot_general | solution.py:27
  685.1 8.0 all-to-all-start.7
  693.5 44.9 %all-reduce.2 = f32[2,512,8]{1,0,2:T(2,128)S(1)} all-reduce(f32[2,512,8]{1,0,2:T(2,128)S(1)} %copy.206), channel_id=16, replica_groups=mesh['expert'=8,'tensor'=4] {'expert'}, use_global_device_ids=true, to_apply=%region_44.45.clone | all-reduce | flops 8192 | bytes 65536
  827.1 22.8 %reduce-scatter.4.cloned.1.call-done = f32[64,4]{1,0:T(8,128)} async-done(((f32[512,4]{1,0:T(8,128)}), f32[64,4]{1,0:T(8,128)}) %reduce-scatter.4.cloned.1.call-update) | async-done | bytes 1040
  851.5 63.0 %all-reduce.6.cloned.1.call-done = (f32[2,3,512,128]{3,0,1,2:T(2,128)}, f32[2,128,512]{1,0,2:T(2,128)}) async-done(((f32[2,3,512,128]{3,0,1,2:T(2,128)}, f32[2,128,512]{1,0,2:T(2,128)}), (f32[2,3,512,128]{3,0,1,2:T(2,128)}, f32[2,128,512]{1,0,2:T(2,128)})) %all-reduce.6.cloned.1.call-update) | async-done | bytes 2097168
  (470 shorter events, 432.2 us)
Async XLA Ops:
  7.2 70.0 %all-gather.19.cloned.1.call-start = ((), (), s32[]{:S(2)}) async-start(), calls=%async_computation.9 | async-start | bytes 1769472 | tf_op jit(solution)/shard_map/all_gather | solution.py:91
  20.7 148.7 %all-gather.21.cloned.1.call-start = ((), (), s32[]{:S(2)}) async-start(), calls=%async_computation.10 | async-start | bytes 2621440 | tf_op jit(solution)/shard_map/all_gather | solution.py:97
  23.6 159.4 %all-gather.23.cloned.1.call-start = ((), (), s32[]{:S(2)}) async-start(), calls=%async_computation.11 | async-start | bytes 2621440 | tf_op jit(solution)/shard_map/all_gather | solution.py:102
  26.8 50.3 %copy-start.76 = (f32[985]{0:T(1024)}, f32[985]{0:T(1024)S(1)}, u32[]{:S(2)}) copy-start(f32[985]{0:T(1024)S(1)} %broadcast_multiply_fusion.3) | copy-start | bytes 11824
  43.7 81.0 %copy-start.92 = (f32[512]{0:T(512)}, f32[512]{0:T(512)S(1)}, u32[]{:S(2)}) copy-start(f32[512]{0:T(512)S(1)} %get-tuple-element.62) | copy-start | bytes 6148
  74.5 50.6 %copy-start.66 = (bf16[1,512,8]{1,0,2:T(2,128)(2,1)}, bf16[1,512,8]{1,0,2:T(2,128)(2,1)S(1)}, u32[]{:S(2)}) copy-start(bf16[1,512,8]{1,0,2:T(2,128)(2,1)S(1)} %get-tuple-element.101) | copy-start | bytes 24580
  74.5 51.0 %copy-start.74 = (s32[985,1]{0,1:T(1,128)}, s32[985,1]{0,1:T(1,128)S(1)}, u32[]{:S(2)}) copy-start(s32[985,1]{0,1:T(1,128)S(1)} %get-tuple-element.143) | copy-start | bytes 11824
  74.5 51.7 %copy-start.72 = (s32[985,1]{0,1:T(1,128)}, s32[985,1]{0,1:T(1,128)S(1)}, u32[]{:S(2)}) copy-start(s32[985,1]{0,1:T(1,128)S(1)} %get-tuple-element.142) | copy-start | bytes 11824
  126.2 122.0 %copy-start.99 = (f32[985]{0:T(1024)}, f32[985]{0:T(1024)S(1)}, u32[]{:S(2)}) copy-start(f32[985]{0:T(1024)S(1)} %get-tuple-element.67) | copy-start | bytes 11824
  126.2 122.0 %copy-start.101 = (f32[985]{0:T(1024)}, f32[985]{0:T(1024)S(1)}, u32[]{:S(2)}) copy-start(f32[985]{0:T(1024)S(1)} %get-tuple-element.68) | copy-start | bytes 11824
  127.2 116.3 %copy-start.104 = (s32[985,1]{0,1:T(1,128)}, s32[985,1]{0,1:T(1,128)S(1)}, u32[]{:S(2)}) copy-start(s32[985,1]{0,1:T(1,128)S(1)} %get-tuple-element.112) | copy-start | bytes 11824
  127.2 121.0 %copy-start.106 = (s32[985,1]{0,1:T(1,128)}, s32[985,1]{0,1:T(1,128)S(1)}, u32[]{:S(2)}) copy-start(s32[985,1]{0,1:T(1,128)S(1)} %get-tuple-element.113) | copy-start | bytes 11824
  133.4 33.8 %all-to-all-start = ((bf16[8,308,512]{2,1,0:T(8,128)(2,1)}), bf16[8,308,512]{2,1,0:T(8,128)(2,1)S(1)}, u32[]{:S(2)}, u32[]{:S(2)}) async-start(bf16[8,308,512]{2,1,0:T(8,128)(2,1)} %reshape.291), calls=%async_computation | async-start | bytes 5111808 | tf_op jit(solution)/shard_map/all_to_all | solution.py:33
  137.1 116.3 %all-gather.25.cloned.1.call-start = ((), (), s32[]{:S(2)}) async-start(), calls=%async_computation.12 | async-start | bytes 1769472 | tf_op jit(solution)/shard_map/all_gather | solution.py:91
  194.9 46.4 %all-to-all-start.1 = ((bf16[8,308,512]{2,1,0:T(8,128)(2,1)}), bf16[8,308,512]{2,1,0:T(8,128)(2,1)S(1)}, u32[]{:S(2)}, u32[]{:S(2)}) async-start(bf16[8,308,512]{2,1,0:T(8,128)(2,1)} %reshape.293), calls=%async_computation.1 | async-start | bytes 5111808 | tf_op jit(solution)/shard_map/all_to_all | solution.py:33
  202.0 138.4 %all-gather.27.cloned.1.call-start = ((), (), s32[]{:S(2)}) async-start(), calls=%async_computation.13 | async-start | bytes 2621440 | tf_op jit(solution)/shard_map/all_gather | solution.py:97
  303.7 32.5 %all-to-all-start.2 = ((bf16[8,308,512]{2,1,0:T(8,128)(2,1)}), bf16[8,308,512]{2,1,0:T(8,128)(2,1)}, u32[]{:S(2)}, u32[]{:S(2)}) async-start(bf16[8,308,512]{2,1,0:T(8,128)(2,1)} %reshape.296), calls=%async_computation.2 | async-start | bytes 5111808 | tf_op jit(solution)/shard_map/all_to_all | solution.py:33
  308.2 46.6 %all-gather.29.cloned.1.call-start = ((), (), s32[]{:S(2)}) async-start(), calls=%async_computation.14 | async-start | bytes 2621440 | tf_op jit(solution)/shard_map/all_gather | solution.py:102
  369.9 35.1 %all-to-all-start.3 = ((bf16[8,308,512]{2,1,0:T(8,128)(2,1)}), bf16[8,308,512]{2,1,0:T(8,128)(2,1)}, u32[]{:S(2)}, u32[]{:S(2)}) async-start(bf16[8,308,512]{2,1,0:T(8,128)(2,1)} %reshape.298), calls=%async_computation.3 | async-start | bytes 5111808 | tf_op jit(solution)/shard_map/all_to_all | solution.py:33
  505.1 33.7 %all-to-all-start.5 = ((bf16[8,308,512]{2,1,0:T(8,128)(2,1)}), bf16[8,308,512]{2,1,0:T(8,128)(2,1)}, u32[]{:S(2)}, u32[]{:S(2)}) async-start(bf16[8,308,512]{2,1,0:T(8,128)(2,1)} %reshape.302), calls=%async_computation.5 | async-start | bytes 5111808 | tf_op jit(solution)/shard_map/all_to_all | solution.py:33
  614.7 36.1 %all-to-all-start.6 = ((bf16[8,308,512]{2,1,0:T(8,128)(2,1)}), bf16[8,308,512]{2,1,0:T(8,128)(2,1)}, u32[]{:S(2)}, u32[]{:S(2)}) async-start(bf16[8,308,512]{2,1,0:T(8,128)(2,1)} %reshape.305), calls=%async_computation.6 | async-start | bytes 5111808 | tf_op jit(solution)/shard_map/all_to_all | solution.py:33
  685.1 70.9 %all-to-all-start.7 = ((bf16[8,308,512]{2,1,0:T(8,128)(2,1)}), bf16[8,308,512]{2,1,0:T(8,128)(2,1)}, u32[]{:S(2)}, u32[]{:S(2)}) async-start(bf16[8,308,512]{2,1,0:T(8,128)(2,1)} %reshape.307), calls=%async_computation.7 | async-start | bytes 5111808 | tf_op jit(solution)/shard_map/all_to_all | solution.py:33
  693.1 156.8 %reduce-scatter.4.cloned.1.call-start = ((), (), s32[]{:S(2)}) async-start(), calls=%async_computation.15 | async-start | bytes 294912
  815.7 98.8 %all-reduce.6.cloned.1.call-start = ((), (), s32[]{:S(2)}) async-start(), calls=%async_computation.16 | async-start | bytes 4194304
  (111 other events, 680.2 us)
Sparse Core Ops, SparseCore 0:
  20.8 28.3 all-gather.18
  51.3 45.0 all-gather.20
  98.0 44.4 all-gather.22
  149.4 28.2 all-gather.24
  204.1 44.5 all-gather.26
  310.2 44.5 all-gather.28
  815.8 34.0 reduce-scatter.3
  853.2 61.2 all-reduce.5

commit v2 on v1

--- a/solution.py
+++ b/solution.py
@@ -1,6 +1,10 @@
+import functools
+
 import jax
 import jax.numpy as jnp
 from jax import lax
+from jax.experimental import pallas as pl
+from jax.experimental.pallas import tpu as pltpu
 from jax.sharding import PartitionSpec as P
 
 HEAD_DIM = 64
@@ -29,15 +33,247 @@
     )
 
 
-def exchange(rows):
-    return lax.all_to_all(rows, "expert", split_axis=0, concat_axis=0, tiled=True)
+def gelu_parts(rows_in):
+    half = 0.5 * (1.0 + lax.erf(rows_in * 0.7071067811865476))
+    slope = half + rows_in * (jnp.exp(-0.5 * rows_in * rows_in) * 0.3989422804014327)
+    return rows_in * half, slope
+
+
+def meet_peers(me, peers):
+    barrier = pltpu.get_barrier_semaphore()
+
+    def greet(step, carry):
+        pl.semaphore_signal(
+            barrier,
+            inc=1,
+            device_id={"expert": lax.rem(me + step, peers)},
+            device_id_type=pl.DeviceIdType.MESH,
+        )
+        return carry
+
+    lax.fori_loop(1, peers, greet, 0)
+    pl.semaphore_wait(barrier, peers - 1)
+
+
+def send_chunk(source, landing, sends, arrivals, step, peer):
+    return pltpu.make_async_remote_copy(
+        src_ref=source,
+        dst_ref=landing,
+        send_sem=sends.at[step],
+        recv_sem=arrivals.at[step],
+        device_id={"expert": peer},
+        device_id_type=pl.DeviceIdType.MESH,
+    )
+
+
+def exchange_chunks(peers, work, out_rows, landed, results, back, sems):
+    out_send, out_recv, back_send, back_recv = sems
+    me = lax.axis_index("expert")
+    meet_peers(me, peers)
+
+    def start_out(step, carry):
+        peer = lax.rem(me + step, peers)
+        send_chunk(out_rows.at[peer], landed.at[me], out_send, out_recv, step, peer).start()
+        return carry
+
+    lax.fori_loop(1, peers, start_out, 0)
+    landed[me] = out_rows[me]
+
+    def one_chunk(step, carry):
+        peer = lax.rem(me + peers - step, peers)
+
+        @pl.when(step > 0)
+        def _():
+            send_chunk(
+                out_rows.at[peer], landed.at[peer], out_send, out_recv, step, peer
+            ).wait_recv()
+
+        work(step, peer)
+
+        @pl.when(step > 0)
+        def _():
+            send_chunk(results.at[step], back.at[me], back_send, back_recv, step, peer).start()
+
+        return carry
+
+    lax.fori_loop(0, peers, one_chunk, 0)
+    back[me] = results[0]
+
+    def finish(step, carry):
+        ahead = lax.rem(me + step, peers)
+        send_chunk(out_rows.at[ahead], landed.at[me], out_send, out_recv, step, ahead).wait_send()
+        last = send_chunk(results.at[step], back.at[ahead], back_send, back_recv, step, ahead)
+        last.wait_send()
+        last.wait_recv()
+        return carry
+
+    lax.fori_loop(1, peers, finish, 0)
+
+
+def forward_kernel(
+    peers, parts, rows_ref, win_ref, wout_ref, landed, back, results, total, *sems
+):
+    width = win_ref.shape[1] // parts
+
+    def work(step, peer):
+        chunk = landed[peer]
+        for part in range(parts):
+            cols = slice(part * width, (part + 1) * width)
+            before = jnp.dot(chunk, win_ref[:, cols], preferred_element_type=jnp.float32)
+            hidden = gelu_exact(before).astype(jnp.bfloat16)
+            term = jnp.dot(hidden, wout_ref[cols, :], preferred_element_type=jnp.float32)
+            if part == 0:
+                total[...] = term
+            elif part < parts - 1:
+                total[...] += term
+            else:
+                results[step] = (total[...] + term).astype(jnp.bfloat16)
+
+    exchange_chunks(peers, work, rows_ref, landed, results, back, sems)
+
+
+def backward_kernel(
+    peers,
+    parts,
+    rows_ref,
+    arrived_ref,
+    win_ref,
+    wout_ref,
+    back,
+    win_grad,
+    wout_grad,
+    landed,
+    results,
+    total,
+    hidden_all,
+    before_all,
+    *sems,
+):
+    width = win_ref.shape[1] // parts
+    own = lax.axis_index("tensor") * width
+    win_grad[...] = jnp.zeros_like(win_grad)
+    wout_grad[...] = jnp.zeros_like(wout_grad)
+
+    def work(step, peer):
+        chunk = arrived_ref[peer]
+        grad_chunk = landed[peer]
+        for part in range(parts):
+            cols = slice(part * width, (part + 1) * width)
+            before = jnp.dot(chunk, win_ref[:, cols], preferred_element_type=jnp.float32)
+            value, slope = gelu_parts(before)
+            grad_hidden = contract_last(grad_chunk, wout_ref[cols, :])
+            grad_before = (grad_hidden * slope).astype(jnp.bfloat16)
+            hidden_all[:, cols] = value.astype(jnp.bfloat16)
+            before_all[:, cols] = grad_before
+            term = contract_last(grad_before, win_ref[:, cols])
+            if part == 0:
+                total[...] = term
+            elif part < parts - 1:
+                total[...] += term
+            else:
+                results[step] = (total[...] + term).astype(jnp.bfloat16)
+        mine = pl.ds(pl.multiple_of(own, width), width)
+        wout_grad[...] += contract_rows(hidden_all[:, mine], grad_chunk)
+        win_grad[...] += contract_rows(chunk, before_all[:, mine])
+
+    exchange_chunks(peers, work, rows_ref, landed, results, back, sems)
+
+
+def sum_kernel(peers, rows_ref, sum_ref, landed, sends, arrivals):
+    me = lax.axis_index("expert")
+    meet_peers(me, peers)
+
+    def start_out(step, carry):
+        peer = lax.rem(me + step, peers)
+        send_chunk(rows_ref.at[peer], landed.at[me], sends, arrivals, step, peer).start()
+        return carry
+
+    lax.fori_loop(1, peers, start_out, 0)
+    landed[me] = rows_ref[me]
+
+    def finish(step, carry):
+        peer = lax.rem(me + peers - step, peers)
+        one = send_chunk(rows_ref.at[peer], landed.at[peer], sends, arrivals, step, peer)
+        one.wait_send()
+        one.wait_recv()
+        return carry
+
+    lax.fori_loop(1, peers, finish, 0)
+    sum_ref[...] = landed[0].astype(jnp.float32)
+
+    def add_one(source, carry):
+        sum_ref[...] += landed[source].astype(jnp.float32)
+        return carry
+
+    lax.fori_loop(1, peers, add_one, 0)
+
+
+def sum_shares(rows):
+    peers = rows.shape[0]
+    return pl.pallas_call(
+        functools.partial(sum_kernel, peers),
+        out_shape=jax.ShapeDtypeStruct(rows.shape[1:], jnp.float32),
+        in_specs=whole_in_vmem(1),
+        out_specs=whole_in_vmem(1)[0],
+        scratch_shapes=[pltpu.VMEM(rows.shape, rows.dtype)] + exchange_sems(peers)[:2],
+        compiler_params=pltpu.CompilerParams(collective_id=2, has_side_effects=True),
+    )(rows)
+
+
+def whole_in_vmem(count):
+    return [pl.BlockSpec(memory_space=pltpu.VMEM)] * count
+
+
+def exchange_sems(peers):
+    return [pltpu.SemaphoreType.DMA((peers,)) for _ in range(4)]
+
+
+def experts_forward(rows, win, wout, parts):
+    peers, capacity, width = rows.shape
+    like = jax.ShapeDtypeStruct(rows.shape, jnp.bfloat16)
+    return pl.pallas_call(
+        functools.partial(forward_kernel, peers, parts),
+        out_shape=(like, like),
+        in_specs=whole_in_vmem(3),
+        out_specs=tuple(whole_in_vmem(2)),
+        scratch_shapes=[
+            pltpu.VMEM(rows.shape, jnp.bfloat16),
+            pltpu.VMEM((capacity, width), jnp.float32),
+        ]
+        + exchange_sems(peers),
+        compiler_params=pltpu.CompilerParams(collective_id=0, has_side_effects=True),
+    )(rows, win, wout)
+
+
+def experts_backward(rows, arrived, win, wout, parts):
+    peers, capacity, width = rows.shape
+    inner = win.shape[1]
+    return pl.pallas_call(
+        functools.partial(backward_kernel, peers, parts),
+        out_shape=(
+            jax.ShapeDtypeStruct(rows.shape, jnp.bfloat16),
+            jax.ShapeDtypeStruct((width, inner // parts), jnp.float32),
+            jax.ShapeDtypeStruct((inner // parts, width), jnp.float32),
+        ),
+        in_specs=whole_in_vmem(4),
+        out_specs=tuple(whole_in_vmem(3)),
+        scratch_shapes=[
+            pltpu.VMEM(rows.shape, jnp.bfloat16),
+            pltpu.VMEM(rows.shape, jnp.bfloat16),
+            pltpu.VMEM((capacity, width), jnp.float32),
+            pltpu.VMEM((capacity, inner), jnp.bfloat16),
+            pltpu.VMEM((capacity, inner), jnp.bfloat16),
+        ]
+        + exchange_sems(peers),
+        compiler_params=pltpu.CompilerParams(collective_id=1, has_side_effects=True),
+    )(rows, arrived, win, wout)
 
 
 def own_part(rows, width, axis=1):
     return lax.dynamic_slice_in_dim(rows, lax.axis_index("tensor") * width, width, axis=axis)
 
 
-def slot_plan(chosen, rank_rows, experts, capacity):
+def slot_plan(chosen, rank_rows, experts, capacity, spacing):
     columns = lax.broadcasted_iota(jnp.int32, (1, experts), 1)
     first_hot = (chosen[:, 0:1] == columns).astype(jnp.bfloat16)
     second = (chosen[:, 1:2] == columns).astype(jnp.bfloat16)
@@ -50,7 +286,7 @@
     slot_first = jnp.sum(count_first * first_f, axis=1)
     slot_second = jnp.sum((filled + count_second) * second_f, axis=1)
     slot_nums = jnp.stack([slot_first, slot_second], axis=1).astype(jnp.int32)
-    target = jnp.where(slot_nums < capacity, chosen * capacity + slot_nums, experts * capacity)
+    target = jnp.where(slot_nums < capacity, chosen * spacing + slot_nums, experts * spacing)
     return (target, first_f, second_f)
 
 
@@ -75,24 +311,37 @@
     local_heads = head_cols * lax.axis_size("tensor") // HEAD_DIM
     layers = attend_in.shape[0]
     capacity = max(2, (10 * tokens + 4 * experts - 1) // (4 * experts))
-    slots_all = experts * capacity
+    spacing = -(-capacity // 16) * 16
+    slots_all = experts * spacing
+    peers_tensor = lax.axis_size("tensor")
     score_scale = HEAD_DIM ** (-0.5)
-    layer_ids = range(layers)
-    gains_full = lax.all_gather(norm_gains.astype(jnp.bfloat16), "expert", axis=2, tiled=True)
-    router_full = lax.all_gather(router.astype(jnp.bfloat16), "expert", axis=2, tiled=True)
-    in_full = []
-    out_full = []
-    win_full = []
-    wout_full = []
-    for layer_index in layer_ids:
-        in_part = lax.all_gather(
-            attend_in[layer_index].astype(jnp.bfloat16), "tensor", axis=2, tiled=True
-        )
-        in_full.append(lax.all_gather(in_part, "expert", axis=1, tiled=True))
-        out_part = lax.all_gather(
-            attend_out[layer_index].astype(jnp.bfloat16), "tensor", axis=0, tiled=True
-        )
-        out_full.append(lax.all_gather(out_part, "expert", axis=1, tiled=True))
+    row_share = attend_in.shape[2]
+    gain_share = norm_gains.shape[2]
+    in_full, out_full, router_full, gains_full, win_full, wout_full = [], [], [], [], [], []
+    for layer_index in range(layers):
+        out_share = attend_out[layer_index].T[None]
+        packed = [
+            jnp.concatenate([attend_in[layer_index], out_share], axis=0).reshape(-1),
+            router[layer_index].reshape(-1),
+            norm_gains[layer_index].reshape(-1),
+        ]
+        sizes = [piece.shape[0] for piece in packed]
+        flat = jnp.concatenate(packed).astype(jnp.bfloat16)
+        flat = jnp.pad(flat, (0, -flat.shape[0] % 2048)).reshape(-1, 128)
+        across = lax.all_gather(flat, "tensor", axis=0)
+        whole = lax.all_gather(across, "expert", axis=0).reshape(experts, peers_tensor, -1)
+        mats = whole[:, :, : sizes[0]].reshape(experts, peers_tensor, 4, row_share, head_cols)
+        mats = mats.transpose(2, 0, 3, 1, 4).reshape(4, model_width, head_cols * peers_tensor)
+        in_full.append(mats[:3])
+        out_full.append(mats[3])
+        smalls = whole[:, 0, sizes[0] :]
+        router_full.append(smalls[:, : sizes[1]].T)
+        gains_full.append(
+            smalls[:, sizes[1] : sizes[1] + sizes[2]]
+            .reshape(experts, 2, gain_share)
+            .transpose(1, 0, 2)
+            .reshape(2, model_width)
+        )
         win_full.append(
             lax.all_gather(
                 expert_in[layer_index, 0].astype(jnp.bfloat16), "tensor", axis=1, tiled=True
@@ -125,14 +374,14 @@
             .astype(jnp.bfloat16)
             .reshape(tokens, -1)
         )
-        middle = stream + jnp.dot(
-            mixed_heads, out_full[layer_index], preferred_element_type=jnp.float32
-        )
+        middle = stream + contract_last(mixed_heads, out_full[layer_index])
         normed_two = norm_rows(middle, gains_now[1]).astype(jnp.bfloat16)
         logits = jnp.dot(normed_two, router_full[layer_index], preferred_element_type=jnp.float32)
         probs_all = jax.nn.softmax(logits, axis=-1)
         chosen = routes[layer_index]
-        target, first_f, second_f = slot_plan(chosen, priority[layer_index], experts, capacity)
+        target, first_f, second_f = slot_plan(
+            chosen, priority[layer_index], experts, capacity, spacing
+        )
         gate_values = jnp.stack(
             [jnp.sum(probs_all * first_f, axis=1), jnp.sum(probs_all * second_f, axis=1)], axis=1
         )
@@ -141,17 +390,13 @@
         pick_both = pick_first + pick_second
 
         dispatched = contract_rows(pick_both, normed_two).astype(jnp.bfloat16)
-        arrived = exchange(dispatched.reshape(experts, capacity, model_width)).reshape(
-            slots_all, model_width
-        )
-        before = jnp.dot(arrived, win_full[layer_index], preferred_element_type=jnp.float32)
-        hidden = gelu_exact(before).astype(jnp.bfloat16)
-        expert_rows = jnp.dot(
-            hidden, wout_full[layer_index], preferred_element_type=jnp.float32
-        ).astype(jnp.bfloat16)
-        returned = exchange(expert_rows.reshape(experts, capacity, model_width)).reshape(
-            slots_all, model_width
-        )
+        arrived, returned = experts_forward(
+            dispatched.reshape(experts, spacing, model_width),
+            win_full[layer_index],
+            wout_full[layer_index],
+            peers_tensor,
+        )
+        returned = returned.reshape(slots_all, model_width)
         rows_first = jnp.dot(pick_first, returned, preferred_element_type=jnp.float32)
         rows_second = jnp.dot(pick_second, returned, preferred_element_type=jnp.float32)
         output = middle + gate_values[:, 0:1] * rows_first + gate_values[:, 1:2] * rows_second
@@ -181,6 +426,7 @@
         stream = output
     upstream = cotangent
     grads_in, grads_out, grads_router, grads_gain, grads_win, grads_wout = ([], [], [], [], [], [])
+    grads_shared = []
     for layer_index in reversed(range(layers)):
         (
             stream_in,
@@ -210,32 +456,29 @@
         grad_slots = (
             contract_rows(pick_first, scaled_first) + contract_rows(pick_second, scaled_second)
         ).astype(jnp.bfloat16)
-        grad_arrived = exchange(grad_slots.reshape(experts, capacity, model_width)).reshape(
-            slots_all, model_width
-        )
-        before = jnp.dot(arrived, win_full[layer_index], preferred_element_type=jnp.float32)
-        hidden = gelu_exact(before).astype(jnp.bfloat16)
-        grads_wout.append(contract_rows(own_part(hidden, hidden_cols), grad_arrived))
-        grad_hidden = contract_last(grad_arrived, wout_full[layer_index])
-        grad_before = jax.vjp(gelu_exact, before)[1](grad_hidden)[0].astype(jnp.bfloat16)
-        grads_win.append(contract_rows(arrived, own_part(grad_before, hidden_cols)))
-        grad_rows = contract_last(grad_before, win_full[layer_index]).astype(jnp.bfloat16)
-        grad_dispatched = exchange(grad_rows.reshape(experts, capacity, model_width)).reshape(
-            slots_all, model_width
-        )
+        grad_dispatched, win_grad, wout_grad = experts_backward(
+            grad_slots.reshape(experts, spacing, model_width),
+            arrived,
+            win_full[layer_index],
+            wout_full[layer_index],
+            peers_tensor,
+        )
+        grads_win.append(win_grad)
+        grads_wout.append(wout_grad)
+        grad_dispatched = grad_dispatched.reshape(slots_all, model_width)
         grad_normed = jnp.dot(pick_both, grad_dispatched, preferred_element_type=jnp.float32)
         grad_probs = first_f * gate_first[:, None] + second_f * gate_second[:, None]
         grad_logits = (
             probs_all * (grad_probs - jnp.sum(probs_all * grad_probs, axis=1, keepdims=True))
         ).astype(jnp.bfloat16)
-        grads_router.append(contract_rows(normed_two, grad_logits))
+        router_grad = contract_rows(grad_logits, normed_two)
         grad_normed = grad_normed + contract_last(grad_logits, router_full[layer_index])
         norm_back = jax.vjp(norm_rows, middle, gains_now[1])[1](grad_normed)
         grad_middle = upstream + norm_back[0]
         grad_branch = grad_middle.astype(jnp.bfloat16)
-        grads_out.append(contract_rows(own_part(mixed_heads, head_cols), grad_branch))
+        out_grad = contract_rows(grad_branch, own_part(mixed_heads, head_cols))
         grad_mixed = (
-            contract_last(grad_branch, out_full[layer_index])
+            jnp.dot(grad_branch, out_full[layer_index], preferred_element_type=jnp.float32)
             .astype(jnp.bfloat16)
             .reshape(images, SEQ, local_heads, HEAD_DIM)
         )
@@ -268,40 +511,52 @@
             * score_scale
         ).astype(jnp.bfloat16)
         grad_triple = jnp.stack([grad_query, grad_key, grad_value]).reshape(3, tokens, -1)
-        grads_in.append(
-            jnp.einsum(
-                "td,jth->jdh",
-                normed,
-                own_part(grad_triple, head_cols, 2),
-                preferred_element_type=jnp.float32,
-            )
+        in_grad = jnp.einsum(
+            "td,jth->jdh",
+            normed,
+            own_part(grad_triple, head_cols, 2),
+            preferred_element_type=jnp.float32,
         )
         project = in_full[layer_index]
         grad_normed_one = jnp.einsum(
             "jth,jdh->td", grad_triple, project, preferred_element_type=jnp.float32
         )
         norm_back_one = jax.vjp(norm_rows, stream_in, gains_now[0])[1](grad_normed_one)
-        grads_gain.append(jnp.stack([norm_back_one[1], norm_back[1]]))
+        mats_grad = jnp.concatenate([in_grad, out_grad[None]], axis=0)
+        mats_grad = mats_grad.reshape(4, experts, row_share, head_cols).transpose(1, 0, 2, 3)
+        gain_grad = jnp.stack([norm_back_one[1], norm_back[1]]).reshape(2, experts, gain_share)
+        smalls = jnp.concatenate(
+            [router_grad, gain_grad.transpose(1, 0, 2).reshape(experts, -1)], axis=1
+        )
+        smalls = jnp.pad(smalls, ((0, 0), (0, -smalls.shape[1] % 2048)))
+        grads_shared.append(
+            jnp.concatenate(
+                [mats_grad.reshape(experts, -1, 128), smalls.reshape(experts, -1, 128)], axis=1
+            ).astype(jnp.bfloat16)
+        )
         upstream = grad_middle + norm_back_one[0]
-    in_grad_all = jnp.stack(grads_in[::-1])
-    out_grad_all = jnp.stack(grads_out[::-1])
-    router_grad_all = jnp.stack(grads_router[::-1])
-    gain_grad_all = jnp.stack(grads_gain[::-1])
-    reduced = (
-        lax.psum_scatter(in_grad_all, "expert", scatter_dimension=2, tiled=True),
-        lax.psum_scatter(out_grad_all, "expert", scatter_dimension=2, tiled=True),
-        lax.psum_scatter(router_grad_all, "expert", scatter_dimension=2, tiled=True),
-        lax.psum_scatter(gain_grad_all, "expert", scatter_dimension=2, tiled=True),
-    )
+    total_rows = grads_shared[0].shape[1]
+    mat_rows = 4 * row_share * head_cols // 128
+    shared_all = sum_shares(jnp.concatenate(grads_shared, axis=1))
+    for order in range(layers):
+        shared = shared_all[order * total_rows : (order + 1) * total_rows]
+        mats_own = shared[:mat_rows].reshape(4, row_share, head_cols)
+        small_own = shared[mat_rows:].reshape(-1)
+        grads_in.append(mats_own[:3])
+        grads_out.append(mats_own[3].T)
+        grads_router.append(small_own[:model_width, None])
+        grads_gain.append(
+            small_own[model_width : model_width + 2 * gain_share].reshape(2, gain_share)
+        )
     win_grad_all = jnp.stack(grads_win[::-1])[:, None]
     wout_grad_all = jnp.stack(grads_wout[::-1])[:, None]
     return (
         stream,
         upstream,
-        reduced[0],
-        reduced[1],
-        reduced[2],
-        reduced[3],
+        jnp.stack(grads_in[::-1]),
+        jnp.stack(grads_out[::-1]),
+        jnp.stack(grads_router[::-1]),
+        jnp.stack(grads_gain[::-1]),
         win_grad_all,
         wout_grad_all,
     )

time: 937 us -> 726 us (0.77)
  Pallas kernels: 0 us -> 283 us
  waiting for transfers between devices: 205 us -> 34.7 us
  blocking collectives: 187 us -> 25.9 us
  matrix products: 244 us -> 136 us
  starting transfers between devices: 44.1 us -> 0.24 us
    pallas_call x0 -> x5, Pallas kernels: none -> 283 us  [the longest x2 133 us: experts_backward(): pl.pallas_call(functools.partial(backward_kernel, peers, parts), out_shap...]
    all_to_all x7 -> x0, waiting for transfers between devices: 117 us -> none  [exchange(): lax.all_to_all(rows, 'expert', split_axis=0, concat_axis=0, tiled=True)]
    unnamed x10 -> x6, waiting for transfers between devices: 87.1 us -> 1.12 us
    all_gather x8 -> x2, blocking collectives: 103 us -> 25.9 us  [local(): across = lax.all_gather(flat, 'tensor', axis=0)]
    dot_general x6 -> x2, matrix products: 52.9 us -> 2.36 us  [local(): jnp.dot(grad_branch, out_full[layer_index], preferred_element_type=jnp.fl...]
    unnamed x1 -> x0, blocking collectives: 44.9 us -> none
    all_to_all x7 -> x0, starting transfers between devices: 43.9 us -> none  [exchange(): lax.all_to_all(rows, 'expert', split_axis=0, concat_axis=0, tiled=True)]
    dot_general x8 -> x4, matrix products: 47.8 us -> 8.27 us  [contract_last(): lax.dot_general(left_side, right_side, (((1,), (1,)), ((), ())), preferre...]
  transfers between devices with their start and end apart: 15 -> 6, of which waited for: 8 -> 2; matrix products, arithmetic and copies ran while one was open for 23% -> 24% of each run, Pallas kernels for 0% -> 9%
where the time goes in v2:
time: 726 us; the launch traced here: 720 us
  Pallas kernels  283 us (39%)
  local copies, waits for them, and re-layouts  190 us (26%)
  matrix products  136 us (19%)
  waiting for transfers between devices  34.7 us (5%)
  other arithmetic  34.5 us (5%)
  blocking collectives  25.9 us (4%)
  between operations  16.2 us (2%)
    pallas_call x2, Pallas kernels, experts_backward(): pl.pallas_call(functools.partial(backward_kernel, peers, parts), out_shap...  133 us
    pallas_call x2, Pallas kernels, experts_forward(): pl.pallas_call(functools.partial(forward_kernel, peers, parts), out_shape...  129 us
    dot_general x10, matrix products, contract_rows(): lax.dot_general(left_side, right_side, (((0,), (0,)), ((), ())), preferre...  35.5 us
    all_gather x2, waiting for transfers between devices, local(): lax.all_gather(across, 'expert', axis=0).reshape(experts, peers_tensor, -1)  33.5 us
    all_gather x2, blocking collectives, local(): across = lax.all_gather(flat, 'tensor', axis=0)  25.9 us
    unnamed x238, local copies, waits for them, and re-layouts  21.3 us
    pallas_call x1, Pallas kernels, sum_shares(): pl.pallas_call(functools.partial(sum_kernel, peers), out_shape=jax.ShapeD...  20.4 us
    another operation x8, local copies, waits for them, and re-layouts, local(): jnp.stack([grad_query, grad_key, grad_value]).reshape(3, tokens, -1)  19.9 us
  transfers between devices with their start and end apart: 6, of which 2 were waited for; matrix products, arithmetic and copies ran while one was open for 24% of the time, Pallas kernels for 9%

profile of v2, /device:TPU:1, one launch (start us, length us, event | category | flops | bytes accessed | tf_op | source)
XLA Modules:
  0.0 719.8 jit_solution(10933821077388567057)
XLA Ops:
  10.7 14.1 %all_gather.30 = bf16[4,272,128]{2,1,0:T(8,128)(2,1)} all-gather(bf16[1,272,128]{2,1,0:T(8,128)(2,1)S(1)} %fusion.138), channel_id=1, replica_groups=mesh['expert'=8,'tensor'=4] {'tensor'}, dimensions={0}, use_global_device_ids=true | all-gather | bytes 348160 | tf_op jit(solution)/shard_map/all_gather | solution.py:331
  25.0 11.8 %all_gather.35 = bf16[4,272,128]{2,1,0:T(8,128)(2,1)} all-gather(bf16[1,272,128]{2,1,0:T(8,128)(2,1)S(1)} %fusion.141), channel_id=1, replica_groups=mesh['expert'=8,'tensor'=4] {'tensor'}, dimensions={0}, use_global_device_ids=true | all-gather | bytes 348160 | tf_op jit(solution)/shard_map/all_gather | solution.py:331
  44.8 12.2 %all-gather.13.cloned.1.call-done = bf16[32,272,128]{2,1,0:T(8,128)(2,1)} async-done(((bf16[4,272,128]{2,1,0:T(8,128)(2,1)}), bf16[32,272,128]{2,1,0:T(8,128)(2,1)}) %all-gather.13.cloned.1.call-update) | async-done | bytes 2228240 | tf_op jit(solution)/shard_map/all_gather | solution.py:332
  65.9 21.4 %all-gather.19.cloned.1.call-done = bf16[32,272,128]{2,1,0:T(8,128)(2,1)} async-done(((bf16[4,272,128]{2,1,0:T(8,128)(2,1)}), bf16[32,272,128]{2,1,0:T(8,128)(2,1)}) %all-gather.19.cloned.1.call-update) | async-done | bytes 2228240 | tf_op jit(solution)/shard_map/all_gather | solution.py:332
  96.0 4.8 reshape.398
  104.2 4.8 reshape.399
  175.5 5.6 fusion.51
  181.1 63.5 %shard_map.161 = (bf16[8,320,512]{2,1,0:T(8,128)(2,1)}, bf16[8,320,512]{2,1,0:T(8,128)(2,1)}) custom-call(bf16[8,320,512]{2,1,0:T(8,128)(2,1)} %bitcast.270, bf16[512,2048]{1,0:T(8,128)(2,1)} %bitcast.256, bf16[2048,512]{1,0:T(8,128)(2,1)} %bitcast.258), custom_call_target="tpu_custom_call" | custom-call | tf_op jit(solution)/shard_map/pallas_call | solution.py:234
  244.6 4.7 fusion.10
  249.4 4.9 fusion.192
  291.0 6.5 fusion.69
  310.4 5.6 fusion.48
  315.9 65.7 %shard_map.162 = (bf16[8,320,512]{2,1,0:T(8,128)(2,1)}, bf16[8,320,512]{2,1,0:T(8,128)(2,1)}) custom-call(bf16[8,320,512]{2,1,0:T(8,128)(2,1)} %bitcast.271, bf16[512,2048]{1,0:T(8,128)(2,1)} %bitcast.260, bf16[2048,512]{1,0:T(8,128)(2,1)} %bitcast.262), custom_call_target="tpu_custom_call" | custom-call | tf_op jit(solution)/shard_map/pallas_call | solution.py:234
  381.6 4.7 fusion.1
  395.5 5.8 add_convert_fusion.1
  401.3 66.6 %shard_map.163 = (bf16[8,320,512]{2,1,0:T(8,128)(2,1)}, f32[512,512]{1,0:T(8,128)}, f32[512,512]{1,0:T(8,128)}) custom-call(bf16[8,320,512]{2,1,0:T(8,128)(2,1)} %bitcast.269, bf16[8,320,512]{2,1,0:T(8,128)(2,1)} %get-tuple-element.20.arrived_ref, bf16[512,2048]{1,0:T(8,128)(2,1)} %bitcast.261, bf16[2048,512]{1,0:T(8,128)(2,1)} %bitcast.263), custom_call_target="tpu_custom_call" | custom-call | tf_op jit(solution)/shard_map/pallas_call | solution.py:251
  467.9 4.7 fusion.28
  488.4 6.5 fusion.70
  495.0 4.8 multiply_reduce_fusion.1
  543.8 5.7 add_convert_fusion
  549.5 66.7 %shard_map.164 = (bf16[8,320,512]{2,1,0:T(8,128)(2,1)}, f32[512,512]{1,0:T(8,128)}, f32[512,512]{1,0:T(8,128)}) custom-call(bf16[8,320,512]{2,1,0:T(8,128)(2,1)} %bitcast.268, bf16[8,320,512]{2,1,0:T(8,128)(2,1)} %get-tuple-element.22.arrived_ref, bf16[512,2048]{1,0:T(8,128)(2,1)} %bitcast.257, bf16[2048,512]{1,0:T(8,128)(2,1)} %bitcast.259), custom_call_target="tpu_custom_call" | custom-call | tf_op jit(solution)/shard_map/pallas_call | solution.py:251
  630.8 6.2 fusion.71
  637.0 5.0 multiply_reduce_fusion
  675.4 20.4 %shard_map.165 = f32[544,128]{1,0:T(8,128)} custom-call(bf16[8,544,128]{2,1,0:T(8,128)(2,1)} %pad_maximum_fusion.rows_ref), custom_call_target="tpu_custom_call" | custom-call | tf_op jit(solution)/shard_map/pallas_call | solution.py:213
  (454 shorter events, 281.1 us)
Async XLA Ops:
  7.2 29.7 %copy-start.42 = (f32[2,1,512,512]{3,2,1,0:T(8,128)S(1)}, f32[2,1,512,512]{3,2,1,0:T(8,128)}, u32[]{:S(2)}) copy-start(f32[2,1,512,512]{3,2,1,0:T(8,128)} %param.18) | copy-start | bytes 6291460
  7.2 49.8 %all-gather.13.cloned.1.call-start = ((), (), s32[]{:S(2)}) async-start(), calls=%async_computation | async-start | bytes 2506752 | tf_op jit(solution)/shard_map/all_gather | solution.py:332
  24.8 62.4 %all-gather.19.cloned.1.call-start = ((), (), s32[]{:S(2)}) async-start(), calls=%async_computation.3 | async-start | bytes 2506752 | tf_op jit(solution)/shard_map/all_gather | solution.py:332
  36.8 144.3 %all-gather.15.cloned.1.call-start = ((), (), s32[]{:S(2)}) async-start(), calls=%async_computation.1 | async-start | bytes 2621440 | tf_op jit(solution)/shard_map/all_gather | solution.py:346
  38.1 143.1 %all-gather.17.cloned.1.call-start = ((), (), s32[]{:S(2)}) async-start(), calls=%async_computation.2 | async-start | bytes 2621440 | tf_op jit(solution)/shard_map/all_gather | solution.py:351
  40.2 275.7 %all-gather.21.cloned.1.call-start = ((), (), s32[]{:S(2)}) async-start(), calls=%async_computation.4 | async-start | bytes 2621440 | tf_op jit(solution)/shard_map/all_gather | solution.py:346
  40.8 275.1 %all-gather.23.cloned.1.call-start = ((), (), s32[]{:S(2)}) async-start(), calls=%async_computation.5 | async-start | bytes 2621440 | tf_op jit(solution)/shard_map/all_gather | solution.py:351
  41.7 87.3 %copy-start.69 = (f32[985]{0:T(1024)}, f32[985]{0:T(1024)S(1)}, u32[]{:S(2)}) copy-start(f32[985]{0:T(1024)S(1)} %broadcast_multiply_fusion.3) | copy-start | bytes 11824
  42.1 19.2 %copy-start.75 = (f32[985]{0:T(1024)}, f32[985]{0:T(1024)S(1)}, u32[]{:S(2)}) copy-start(f32[985]{0:T(1024)S(1)} %multiply_reduce_fusion.17) | copy-start | bytes 11824
  42.1 86.9 %copy-start.81 = (f32[985]{0:T(1024)}, f32[985]{0:T(1024)S(1)}, u32[]{:S(2)}) copy-start(f32[985]{0:T(1024)S(1)} %fusion.172) | copy-start | bytes 11824
  42.2 132.2 %copy-start.67 = (s32[985,1]{0,1:T(1,128)}, s32[985,1]{0,1:T(1,128)S(1)}, u32[]{:S(2)}) copy-start(s32[985,1]{0,1:T(1,128)S(1)} %get-tuple-element.159) | copy-start | bytes 11824
  42.2 132.4 %copy-start.65 = (s32[985,1]{0,1:T(1,128)}, s32[985,1]{0,1:T(1,128)S(1)}, u32[]{:S(2)}) copy-start(s32[985,1]{0,1:T(1,128)S(1)} %get-tuple-element.158) | copy-start | bytes 11824
  103.9 70.1 %copy-start.63 = (bf16[8,1,2048]{2,0,1:T(8,128)(2,1)}, bf16[8,1,2048]{2,0,1:T(8,128)(2,1)S(1)}, u32[]{:S(2)}) copy-start(bf16[8,1,2048]{2,0,1:T(8,128)(2,1)S(1)} %copy.229) | copy-start | bytes 98308
  104.1 68.1 %copy-start.86 = (f32[512]{0:T(512)}, f32[512]{0:T(512)S(1)}, u32[]{:S(2)}) copy-start(f32[512]{0:T(512)S(1)} %mul.434) | copy-start | bytes 6148
  104.2 24.8 %copy-start.88 = (f32[512]{0:T(512)}, f32[512]{0:T(512)S(1)}, u32[]{:S(2)}) copy-start(f32[512]{0:T(512)S(1)} %mul.427) | copy-start | bytes 6148
  112.4 142.3 %copy-start.90 = (f32[512]{0:T(512)}, f32[512]{0:T(512)S(1)}, u32[]{:S(2)}) copy-start(f32[512]{0:T(512)S(1)} %mul.449) | copy-start | bytes 6148
  174.6 74.8 %copy-start.93 = (f32[985]{0:T(1024)}, f32[985]{0:T(1024)S(1)}, u32[]{:S(2)}) copy-start(f32[985]{0:T(1024)S(1)} %get-tuple-element.77) | copy-start | bytes 11824
  174.6 74.8 %copy-start.95 = (f32[985]{0:T(1024)}, f32[985]{0:T(1024)S(1)}, u32[]{:S(2)}) copy-start(f32[985]{0:T(1024)S(1)} %get-tuple-element.78) | copy-start | bytes 11824
  175.5 69.1 %copy-start.97 = (s32[985,1]{0,1:T(1,128)}, s32[985,1]{0,1:T(1,128)S(1)}, u32[]{:S(2)}) copy-start(s32[985,1]{0,1:T(1,128)S(1)} %get-tuple-element.128) | copy-start | bytes 11824
  175.5 73.9 %copy-start.99 = (s32[985,1]{0,1:T(1,128)}, s32[985,1]{0,1:T(1,128)S(1)}, u32[]{:S(2)}) copy-start(s32[985,1]{0,1:T(1,128)S(1)} %get-tuple-element.129) | copy-start | bytes 11824
  308.6 73.0 %copy-start.103 = (s32[985,1]{0,1:T(1,128)}, s32[985,1]{0,1:T(1,128)S(1)}, u32[]{:S(2)}) copy-start(s32[985,1]{0,1:T(1,128)S(1)} %get-tuple-element.123) | copy-start | bytes 11824
  308.6 77.8 %copy-start.101 = (s32[985,1]{0,1:T(1,128)}, s32[985,1]{0,1:T(1,128)S(1)}, u32[]{:S(2)}) copy-start(s32[985,1]{0,1:T(1,128)S(1)} %get-tuple-element.122) | copy-start | bytes 11824
  401.3 66.6 %copy-start.105 = (s32[985,1]{0,1:T(1,128)S(1)}, s32[985,1]{0,1:T(1,128)}, u32[]{:S(2)}) copy-start(s32[985,1]{0,1:T(1,128)} %copy-done.103) | copy-start | bytes 11824
  674.4 24.6 %copy-start.76 = (f32[985]{0:T(1024)S(1)}, f32[985]{0:T(1024)}, u32[]{:S(2)}) copy-start(f32[985]{0:T(1024)} %copy-done.75) | copy-start | bytes 11824
  (97 other events, 291.7 us)
Sparse Core Ops, SparseCore 0:
  25.0 31.9 all-gather.12
  58.9 28.3 all-gather.18
  88.8 45.0 all-gather.14
  135.4 44.4 all-gather.16
  181.3 44.4 all-gather.20
  227.2 44.4 all-gather.22

commit v3 on v2

--- a/solution.py
+++ b/solution.py
@@ -9,12 +9,6 @@
 
 HEAD_DIM = 64
 SEQ = 197
-
-
-def norm_rows(rows_in, gain_row):
-    centred = rows_in - jnp.mean(rows_in, axis=-1, keepdims=True)
-    spread = jnp.mean(centred * centred, axis=-1, keepdims=True)
-    return centred * lax.rsqrt(spread + 1e-06) * gain_row
 
 
 def gelu_exact(rows_in):
@@ -269,8 +263,180 @@
     )(rows, arrived, win, wout)
 
 
-def own_part(rows, width, axis=1):
-    return lax.dynamic_slice_in_dim(rows, lax.axis_index("tensor") * width, width, axis=axis)
+def norm_parts(rows_in):
+    centred = rows_in - jnp.mean(rows_in, axis=-1, keepdims=True)
+    inverse = lax.rsqrt(jnp.mean(centred * centred, axis=-1, keepdims=True) + 1e-06)
+    return centred * inverse, inverse
+
+
+def norm_back(unit, inverse, gain_row, grad_rows):
+    scaled = grad_rows * gain_row
+    inner = scaled - jnp.mean(scaled, axis=-1, keepdims=True)
+    return inverse * (inner - unit * jnp.mean(scaled * unit, axis=-1, keepdims=True))
+
+
+def two_heads(rows):
+    low_half = lax.broadcasted_iota(jnp.int32, rows.shape, 1) < HEAD_DIM
+    none = jnp.zeros_like(rows)
+    return jnp.concatenate([jnp.where(low_half, rows, none), jnp.where(low_half, none, rows)], 0)
+
+
+def join_heads(stacked):
+    rows = stacked.shape[0] // 2
+    low_half = lax.broadcasted_iota(jnp.int32, (rows, stacked.shape[1]), 1) < HEAD_DIM
+    return jnp.where(low_half, stacked[:rows], stacked[rows:])
+
+
+def pair_attention(query_two, key_pair):
+    scores = contract_last(query_two, key_pair) * (HEAD_DIM ** (-0.5))
+    real_key = lax.broadcasted_iota(jnp.int32, scores.shape, 1) < SEQ
+    scores = jnp.where(real_key, scores, -jnp.inf)
+    weights = jnp.exp(scores - jnp.max(scores, axis=-1, keepdims=True))
+    return weights * (1.0 / jnp.sum(weights, axis=-1, keepdims=True))
+
+
+def project_qkv(normed, mats_ref):
+    return [
+        jnp.dot(normed, mats_ref[part], preferred_element_type=jnp.float32).astype(jnp.bfloat16)
+        for part in range(3)
+    ]
+
+
+def attend_kernel(
+    experts, stream_ref, mats_ref, gains_ref, router_ref, middle_ref, normed_ref, probs_ref, mixed_ref
+):
+    rows = stream_ref[0]
+    normed = (norm_parts(rows)[0] * gains_ref[0:1]).astype(jnp.bfloat16)
+    query, keys, values = project_qkv(normed, mats_ref)
+    for pair in range(query.shape[1] // (2 * HEAD_DIM)):
+        cols = slice(pair * 2 * HEAD_DIM, (pair + 1) * 2 * HEAD_DIM)
+        attention = pair_attention(two_heads(query[:, cols]), keys[:, cols]).astype(jnp.bfloat16)
+        mixed = jnp.dot(attention, values[:, cols], preferred_element_type=jnp.float32)
+        mixed_ref[0, :, cols] = join_heads(mixed).astype(jnp.bfloat16)
+    middle = rows + contract_last(mixed_ref[0], mats_ref[3])
+    middle_ref[0] = middle
+    normed_two = (norm_parts(middle)[0] * gains_ref[1:2]).astype(jnp.bfloat16)
+    normed_ref[0] = normed_two
+    logits = jnp.dot(normed_two, router_ref[...], preferred_element_type=jnp.float32)
+    real = lax.broadcasted_iota(jnp.int32, logits.shape, 1) < experts
+    logits = jnp.where(real, logits, -jnp.inf)
+    odds = jnp.exp(logits - jnp.max(logits, axis=-1, keepdims=True))
+    probs_ref[0] = odds * (1.0 / jnp.sum(odds, axis=-1, keepdims=True))
+
+
+def attend_back_kernel(
+    own_ref,
+    upstream_ref,
+    grad_ref,
+    grad_logits_ref,
+    stream_ref,
+    middle_ref,
+    mixed_ref,
+    mats_ref,
+    gains_ref,
+    router_ref,
+    down_ref,
+    mats_grad,
+    router_grad,
+    gains_grad,
+    triple,
+):
+    @pl.when(pl.program_id(0) == 0)
+    def _():
+        mats_grad[...] = jnp.zeros_like(mats_grad)
+        router_grad[...] = jnp.zeros_like(router_grad)
+        gains_grad[...] = jnp.zeros_like(gains_grad)
+
+    head_cols = mats_grad.shape[2]
+    mine = pl.ds(pl.multiple_of(own_ref[0] * head_cols, head_cols), head_cols)
+    gain_one, gain_two = gains_ref[0:1], gains_ref[1:2]
+    unit_two, inverse_two = norm_parts(middle_ref[0])
+    grad_logits = grad_logits_ref[0]
+    router_grad[...] += contract_rows(
+        grad_logits, (unit_two * gain_two).astype(jnp.bfloat16)
+    )
+    grad_normed = grad_ref[0] + contract_last(grad_logits, router_ref[...])
+    gains_grad[1:2] += jnp.sum(grad_normed * unit_two, axis=0, keepdims=True)
+    grad_middle = upstream_ref[0] + norm_back(unit_two, inverse_two, gain_two, grad_normed)
+    grad_branch = grad_middle.astype(jnp.bfloat16)
+    mats_grad[3] += contract_rows(grad_branch, mixed_ref[0, :, mine])
+    grad_mixed = jnp.dot(
+        grad_branch, mats_ref[3], preferred_element_type=jnp.float32
+    ).astype(jnp.bfloat16)
+    unit_one, inverse_one = norm_parts(stream_ref[0])
+    normed = (unit_one * gain_one).astype(jnp.bfloat16)
+    query, keys, values = project_qkv(normed, mats_ref)
+    scale = HEAD_DIM ** (-0.5)
+    for pair in range(query.shape[1] // (2 * HEAD_DIM)):
+        cols = slice(pair * 2 * HEAD_DIM, (pair + 1) * 2 * HEAD_DIM)
+        query_two = two_heads(query[:, cols])
+        attention = pair_attention(query_two, keys[:, cols])
+        grad_two = two_heads(grad_mixed[:, cols])
+        triple[2, :, cols] = contract_rows(attention.astype(jnp.bfloat16), grad_two).astype(
+            jnp.bfloat16
+        )
+        grad_attention = contract_last(grad_two, values[:, cols])
+        grad_scores = (
+            attention
+            * (grad_attention - jnp.sum(attention * grad_attention, axis=-1, keepdims=True))
+        ).astype(jnp.bfloat16)
+        grad_query = jnp.dot(grad_scores, keys[:, cols], preferred_element_type=jnp.float32)
+        triple[0, :, cols] = (join_heads(grad_query) * scale).astype(jnp.bfloat16)
+        triple[1, :, cols] = (contract_rows(grad_scores, query_two) * scale).astype(jnp.bfloat16)
+    grad_one = contract_last(triple[0], mats_ref[0])
+    for part in range(3):
+        if part:
+            grad_one += contract_last(triple[part], mats_ref[part])
+        mats_grad[part] += contract_rows(normed, triple[part, :, mine])
+    gains_grad[0:1] += jnp.sum(grad_one * unit_one, axis=0, keepdims=True)
+    down_ref[0] = grad_middle + norm_back(unit_one, inverse_one, gain_one, grad_one)
+
+
+def image_spec(array):
+    return pl.BlockSpec((1,) + array.shape[1:], lambda image: (image, 0, 0))
+
+
+def fixed_spec(array):
+    return pl.BlockSpec(array.shape, lambda image: (0,) * len(array.shape))
+
+
+def attend(stream, mats, gains, router, experts):
+    images, rows, width = stream.shape
+    outs = (
+        jax.ShapeDtypeStruct(stream.shape, jnp.float32),
+        jax.ShapeDtypeStruct(stream.shape, jnp.bfloat16),
+        jax.ShapeDtypeStruct((images, rows, router.shape[1]), jnp.float32),
+        jax.ShapeDtypeStruct((images, rows, mats.shape[2]), jnp.bfloat16),
+    )
+    return pl.pallas_call(
+        functools.partial(attend_kernel, experts),
+        grid=(images,),
+        out_shape=outs,
+        in_specs=[image_spec(stream), fixed_spec(mats), fixed_spec(gains), fixed_spec(router)],
+        out_specs=tuple(image_spec(one) for one in outs),
+    )(stream, mats, gains, router)
+
+
+def attend_back(upstream, grad_normed, grad_logits, stream, middle, mixed, mats, gains, router, head_cols):
+    images, rows, width = stream.shape
+    own = lax.axis_index("tensor").astype(jnp.int32).reshape(1)
+    sums = (
+        jax.ShapeDtypeStruct((4, width, head_cols), jnp.float32),
+        jax.ShapeDtypeStruct((router.shape[1], width), jnp.float32),
+        jax.ShapeDtypeStruct(gains.shape, jnp.float32),
+    )
+    per_image = [upstream, grad_normed, grad_logits, stream, middle, mixed]
+    fixed = [mats, gains, router]
+    return pl.pallas_call(
+        attend_back_kernel,
+        grid=(images,),
+        out_shape=(jax.ShapeDtypeStruct(stream.shape, jnp.float32),) + sums,
+        in_specs=[pl.BlockSpec(memory_space=pltpu.SMEM)]
+        + [image_spec(one) for one in per_image]
+        + [fixed_spec(one) for one in fixed],
+        out_specs=(image_spec(stream),) + tuple(fixed_spec(one) for one in sums),
+        scratch_shapes=[pltpu.VMEM((3, rows, mats.shape[2]), jnp.bfloat16)],
+    )(own, *per_image, *fixed)
 
 
 def slot_plan(chosen, rank_rows, experts, capacity, spacing):
@@ -307,91 +473,68 @@
     model_width = inputs.shape[1]
     images = tokens // SEQ
     head_cols = attend_in.shape[3]
-    hidden_cols = expert_in.shape[3]
-    local_heads = head_cols * lax.axis_size("tensor") // HEAD_DIM
     layers = attend_in.shape[0]
     capacity = max(2, (10 * tokens + 4 * experts - 1) // (4 * experts))
     spacing = -(-capacity // 16) * 16
     slots_all = experts * spacing
     peers_tensor = lax.axis_size("tensor")
-    score_scale = HEAD_DIM ** (-0.5)
     row_share = attend_in.shape[2]
     gain_share = norm_gains.shape[2]
-    in_full, out_full, router_full, gains_full, win_full, wout_full = [], [], [], [], [], []
-    for layer_index in range(layers):
-        out_share = attend_out[layer_index].T[None]
-        packed = [
-            jnp.concatenate([attend_in[layer_index], out_share], axis=0).reshape(-1),
-            router[layer_index].reshape(-1),
-            norm_gains[layer_index].reshape(-1),
+    image_rows = -(-SEQ // 16) * 16
+    tokens_all = images * image_rows
+
+    def spread(rows, fill):
+        shaped = rows.reshape((images, SEQ) + rows.shape[1:])
+        edges = ((0, 0), (0, image_rows - SEQ)) + ((0, 0),) * (rows.ndim - 1)
+        return jnp.pad(shaped, edges, constant_values=fill)
+
+    def gather_tensor(rows, axis):
+        return lax.all_gather(rows.astype(jnp.bfloat16), "tensor", axis=axis, tiled=True)
+
+    smalls = jnp.concatenate([router.reshape(-1), norm_gains.reshape(-1)])
+    block = row_share * head_cols
+    smalls = jnp.pad(smalls, (0, -smalls.shape[0] % block)).reshape(-1, row_share, head_cols)
+    packed = jnp.concatenate(
+        [
+            jnp.concatenate([attend_in, attend_out.transpose(0, 2, 1)[:, None]], axis=1).reshape(
+                -1, row_share, head_cols
+            ),
+            smalls,
         ]
-        sizes = [piece.shape[0] for piece in packed]
-        flat = jnp.concatenate(packed).astype(jnp.bfloat16)
-        flat = jnp.pad(flat, (0, -flat.shape[0] % 2048)).reshape(-1, 128)
-        across = lax.all_gather(flat, "tensor", axis=0)
-        whole = lax.all_gather(across, "expert", axis=0).reshape(experts, peers_tensor, -1)
-        mats = whole[:, :, : sizes[0]].reshape(experts, peers_tensor, 4, row_share, head_cols)
-        mats = mats.transpose(2, 0, 3, 1, 4).reshape(4, model_width, head_cols * peers_tensor)
-        in_full.append(mats[:3])
-        out_full.append(mats[3])
-        smalls = whole[:, 0, sizes[0] :]
-        router_full.append(smalls[:, : sizes[1]].T)
-        gains_full.append(
-            smalls[:, sizes[1] : sizes[1] + sizes[2]]
-            .reshape(experts, 2, gain_share)
-            .transpose(1, 0, 2)
-            .reshape(2, model_width)
-        )
-        win_full.append(
-            lax.all_gather(
-                expert_in[layer_index, 0].astype(jnp.bfloat16), "tensor", axis=1, tiled=True
-            )
-        )
-        wout_full.append(
-            lax.all_gather(
-                expert_out[layer_index, 0].astype(jnp.bfloat16), "tensor", axis=0, tiled=True
-            )
-        )
+    )
+    whole = lax.all_gather(gather_tensor(packed, 2), "expert", axis=1, tiled=True)
+    small_rows = whole[4 * layers :, :, :head_cols].reshape(-1, experts, block)
+    small_rows = small_rows.transpose(1, 0, 2).reshape(experts, -1)
+    router_all = small_rows[:, : layers * model_width].reshape(experts, layers, model_width)
+    gains_all = small_rows[:, layers * model_width :][:, : layers * 2 * gain_share]
+    gains_all = gains_all.reshape(experts, layers, 2, gain_share).transpose(1, 2, 0, 3)
+    gains_all = gains_all.reshape(layers, 2, model_width).astype(jnp.float32)
+    router_all = jnp.pad(router_all.transpose(1, 2, 0), ((0, 0), (0, 0), (0, -experts % 128)))
+    win_full = [gather_tensor(expert_in[layer_index, 0], 1) for layer_index in range(layers)]
+    wout_full = [gather_tensor(expert_out[layer_index, 0], 0) for layer_index in range(layers)]
     slot_ids = lax.broadcasted_iota(jnp.int32, (1, slots_all), 1)
-    stream = inputs
+    stream = spread(inputs, 0)
     stash_list = []
     for layer_index in range(layers):
-        gains_now = gains_full[layer_index].astype(jnp.float32)
-        normed = norm_rows(stream, gains_now[0]).astype(jnp.bfloat16)
-        project = in_full[layer_index]
-        triple = jnp.einsum(
-            "td,jdh->jth", normed, project, preferred_element_type=jnp.float32
-        ).astype(jnp.bfloat16)
-        shaped = triple.reshape(3, images, SEQ, local_heads, HEAD_DIM)
-        scores = (
-            jnp.einsum("iqhd,ikhd->ihqk", shaped[0], shaped[1], preferred_element_type=jnp.float32)
-            * score_scale
-        )
-        log_total = jax.nn.logsumexp(scores, axis=-1, keepdims=True)
-        attention = jnp.exp(scores - log_total).astype(jnp.bfloat16)
-        mixed_heads = (
-            jnp.einsum("ihqk,ikhd->iqhd", attention, shaped[2], preferred_element_type=jnp.float32)
-            .astype(jnp.bfloat16)
-            .reshape(tokens, -1)
-        )
-        middle = stream + contract_last(mixed_heads, out_full[layer_index])
-        normed_two = norm_rows(middle, gains_now[1]).astype(jnp.bfloat16)
-        logits = jnp.dot(normed_two, router_full[layer_index], preferred_element_type=jnp.float32)
-        probs_all = jax.nn.softmax(logits, axis=-1)
-        chosen = routes[layer_index]
-        target, first_f, second_f = slot_plan(
-            chosen, priority[layer_index], experts, capacity, spacing
-        )
+        mats = whole[4 * layer_index : 4 * layer_index + 4]
+        gains_now = gains_all[layer_index]
+        router_now = router_all[layer_index]
+        middle, normed_two, probs_all, mixed_heads = attend(
+            stream, mats, gains_now, router_now, experts
+        )
+        probs_all = probs_all.reshape(tokens_all, -1)[:, :experts]
+        chosen = spread(routes[layer_index], -1).reshape(tokens_all, 2)
+        ranks = spread(priority[layer_index], tokens).reshape(tokens_all)
+        target, first_f, second_f = slot_plan(chosen, ranks, experts, capacity, spacing)
         gate_values = jnp.stack(
             [jnp.sum(probs_all * first_f, axis=1), jnp.sum(probs_all * second_f, axis=1)], axis=1
         )
         pick_first = (target[:, 0:1] == slot_ids).astype(jnp.bfloat16)
         pick_second = (target[:, 1:2] == slot_ids).astype(jnp.bfloat16)
         pick_both = pick_first + pick_second
-
-        dispatched = contract_rows(pick_both, normed_two).astype(jnp.bfloat16)
+        dispatched = contract_rows(pick_both, normed_two.reshape(tokens_all, model_width))
         arrived, returned = experts_forward(
-            dispatched.reshape(experts, spacing, model_width),
+            dispatched.astype(jnp.bfloat16).reshape(experts, spacing, model_width),
             win_full[layer_index],
             wout_full[layer_index],
             peers_tensor,
@@ -399,20 +542,21 @@
         returned = returned.reshape(slots_all, model_width)
         rows_first = jnp.dot(pick_first, returned, preferred_element_type=jnp.float32)
         rows_second = jnp.dot(pick_second, returned, preferred_element_type=jnp.float32)
-        output = middle + gate_values[:, 0:1] * rows_first + gate_values[:, 1:2] * rows_second
+        output = (
+            middle.reshape(tokens_all, model_width)
+            + gate_values[:, 0:1] * rows_first
+            + gate_values[:, 1:2] * rows_second
+        )
         stash_list.append(
             (
                 stream,
+                mats,
                 gains_now,
-                normed,
-                shaped,
-                log_total,
+                router_now,
                 mixed_heads,
                 middle,
-                normed_two,
                 probs_all,
                 gate_values,
-                target,
                 first_f,
                 second_f,
                 pick_first,
@@ -423,23 +567,20 @@
                 rows_second,
             )
         )
-        stream = output
-    upstream = cotangent
+        stream = output.reshape(images, image_rows, model_width)
+    upstream = spread(cotangent, 0).reshape(tokens_all, model_width)
     grads_in, grads_out, grads_router, grads_gain, grads_win, grads_wout = ([], [], [], [], [], [])
     grads_shared = []
     for layer_index in reversed(range(layers)):
         (
             stream_in,
+            mats,
             gains_now,
-            normed,
-            shaped,
-            log_total,
+            router_now,
             mixed_heads,
             middle,
-            normed_two,
             probs_all,
             gate_values,
-            target,
             first_f,
             second_f,
             pick_first,
@@ -471,60 +612,23 @@
         grad_logits = (
             probs_all * (grad_probs - jnp.sum(probs_all * grad_probs, axis=1, keepdims=True))
         ).astype(jnp.bfloat16)
-        router_grad = contract_rows(grad_logits, normed_two)
-        grad_normed = grad_normed + contract_last(grad_logits, router_full[layer_index])
-        norm_back = jax.vjp(norm_rows, middle, gains_now[1])[1](grad_normed)
-        grad_middle = upstream + norm_back[0]
-        grad_branch = grad_middle.astype(jnp.bfloat16)
-        out_grad = contract_rows(grad_branch, own_part(mixed_heads, head_cols))
-        grad_mixed = (
-            jnp.dot(grad_branch, out_full[layer_index], preferred_element_type=jnp.float32)
-            .astype(jnp.bfloat16)
-            .reshape(images, SEQ, local_heads, HEAD_DIM)
-        )
-        scores = (
-            jnp.einsum("iqhd,ikhd->ihqk", shaped[0], shaped[1], preferred_element_type=jnp.float32)
-            * score_scale
-        )
-        attention_f = jnp.exp(scores - log_total)
-        attention = attention_f.astype(jnp.bfloat16)
-        grad_value = jnp.einsum(
-            "ihqk,iqhd->ikhd", attention, grad_mixed, preferred_element_type=jnp.float32
-        ).astype(jnp.bfloat16)
-        grad_attention = jnp.einsum(
-            "iqhd,ikhd->ihqk", grad_mixed, shaped[2], preferred_element_type=jnp.float32
-        )
-        grad_scores = (
-            attention_f
-            * (grad_attention - jnp.sum(attention_f * grad_attention, axis=-1, keepdims=True))
-        ).astype(jnp.bfloat16)
-        grad_query = (
-            jnp.einsum(
-                "ihqk,ikhd->iqhd", grad_scores, shaped[1], preferred_element_type=jnp.float32
-            )
-            * score_scale
-        ).astype(jnp.bfloat16)
-        grad_key = (
-            jnp.einsum(
-                "ihqk,iqhd->ikhd", grad_scores, shaped[0], preferred_element_type=jnp.float32
-            )
-            * score_scale
-        ).astype(jnp.bfloat16)
-        grad_triple = jnp.stack([grad_query, grad_key, grad_value]).reshape(3, tokens, -1)
-        in_grad = jnp.einsum(
-            "td,jth->jdh",
-            normed,
-            own_part(grad_triple, head_cols, 2),
-            preferred_element_type=jnp.float32,
-        )
-        project = in_full[layer_index]
-        grad_normed_one = jnp.einsum(
-            "jth,jdh->td", grad_triple, project, preferred_element_type=jnp.float32
-        )
-        norm_back_one = jax.vjp(norm_rows, stream_in, gains_now[0])[1](grad_normed_one)
-        mats_grad = jnp.concatenate([in_grad, out_grad[None]], axis=0)
+        grad_logits = jnp.pad(grad_logits, ((0, 0), (0, router_now.shape[1] - experts)))
+        shape = stream_in.shape
+        down, mats_grad, router_grad, gain_grad = attend_back(
+            upstream.reshape(shape),
+            grad_normed.reshape(shape),
+            grad_logits.reshape(images, image_rows, -1),
+            stream_in,
+            middle,
+            mixed_heads,
+            mats,
+            gains_now,
+            router_now,
+            head_cols,
+        )
         mats_grad = mats_grad.reshape(4, experts, row_share, head_cols).transpose(1, 0, 2, 3)
-        gain_grad = jnp.stack([norm_back_one[1], norm_back[1]]).reshape(2, experts, gain_share)
+        router_grad = router_grad[:experts]
+        gain_grad = gain_grad.reshape(2, experts, gain_share)
         smalls = jnp.concatenate(
             [router_grad, gain_grad.transpose(1, 0, 2).reshape(experts, -1)], axis=1
         )
@@ -534,7 +638,7 @@
                 [mats_grad.reshape(experts, -1, 128), smalls.reshape(experts, -1, 128)], axis=1
             ).astype(jnp.bfloat16)
         )
-        upstream = grad_middle + norm_back_one[0]
+        upstream = down.reshape(tokens_all, model_width)
     total_rows = grads_shared[0].shape[1]
     mat_rows = 4 * row_share * head_cols // 128
     shared_all = sum_shares(jnp.concatenate(grads_shared, axis=1))
@@ -551,8 +655,8 @@
     win_grad_all = jnp.stack(grads_win[::-1])[:, None]
     wout_grad_all = jnp.stack(grads_wout[::-1])[:, None]
     return (
-        stream,
-        upstream,
+        stream[:, :SEQ].reshape(tokens, model_width),
+        upstream.reshape(stream.shape)[:, :SEQ].reshape(tokens, model_width),
         jnp.stack(grads_in[::-1]),
         jnp.stack(grads_out[::-1]),
         jnp.stack(grads_router[::-1]),

time: 726 us -> 625 us (0.86)
  local copies, waits for them, and re-layouts: 190 us -> 33 us
  Pallas kernels: 283 us -> 371 us
  matrix products: 136 us -> 80.8 us
  waiting for transfers between devices: 34.7 us -> 85.6 us
  other arithmetic: 34.5 us -> 17.5 us
  blocking collectives: 25.9 us -> 16 us
    pallas_call x0 -> x4, Pallas kernels: none -> 88.4 us  [the longest x2 59.1 us: attend_back(): pl.pallas_call(attend_back_kernel, grid=(images,), out_shape=(jax.ShapeDt...]
    dot_general x26 -> x0, matrix products: 69 us -> none  [the longest x2 12.7 us: local(): jnp.einsum('ihqk,iqhd->ikhd', attention, grad_mixed, preferred_element_ty...]
    all_gather x6 -> x5, waiting for transfers between devices: 33.5 us -> 84.5 us  [the longest x4 59.9 us: gather_tensor(): lax.all_gather(rows.astype(jnp.bfloat16), 'tensor', axis=axis, tiled=True)]
    squeeze x14 -> x3, local copies, waits for them, and re-layouts: 42.6 us -> 2.09 us  [the longest x2 1.34 us: local(): gains_now = gains_all[layer_index]]
    reshape x12, local copies, waits for them, and re-layouts: 41.6 us -> 8.53 us  [the longest x2 4.96 us: spread(): shaped = rows.reshape((images, SEQ) + rows.shape[1:])]
    slice x23 -> x15, local copies, waits for them, and re-layouts: 36.3 us -> 11.2 us  [the longest x1 4.5 us: local(): mats = whole[4 * layer_index:4 * layer_index + 4]]
    convert_element_type x10 -> x1, local copies, waits for them, and re-layouts: 23.4 us -> 0.08 us  [local(): gains_all = gains_all.reshape(layers, 2, model_width).astype(jnp.float32)]
    another operation x14 -> x9, local copies, waits for them, and re-layouts: 20.4 us -> 0.39 us  [the longest x4 0.3 us: spread(): shaped = rows.reshape((images, SEQ) + rows.shape[1:])]
  transfers between devices with their start and end apart: 6 -> 5, of which waited for: 2 -> 3; matrix products, arithmetic and copies ran while one was open for 24% -> 8% of each run, Pallas kernels for 9% -> 15%
where the time goes in v3:
time: 625 us; the launch traced here: 619 us
  Pallas kernels  371 us (59%)
  waiting for transfers between devices  85.6 us (14%)
  matrix products  80.8 us (13%)
  local copies, waits for them, and re-layouts  33 us (5%)
  other arithmetic  17.5 us (3%)
  blocking collectives  16 us (3%)
  between operations  14.6 us (2%)
    pallas_call x2, Pallas kernels, experts_backward(): pl.pallas_call(functools.partial(backward_kernel, peers, parts), out_shap...  133 us
    pallas_call x2, Pallas kernels, experts_forward(): pl.pallas_call(functools.partial(forward_kernel, peers, parts), out_shape...  130 us
    all_gather x4, waiting for transfers between devices, gather_tensor(): lax.all_gather(rows.astype(jnp.bfloat16), 'tensor', axis=axis, tiled=True)  59.9 us
    pallas_call x2, Pallas kernels, attend_back(): pl.pallas_call(attend_back_kernel, grid=(images,), out_shape=(jax.ShapeDt...  59.1 us
    dot_general x6, matrix products, contract_rows(): lax.dot_general(left_side, right_side, (((0,), (0,)), ((), ())), preferre...  41.2 us
    pallas_call x2, Pallas kernels, attend(): pl.pallas_call(functools.partial(attend_kernel, experts), grid=(images,),...  29.3 us
    all_gather x1, waiting for transfers between devices, local(): lax.all_gather(gather_tensor(packed, 2), 'expert', axis=1, tiled=True)  24.6 us
    pallas_call x1, Pallas kernels, sum_shares(): pl.pallas_call(functools.partial(sum_kernel, peers), out_shape=jax.ShapeD...  20.1 us
  transfers between devices with their start and end apart: 5, of which 3 were waited for; matrix products, arithmetic and copies ran while one was open for 8% of the time, Pallas kernels for 15%

profile of v3, /device:TPU:1, one launch (start us, length us, event | category | flops | bytes accessed | tf_op | source)
XLA Modules:
  0.0 619.2 jit_solution(10509665842587772727)
XLA Ops:
  10.7 16.0 %all_gather.18 = bf16[9,64,512]{2,1,0:T(8,128)(2,1)} all-gather(bf16[9,64,128]{2,1,0:T(8,128)(2,1)S(1)} %pad_maximum_fusion.2), channel_id=1, replica_groups=mesh['expert'=8,'tensor'=4] {'tensor'}, dimensions={2}, use_global_device_ids=true | all-gather | bytes 737280 | tf_op jit(solution)/shard_map/all_gather | solution.py:492
  42.9 24.6 %all-gather.10.cloned.1.call-done = bf16[9,512,512]{2,1,0:T(8,128)(2,1)} async-done(((bf16[9,64,512]{2,1,0:T(8,128)(2,1)}), bf16[9,512,512]{2,1,0:T(8,128)(2,1)}) %all-gather.10.cloned.1.call-update) | async-done | bytes 4718608 | tf_op jit(solution)/shard_map/all_gather | solution.py:505
  74.7 14.9 %shard_map.161 = (f32[5,208,512]{2,1,0:T(8,128)}, bf16[5,208,512]{2,1,0:T(8,128)(2,1)}, f32[5,208,128]{2,1,0:T(8,128)}, bf16[5,208,512]{2,1,0:T(8,128)(2,1)}) custom-call(f32[5,208,512]{2,1,0:T(8,128)} %pad.46.stream_ref, bf16[4,512,512]{2,1,0:T(8,128)(2,1)} %get-tuple-element.99.mats_ref, f32[2,512]{1,0:T(2,128)} %squeeze.8.gains_ref, ...), custom_call_target="tpu_custom_call" | custom-call | tf_op jit(solution)/shard_map/pallas_call | solution.py:411
  92.8 7.6 %fusion.61 = bf16[2560,512]{1,0:T(8,128)(2,1)} fusion(bf16[1040,512]{1,0:T(8,128)(2,1)} %bitcast.174, s32[1040]{0:T(1024)S(1)} %get-tuple-element.92, s32[1040]{0:T(1024)S(1)} %get-tuple-element.91), kind=kOutput, calls=%fused_computation.61 | convolution fusion | flops 2748907520 | bytes 3694720 | tf_op jit(solution)/shard_map/dot_general | solution.py:19
  100.3 13.8 %all-gather.12.cloned.1.call-done = bf16[1,1,512,2048]{3,2,1,0:T(8,128)(2,1)} async-done(((bf16[1,1,512,512]{3,2,1,0:T(8,128)(2,1)}), bf16[1,1,512,2048]{3,2,1,0:T(8,128)(2,1)}) %all-gather.12.cloned.1.call-update) | async-done | bytes 2097168 | tf_op jit(solution)/shard_map/all_gather | solution.py:492
  114.2 46.1 %all-gather.14.cloned.1.call-done = bf16[1,1,2048,512]{3,2,1,0:T(8,128)(2,1)} async-done(((bf16[1,1,512,512]{3,2,1,0:T(8,128)(2,1)}), bf16[1,1,2048,512]{3,2,1,0:T(8,128)(2,1)}) %all-gather.14.cloned.1.call-update) | async-done | bytes 2097168 | tf_op jit(solution)/shard_map/all_gather | solution.py:492
  160.2 64.6 %shard_map.162 = (bf16[8,320,512]{2,1,0:T(8,128)(2,1)}, bf16[8,320,512]{2,1,0:T(8,128)(2,1)}) custom-call(bf16[8,320,512]{2,1,0:T(8,128)(2,1)} %bitcast.143, bf16[512,2048]{1,0:T(8,128)(2,1)} %bitcast.132, bf16[2048,512]{1,0:T(8,128)(2,1)} %bitcast.134), custom_call_target="tpu_custom_call" | custom-call | tf_op jit(solution)/shard_map/pallas_call | solution.py:228
  224.9 4.8 fusion.10
  234.6 14.4 %shard_map.163 = (f32[5,208,512]{2,1,0:T(8,128)}, bf16[5,208,512]{2,1,0:T(8,128)(2,1)}, f32[5,208,128]{2,1,0:T(8,128)}, bf16[5,208,512]{2,1,0:T(8,128)(2,1)}) custom-call(f32[5,208,512]{2,1,0:T(8,128)} %bitcast.127, bf16[4,512,512]{2,1,0:T(8,128)(2,1)} %get-tuple-element.98.mats_ref, f32[2,512]{1,0:T(2,128)} %squeeze.20.gains_ref, ...), custom_call_target="tpu_custom_call" | custom-call | tf_op jit(solution)/shard_map/pallas_call | solution.py:411
  249.0 7.6 %fusion.58 = bf16[2560,512]{1,0:T(8,128)(2,1)} fusion(bf16[1040,512]{1,0:T(8,128)(2,1)} %bitcast.175, s32[1040]{0:T(1024)S(1)} %get-tuple-element.88, s32[1040]{0:T(1024)S(1)} %get-tuple-element.87), kind=kOutput, calls=%fused_computation.60 | convolution fusion | flops 2748907520 | bytes 3694720 | tf_op jit(solution)/shard_map/dot_general | solution.py:19
  256.6 65.5 %shard_map.164 = (bf16[8,320,512]{2,1,0:T(8,128)(2,1)}, bf16[8,320,512]{2,1,0:T(8,128)(2,1)}) custom-call(bf16[8,320,512]{2,1,0:T(8,128)(2,1)} %bitcast.144, bf16[512,2048]{1,0:T(8,128)(2,1)} %bitcast.136, bf16[2048,512]{1,0:T(8,128)(2,1)} %bitcast.138), custom_call_target="tpu_custom_call" | custom-call | tf_op jit(solution)/shard_map/pallas_call | solution.py:228
  322.1 6.1 fusion.1
  328.4 6.8 %multiply_reduce_fusion.3 = (f32[1040]{0:T(1024)S(1)}, f32[1040]{0:T(1024)S(1)}, f32[1040,512]{1,0:T(8,128)}) fusion(f32[1040,512]{1,0:T(8,128)S(1)} %bitcast.124, f32[1040,512]{1,0:T(8,128)} %fusion.1, bf16[2560,512]{1,0:T(8,128)(2,1)} %bitcast.170, s32[1040]{0:T(1024)S(1)} %get-tuple-element.87), kind=kOutput, calls=%fused_computation.85 | convolution fusion | flops 2731087872 | bytes 9023680 | tf_op jit(solution)/shard_map/dot_general | solution.py:543
  335.2 6.4 %fusion = f32[2560,512]{1,0:T(8,128)} fusion(s32[1040]{0:T(1024)S(1)} %get-tuple-element.88, f32[1040,512]{1,0:T(8,128)S(1)} %bitcast.125, f32[1040]{0:T(1024)S(1)} %get-tuple-element.83), kind=kOutput, calls=%fused_computation.5 | convolution fusion | flops 2730024960 | bytes 7381120 | tf_op jit(solution)/shard_map/dot_general | solution.py:19
  341.8 7.9 %add_convert_fusion.1 = bf16[2560,512]{1,0:T(8,128)(2,1)} fusion(f32[2560,512]{1,0:T(8,128)} %fusion, s32[1040]{0:T(1024)S(1)} %get-tuple-element.87, f32[1040,512]{1,0:T(8,128)S(1)} %bitcast.126, f32[1040]{0:T(1024)S(1)} %get-tuple-element.84), kind=kOutput, calls=%fused_computation.59 | convolution fusion | flops 2732646400 | bytes 10002560 | tf_op jit(solution)/shard_map/dot_general | solution.py:19
  349.7 66.3 %shard_map.165 = (bf16[8,320,512]{2,1,0:T(8,128)(2,1)}, f32[512,512]{1,0:T(8,128)}, f32[512,512]{1,0:T(8,128)}) custom-call(bf16[8,320,512]{2,1,0:T(8,128)(2,1)} %bitcast.142, bf16[8,320,512]{2,1,0:T(8,128)(2,1)} %get-tuple-element.42.arrived_ref, bf16[512,2048]{1,0:T(8,128)(2,1)} %bitcast.137, bf16[2048,512]{1,0:T(8,128)(2,1)} %bitcast.139), custom_call_target="tpu_custom_call" | custom-call | tf_op jit(solution)/shard_map/pallas_call | solution.py:245
  416.8 6.7 %fusion.31.grad_ref = f32[5,208,512]{2,1,0:T(8,128)} fusion(bf16[2560,512,1]{1,0,2:T(8,128)(2,1)} %bitcast.168, s32[5,208]{1,0:T(8,128)S(1)} %eq.244, s32[5,208]{1,0:T(8,128)S(1)} %eq.240), kind=kOutput, calls=%fused_computation.37 | convolution fusion | flops 2747596800 | bytes 4759680 | tf_op jit(solution)/shard_map/dot_general | solution.py:610
  423.4 29.6 %shard_map.166 = (f32[5,208,512]{2,1,0:T(8,128)}, f32[4,512,128]{2,1,0:T(8,128)}, f32[128,512]{1,0:T(8,128)}, f32[2,512]{1,0:T(2,128)}) custom-call(s32[1]{0:T(128)} %bitcast.26.own_ref, f32[5,208,512]{2,1,0:T(8,128)} %copy-done, f32[5,208,512]{2,1,0:T(8,128)} %fusion.31.grad_ref, bf16[5,208,128]{2,1,0:T(8,128)(2,1)} %bitcast.150, f32[5,208,512]{2,1,0:T(8,128)} %bitcast.128, ...), custom_call_target="tpu_custom_call" | custom-call | tf_op jit(solution)/shard_map/pallas_call | solution.py:430
  453.1 5.7 fusion.6
  458.9 6.0 add_convert_fusion
  466.5 66.5 %shard_map.167 = (bf16[8,320,512]{2,1,0:T(8,128)(2,1)}, f32[512,512]{1,0:T(8,128)}, f32[512,512]{1,0:T(8,128)}) custom-call(bf16[8,320,512]{2,1,0:T(8,128)(2,1)} %bitcast.141, bf16[8,320,512]{2,1,0:T(8,128)(2,1)} %get-tuple-element.46.arrived_ref, bf16[512,2048]{1,0:T(8,128)(2,1)} %bitcast.133, bf16[2048,512]{1,0:T(8,128)(2,1)} %bitcast.135), custom_call_target="tpu_custom_call" | custom-call | tf_op jit(solution)/shard_map/pallas_call | solution.py:245
  533.0 6.7 %fusion.26.grad_ref = f32[5,208,512]{2,1,0:T(8,128)} fusion(bf16[2560,512,1]{1,0,2:T(8,128)(2,1)} %bitcast.171, s32[5,208]{1,0:T(8,128)S(1)} %eq.252, s32[5,208]{1,0:T(8,128)S(1)} %eq.248), kind=kOutput, calls=%fused_computation.34 | convolution fusion | flops 2747596800 | bytes 4759680 | tf_op jit(solution)/shard_map/dot_general | solution.py:610
  539.7 29.4 %shard_map.168 = (f32[5,208,512]{2,1,0:T(8,128)}, f32[4,512,128]{2,1,0:T(8,128)}, f32[128,512]{1,0:T(8,128)}, f32[2,512]{1,0:T(2,128)}) custom-call(s32[1]{0:T(128)} %bitcast.26.own_ref, f32[5,208,512]{2,1,0:T(8,128)} %get-tuple-element.45.upstream_ref, f32[5,208,512]{2,1,0:T(8,128)} %fusion.26.grad_ref, bf16[5,208,128]{2,1,0:T(8,128)(2,1)} %bitcast.149, ...), custom_call_target="tpu_custom_call" | custom-call | tf_op jit(solution)/shard_map/pallas_call | solution.py:430
  574.3 20.1 %shard_map.169 = f32[544,128]{1,0:T(8,128)} custom-call(bf16[8,544,128]{2,1,0:T(8,128)(2,1)} %pad_maximum_fusion.rows_ref), custom_call_target="tpu_custom_call" | custom-call | tf_op jit(solution)/shard_map/pallas_call | solution.py:207
  (156 shorter events, 60.3 us)
Async XLA Ops:
  7.2 19.7 %copy-start.8 = (f32[2,1,512,512]{3,2,1,0:T(8,128)S(1)}, f32[2,1,512,512]{3,2,1,0:T(8,128)}, u32[]{:S(2)}) copy-start(f32[2,1,512,512]{3,2,1,0:T(8,128)} %param.18) | copy-start | bytes 6291460
  7.2 60.3 %all-gather.10.cloned.1.call-start = ((), (), s32[]{:S(2)}) async-start(), calls=%async_computation | async-start | bytes 5308416 | tf_op jit(solution)/shard_map/all_gather | solution.py:505
  26.8 87.4 %all-gather.12.cloned.1.call-start = ((), (), s32[]{:S(2)}) async-start(), calls=%async_computation.1 | async-start | bytes 2621440 | tf_op jit(solution)/shard_map/all_gather | solution.py:492
  27.0 2.0 copy-start.9
  28.1 132.1 %all-gather.14.cloned.1.call-start = ((), (), s32[]{:S(2)}) async-start(), calls=%async_computation.2 | async-start | bytes 2621440 | tf_op jit(solution)/shard_map/all_gather | solution.py:492
  30.2 3.0 copy-start.14
  30.2 3.2 copy-start.13
  30.2 226.4 %all-gather.16.cloned.1.call-start = ((), (), s32[]{:S(2)}) async-start(), calls=%async_computation.3 | async-start | bytes 2621440 | tf_op jit(solution)/shard_map/all_gather | solution.py:492
  30.8 225.8 %all-gather.18.cloned.1.call-start = ((), (), s32[]{:S(2)}) async-start(), calls=%async_computation.4 | async-start | bytes 2621440 | tf_op jit(solution)/shard_map/all_gather | solution.py:492
  40.2 2.3 copy-start.3
  42.7 299.1 %copy-start = (f32[5,208,512]{2,1,0:T(8,128)}, f32[5,208,512]{2,1,0:T(8,128)S(1)}, u32[]{:S(2)}) copy-start(f32[5,208,512]{2,1,0:T(8,128)S(1)} %pad.53.upstream_ref) | copy-start | bytes 6389764
  224.8 4.9 copy-start.7
  224.9 4.9 copy-start.16
  229.7 4.8 copy-start.4
  322.1 6.1 copy-start.12
  453.1 5.8 copy-start.1
  458.8 6.1 copy-start.5
  458.8 6.1 copy-start.6
  539.7 31.1 %copy-start.15 = (f32[2,512]{1,0:T(2,128)S(1)}, f32[2,512]{1,0:T(2,128)}, u32[]{:S(2)}) copy-start(f32[2,512]{1,0:T(2,128)} %get-tuple-element.52) | copy-start | bytes 12292
  569.2 3.9 copy-start.10
  573.2 24.4 %copy-start.2 = (f32[5,208,512]{2,1,0:T(8,128)S(1)}, f32[5,208,512]{2,1,0:T(8,128)}, u32[]{:S(2)}) copy-start(f32[5,208,512]{2,1,0:T(8,128)} %get-tuple-element.38.middle_ref) | copy-start | bytes 6389764
  604.0 4.2 copy-start.11
Sparse Core Ops, SparseCore 0:
  26.9 40.5 all-gather.9
  69.1 45.0 all-gather.11
  115.7 44.4 all-gather.13
  161.7 44.4 all-gather.15
  207.6 44.4 all-gather.17

commit v4 on v3

--- a/solution.py
+++ b/solution.py
@@ -33,37 +33,159 @@
     return rows_in * half, slope
 
 
-def meet_peers(me, peers):
-    barrier = pltpu.get_barrier_semaphore()
-
-    def greet(step, carry):
-        pl.semaphore_signal(
-            barrier,
-            inc=1,
-            device_id={"expert": lax.rem(me + step, peers)},
-            device_id_type=pl.DeviceIdType.MESH,
-        )
+def greet(barrier, axis, index):
+    pl.semaphore_signal(
+        barrier, inc=1, device_id={axis: index}, device_id_type=pl.DeviceIdType.MESH
+    )
+
+
+def greet_axis(barrier, axis, me, peers):
+    def one(step, carry):
+        greet(barrier, axis, lax.rem(me + step, peers))
         return carry
 
-    lax.fori_loop(1, peers, greet, 0)
-    pl.semaphore_wait(barrier, peers - 1)
-
-
-def send_chunk(source, landing, sends, arrivals, step, peer):
+    lax.fori_loop(1, peers, one, 0)
+
+
+def send(source, landing, send_sem, recv_sem, axis, index):
     return pltpu.make_async_remote_copy(
         src_ref=source,
         dst_ref=landing,
-        send_sem=sends.at[step],
-        recv_sem=arrivals.at[step],
-        device_id={"expert": peer},
+        send_sem=send_sem,
+        recv_sem=recv_sem,
+        device_id={axis: index},
         device_id_type=pl.DeviceIdType.MESH,
     )
 
 
-def exchange_chunks(peers, work, out_rows, landed, results, back, sems):
-    out_send, out_recv, back_send, back_recv = sems
+def send_chunk(source, landing, sends, arrivals, step, peer):
+    return send(source, landing, sends.at[step], arrivals.at[step], "expert", peer)
+
+
+def meet_peers(me, peers):
+    barrier = pltpu.get_barrier_semaphore()
+    greet_axis(barrier, "expert", me, peers)
+    pl.semaphore_wait(barrier, peers - 1)
+
+
+def gather_kernel(
+    experts,
+    parts,
+    small_ref,
+    win_ref,
+    wout_ref,
+    whole,
+    win_full,
+    wout_full,
+    side_send,
+    side_recv,
+    chip_send,
+    chip_recv,
+    twin_send,
+    twin_recv,
+    local_sem,
+):
     me = lax.axis_index("expert")
-    meet_peers(me, peers)
+    side = lax.axis_index("tensor")
+    twin = me + 1 - 2 * lax.rem(me, 2)
+    chips = experts // 2
+    cols = small_ref.shape[2]
+    width = win_ref.shape[1]
+    barrier = pltpu.get_barrier_semaphore()
+    greet_axis(barrier, "tensor", side, parts)
+    greet(barrier, "expert", twin)
+    for step in range(1, chips):
+        greet(barrier, "expert", lax.rem(me + 2 * step, experts))
+    pl.semaphore_wait(barrier, parts - 1 + chips)
+
+    def places(index):
+        lanes = pl.ds(pl.multiple_of(index * cols, cols), cols)
+        hidden = pl.ds(pl.multiple_of(index * width, width), width)
+        return (whole.at[:, me, :, lanes], win_full.at[:, hidden], wout_full.at[hidden, :])
+
+    sources = (small_ref, win_ref, wout_ref)
+
+    def side_copy(kind, step, owner, target):
+        return send(
+            sources[kind],
+            places(owner)[kind],
+            side_send.at[kind, step],
+            side_recv.at[kind, step],
+            "tensor",
+            target,
+        )
+
+    for kind in range(3):
+        for step in range(1, parts):
+            side_copy(kind, step, side, lax.rem(side + step, parts)).start()
+    for kind in range(3):
+        pltpu.make_async_copy(sources[kind], places(side)[kind], local_sem.at[kind]).start()
+    pltpu.make_async_copy(sources[0], places(side)[0], local_sem.at[0]).wait()
+    for step in range(1, parts):
+        side_copy(0, step, lax.rem(side + parts - step, parts), side).wait_recv()
+
+    def chip_copy(step, owner, target):
+        return send_chunk(whole.at[:, owner], whole.at[:, owner], chip_send, chip_recv, step, target)
+
+    def twin_copy(step, owner):
+        return send_chunk(whole.at[:, owner], whole.at[:, owner], twin_send, twin_recv, step, twin)
+
+    for step in range(1, chips):
+        chip_copy(step, me, lax.rem(me + 2 * step, experts)).start()
+    twin_copy(0, me).start()
+    for step in range(1, chips):
+        owner = lax.rem(me + experts - 2 * step, experts)
+        chip_copy(step, owner, owner).wait_recv()
+        twin_copy(step, owner).start()
+    for step in range(chips):
+        twin_copy(step, lax.rem(twin + experts - 2 * step, experts)).wait_recv()
+        twin_copy(step, lax.rem(me + experts - 2 * step, experts)).wait_send()
+        if step:
+            chip_copy(step, me, lax.rem(me + 2 * step, experts)).wait_send()
+    for kind in range(3):
+        for step in range(1, parts):
+            one = side_copy(kind, step, lax.rem(side + parts - step, parts), side)
+            one.wait_send()
+            if kind:
+                one.wait_recv()
+    for kind in range(1, 3):
+        pltpu.make_async_copy(sources[kind], places(side)[kind], local_sem.at[kind]).wait()
+
+
+def gather_start(small, win, wout, experts, parts):
+    count, rows, cols = small.shape
+    depth, width = win.shape
+    chips = experts // 2
+    return pl.pallas_call(
+        functools.partial(gather_kernel, experts, parts),
+        out_shape=(
+            jax.ShapeDtypeStruct((count, experts, rows, cols * parts), jnp.bfloat16),
+            jax.ShapeDtypeStruct((depth, width * parts), jnp.bfloat16),
+            jax.ShapeDtypeStruct((width * parts, depth), jnp.bfloat16),
+        ),
+        in_specs=whole_in_vmem(3),
+        out_specs=tuple(whole_in_vmem(3)),
+        scratch_shapes=[pltpu.SemaphoreType.DMA((3, parts))] * 2
+        + [pltpu.SemaphoreType.DMA((chips,))] * 4
+        + [pltpu.SemaphoreType.DMA((3,))],
+        compiler_params=pltpu.CompilerParams(collective_id=3, has_side_effects=True),
+    )(small, win, wout)
+
+
+def exchange_chunks(peers, parts, work, out_rows, landed, results, back, sems, sum_up=None):
+    out_send, out_recv, back_send, back_recv, side_send, side_recv = sems
+    me = lax.axis_index("expert")
+    side = lax.axis_index("tensor")
+    share = back.shape[1] // parts
+    barrier = pltpu.get_barrier_semaphore()
+    greet_axis(barrier, "expert", me, peers)
+    greet_axis(barrier, "tensor", side, parts)
+    pl.semaphore_wait(barrier, peers + parts - 2)
+
+    def share_of(index):
+        return pl.ds(pl.multiple_of(index * share, 16), share)
+
+    mine = share_of(side)
 
     def start_out(step, carry):
         peer = lax.rem(me + step, peers)
@@ -72,6 +194,26 @@
 
     lax.fori_loop(1, peers, start_out, 0)
     landed[me] = out_rows[me]
+
+    def side_copy(shift, step, slab, owner, target):
+        place = back.at[slab, share_of(owner)]
+        return send(
+            place, place, side_send.at[shift, step], side_recv.at[shift, step], "tensor", target
+        )
+
+    def pass_on(step):
+        slab = lax.rem(me + step, peers)
+
+        @pl.when(step > 0)
+        def _():
+            send_chunk(
+                results.at[step], back.at[slab, mine], back_send, back_recv, step, slab
+            ).wait_recv()
+
+        for shift in range(1, parts):
+            side_copy(shift, step, slab, side, lax.rem(side + shift, parts)).start()
+
+    lag = 2
 
     def one_chunk(step, carry):
         peer = lax.rem(me + peers - step, peers)
@@ -82,26 +224,53 @@
                 out_rows.at[peer], landed.at[peer], out_send, out_recv, step, peer
             ).wait_recv()
 
-        work(step, peer)
+        work(step, peer, mine)
 
         @pl.when(step > 0)
         def _():
-            send_chunk(results.at[step], back.at[me], back_send, back_recv, step, peer).start()
-
+            send_chunk(
+                results.at[step], back.at[me, mine], back_send, back_recv, step, peer
+            ).start()
+
+        @pl.when(step == 0)
+        def _():
+            back[me, mine] = results[0]
+
+        @pl.when(step >= lag)
+        def _():
+            pass_on(step - lag)
+
+        if sum_up is not None:
+            sum_up(peer)
         return carry
 
     lax.fori_loop(0, peers, one_chunk, 0)
-    back[me] = results[0]
+
+    def pass_last(step, carry):
+        pass_on(step)
+        return carry
+
+    lax.fori_loop(peers - lag, peers, pass_last, 0)
 
     def finish(step, carry):
         ahead = lax.rem(me + step, peers)
-        send_chunk(out_rows.at[ahead], landed.at[me], out_send, out_recv, step, ahead).wait_send()
-        last = send_chunk(results.at[step], back.at[ahead], back_send, back_recv, step, ahead)
-        last.wait_send()
-        last.wait_recv()
+
+        @pl.when(step > 0)
+        def _():
+            send_chunk(
+                out_rows.at[ahead], landed.at[me], out_send, out_recv, step, ahead
+            ).wait_send()
+            send_chunk(
+                results.at[step], back.at[me, mine], back_send, back_recv, step, ahead
+            ).wait_send()
+
+        for shift in range(1, parts):
+            behind = lax.rem(side + parts - shift, parts)
+            side_copy(shift, step, ahead, side, lax.rem(side + shift, parts)).wait_send()
+            side_copy(shift, step, ahead, behind, behind).wait_recv()
         return carry
 
-    lax.fori_loop(1, peers, finish, 0)
+    lax.fori_loop(0, peers, finish, 0)
 
 
 def forward_kernel(
@@ -109,8 +278,8 @@
 ):
     width = win_ref.shape[1] // parts
 
-    def work(step, peer):
-        chunk = landed[peer]
+    def work(step, peer, mine):
+        chunk = landed[peer, mine]
         for part in range(parts):
             cols = slice(part * width, (part + 1) * width)
             before = jnp.dot(chunk, win_ref[:, cols], preferred_element_type=jnp.float32)
@@ -123,7 +292,7 @@
             else:
                 results[step] = (total[...] + term).astype(jnp.bfloat16)
 
-    exchange_chunks(peers, work, rows_ref, landed, results, back, sems)
+    exchange_chunks(peers, parts, work, rows_ref, landed, results, back, sems)
 
 
 def backward_kernel(
@@ -139,26 +308,25 @@
     landed,
     results,
     total,
-    hidden_all,
-    before_all,
     *sems,
 ):
     width = win_ref.shape[1] // parts
-    own = lax.axis_index("tensor") * width
+    own = pl.ds(pl.multiple_of(lax.axis_index("tensor") * width, width), width)
     win_grad[...] = jnp.zeros_like(win_grad)
     wout_grad[...] = jnp.zeros_like(wout_grad)
 
-    def work(step, peer):
-        chunk = arrived_ref[peer]
-        grad_chunk = landed[peer]
+    def hidden_pair(chunk, grad_chunk, cols):
+        before = jnp.dot(chunk, win_ref[:, cols], preferred_element_type=jnp.float32)
+        value, slope = gelu_parts(before)
+        grad_before = contract_last(grad_chunk, wout_ref[cols, :]) * slope
+        return value.astype(jnp.bfloat16), grad_before.astype(jnp.bfloat16)
+
+    def work(step, peer, mine):
+        chunk = arrived_ref[peer, mine]
+        grad_chunk = landed[peer, mine]
         for part in range(parts):
             cols = slice(part * width, (part + 1) * width)
-            before = jnp.dot(chunk, win_ref[:, cols], preferred_element_type=jnp.float32)
-            value, slope = gelu_parts(before)
-            grad_hidden = contract_last(grad_chunk, wout_ref[cols, :])
-            grad_before = (grad_hidden * slope).astype(jnp.bfloat16)
-            hidden_all[:, cols] = value.astype(jnp.bfloat16)
-            before_all[:, cols] = grad_before
+            grad_before = hidden_pair(chunk, grad_chunk, cols)[1]
             term = contract_last(grad_before, win_ref[:, cols])
             if part == 0:
                 total[...] = term
@@ -166,60 +334,23 @@
                 total[...] += term
             else:
                 results[step] = (total[...] + term).astype(jnp.bfloat16)
-        mine = pl.ds(pl.multiple_of(own, width), width)
-        wout_grad[...] += contract_rows(hidden_all[:, mine], grad_chunk)
-        win_grad[...] += contract_rows(chunk, before_all[:, mine])
-
-    exchange_chunks(peers, work, rows_ref, landed, results, back, sems)
-
-
-def sum_kernel(peers, rows_ref, sum_ref, landed, sends, arrivals):
-    me = lax.axis_index("expert")
-    meet_peers(me, peers)
-
-    def start_out(step, carry):
-        peer = lax.rem(me + step, peers)
-        send_chunk(rows_ref.at[peer], landed.at[me], sends, arrivals, step, peer).start()
-        return carry
-
-    lax.fori_loop(1, peers, start_out, 0)
-    landed[me] = rows_ref[me]
-
-    def finish(step, carry):
-        peer = lax.rem(me + peers - step, peers)
-        one = send_chunk(rows_ref.at[peer], landed.at[peer], sends, arrivals, step, peer)
-        one.wait_send()
-        one.wait_recv()
-        return carry
-
-    lax.fori_loop(1, peers, finish, 0)
-    sum_ref[...] = landed[0].astype(jnp.float32)
-
-    def add_one(source, carry):
-        sum_ref[...] += landed[source].astype(jnp.float32)
-        return carry
-
-    lax.fori_loop(1, peers, add_one, 0)
-
-
-def sum_shares(rows):
-    peers = rows.shape[0]
-    return pl.pallas_call(
-        functools.partial(sum_kernel, peers),
-        out_shape=jax.ShapeDtypeStruct(rows.shape[1:], jnp.float32),
-        in_specs=whole_in_vmem(1),
-        out_specs=whole_in_vmem(1)[0],
-        scratch_shapes=[pltpu.VMEM(rows.shape, rows.dtype)] + exchange_sems(peers)[:2],
-        compiler_params=pltpu.CompilerParams(collective_id=2, has_side_effects=True),
-    )(rows)
+
+    def sum_up(peer):
+        chunk = arrived_ref[peer]
+        grad_chunk = landed[peer]
+        hidden, grad_before = hidden_pair(chunk, grad_chunk, own)
+        wout_grad[...] += contract_rows(hidden, grad_chunk)
+        win_grad[...] += contract_rows(chunk, grad_before)
+
+    exchange_chunks(peers, parts, work, rows_ref, landed, results, back, sems, sum_up)
 
 
 def whole_in_vmem(count):
     return [pl.BlockSpec(memory_space=pltpu.VMEM)] * count
 
 
-def exchange_sems(peers):
-    return [pltpu.SemaphoreType.DMA((peers,)) for _ in range(4)]
+def exchange_sems(peers, parts):
+    return [pltpu.SemaphoreType.DMA((peers,))] * 4 + [pltpu.SemaphoreType.DMA((parts, peers))] * 2
 
 
 def experts_forward(rows, win, wout, parts):
@@ -231,10 +362,10 @@
         in_specs=whole_in_vmem(3),
         out_specs=tuple(whole_in_vmem(2)),
         scratch_shapes=[
-            pltpu.VMEM(rows.shape, jnp.bfloat16),
-            pltpu.VMEM((capacity, width), jnp.float32),
+            pltpu.VMEM((peers, capacity // parts, width), jnp.bfloat16),
+            pltpu.VMEM((capacity // parts, width), jnp.float32),
         ]
-        + exchange_sems(peers),
+        + exchange_sems(peers, parts),
         compiler_params=pltpu.CompilerParams(collective_id=0, has_side_effects=True),
     )(rows, win, wout)
 
@@ -253,14 +384,53 @@
         out_specs=tuple(whole_in_vmem(3)),
         scratch_shapes=[
             pltpu.VMEM(rows.shape, jnp.bfloat16),
-            pltpu.VMEM(rows.shape, jnp.bfloat16),
-            pltpu.VMEM((capacity, width), jnp.float32),
-            pltpu.VMEM((capacity, inner), jnp.bfloat16),
-            pltpu.VMEM((capacity, inner), jnp.bfloat16),
+            pltpu.VMEM((peers, capacity // parts, width), jnp.bfloat16),
+            pltpu.VMEM((capacity // parts, width), jnp.float32),
         ]
-        + exchange_sems(peers),
+        + exchange_sems(peers, parts),
         compiler_params=pltpu.CompilerParams(collective_id=1, has_side_effects=True),
     )(rows, arrived, win, wout)
+
+
+def sum_kernel(peers, rows_ref, sum_ref, landed, sends, arrivals):
+    me = lax.axis_index("expert")
+    meet_peers(me, peers)
+
+    def start_out(step, carry):
+        peer = lax.rem(me + step, peers)
+        send_chunk(rows_ref.at[peer], landed.at[me], sends, arrivals, step, peer).start()
+        return carry
+
+    lax.fori_loop(1, peers, start_out, 0)
+    landed[me] = rows_ref[me]
+
+    def finish(step, carry):
+        peer = lax.rem(me + peers - step, peers)
+        one = send_chunk(rows_ref.at[peer], landed.at[peer], sends, arrivals, step, peer)
+        one.wait_send()
+        one.wait_recv()
+        return carry
+
+    lax.fori_loop(1, peers, finish, 0)
+    sum_ref[...] = landed[0].astype(jnp.float32)
+
+    def add_one(source, carry):
+        sum_ref[...] += landed[source].astype(jnp.float32)
+        return carry
+
+    lax.fori_loop(1, peers, add_one, 0)
+
+
+def sum_shares(rows):
+    peers = rows.shape[0]
+    return pl.pallas_call(
+        functools.partial(sum_kernel, peers),
+        out_shape=jax.ShapeDtypeStruct(rows.shape[1:], jnp.float32),
+        in_specs=whole_in_vmem(1),
+        out_specs=whole_in_vmem(1)[0],
+        scratch_shapes=[pltpu.VMEM(rows.shape, rows.dtype)] + [pltpu.SemaphoreType.DMA((peers,))] * 2,
+        compiler_params=pltpu.CompilerParams(collective_id=2, has_side_effects=True),
+    )(rows)
 
 
 def norm_parts(rows_in):
@@ -475,9 +645,9 @@
     head_cols = attend_in.shape[3]
     layers = attend_in.shape[0]
     capacity = max(2, (10 * tokens + 4 * experts - 1) // (4 * experts))
-    spacing = -(-capacity // 16) * 16
+    peers_tensor = lax.axis_size("tensor")
+    spacing = -(-capacity // (16 * peers_tensor)) * 16 * peers_tensor
     slots_all = experts * spacing
-    peers_tensor = lax.axis_size("tensor")
     row_share = attend_in.shape[2]
     gain_share = norm_gains.shape[2]
     image_rows = -(-SEQ // 16) * 16
@@ -502,7 +672,17 @@
             smalls,
         ]
     )
-    whole = lax.all_gather(gather_tensor(packed, 2), "expert", axis=1, tiled=True)
+    whole, win_first, wout_first = gather_start(
+        packed.astype(jnp.bfloat16),
+        expert_in[0, 0].astype(jnp.bfloat16),
+        expert_out[0, 0].astype(jnp.bfloat16),
+        experts,
+        peers_tensor,
+    )
+    whole = whole.reshape(whole.shape[0], model_width, model_width)
+    later_in, later_out, whole = lax.optimization_barrier(
+        (expert_in[1:, 0], expert_out[1:, 0], whole)
+    )
     small_rows = whole[4 * layers :, :, :head_cols].reshape(-1, experts, block)
     small_rows = small_rows.transpose(1, 0, 2).reshape(experts, -1)
     router_all = small_rows[:, : layers * model_width].reshape(experts, layers, model_width)
@@ -510,8 +690,10 @@
     gains_all = gains_all.reshape(experts, layers, 2, gain_share).transpose(1, 2, 0, 3)
     gains_all = gains_all.reshape(layers, 2, model_width).astype(jnp.float32)
     router_all = jnp.pad(router_all.transpose(1, 2, 0), ((0, 0), (0, 0), (0, -experts % 128)))
-    win_full = [gather_tensor(expert_in[layer_index, 0], 1) for layer_index in range(layers)]
-    wout_full = [gather_tensor(expert_out[layer_index, 0], 0) for layer_index in range(layers)]
+    win_full, wout_full = [win_first], [wout_first]
+    for layer_index in range(layers - 1):
+        win_full.append(gather_tensor(later_in[layer_index], 1))
+        wout_full.append(gather_tensor(later_out[layer_index], 0))
     slot_ids = lax.broadcasted_iota(jnp.int32, (1, slots_all), 1)
     stream = spread(inputs, 0)
     stash_list = []

time: 625 us -> 738 us (1.18)
  Pallas kernels: 371 us -> 592 us
  waiting for transfers between devices: 85.6 us -> 0.71 us
  blocking collectives: 16 us -> 0 us
    pallas_call x0 -> x1, Pallas kernels: none -> 102 us  [gather_start(): pl.pallas_call(functools.partial(gather_kernel, experts, parts), out_shap...]
    pallas_call x2, Pallas kernels: 130 us -> 206 us  [experts_forward(): pl.pallas_call(functools.partial(forward_kernel, peers, parts), out_shape...]
    all_gather x4 -> x2, waiting for transfers between devices: 59.9 us -> 0.01 us  [gather_tensor(): lax.all_gather(rows.astype(jnp.bfloat16), 'tensor', axis=axis, tiled=True)]
    pallas_call x2, Pallas kernels: 133 us -> 178 us  [experts_backward(): pl.pallas_call(functools.partial(backward_kernel, peers, parts), out_shap...]
    all_gather x1 -> x0, waiting for transfers between devices: 24.6 us -> none  [local(): lax.all_gather(gather_tensor(packed, 2), 'expert', axis=1, tiled=True)]
    all_gather x1 -> x0, blocking collectives: 16 us -> none  [gather_tensor(): lax.all_gather(rows.astype(jnp.bfloat16), 'tensor', axis=axis, tiled=True)]
  transfers between devices with their start and end apart: 5 -> 2, of which waited for: 3 -> 0; matrix products, arithmetic and copies ran while one was open for 8% -> 6% of each run, Pallas kernels for 15% -> 20%
where the time goes in v4:
time: 738 us; the launch traced here: 735 us
  Pallas kernels  592 us (80%)
  matrix products  75.7 us (10%)
  local copies, waits for them, and re-layouts  34 us (5%)
  other arithmetic  17.7 us (2%)
  between operations  14.8 us (2%)
    pallas_call x2, Pallas kernels, experts_forward(): pl.pallas_call(functools.partial(forward_kernel, peers, parts), out_shape...  206 us
    pallas_call x2, Pallas kernels, experts_backward(): pl.pallas_call(functools.partial(backward_kernel, peers, parts), out_shap...  178 us
    pallas_call x1, Pallas kernels, gather_start(): pl.pallas_call(functools.partial(gather_kernel, experts, parts), out_shap...  102 us
    pallas_call x2, Pallas kernels, attend_back(): pl.pallas_call(attend_back_kernel, grid=(images,), out_shape=(jax.ShapeDt...  59.1 us
    dot_general x6, matrix products, contract_rows(): lax.dot_general(left_side, right_side, (((0,), (0,)), ((), ())), preferre...  39.7 us
    pallas_call x2, Pallas kernels, attend(): pl.pallas_call(functools.partial(attend_kernel, experts), grid=(images,),...  29.1 us
    pallas_call x1, Pallas kernels, sum_shares(): pl.pallas_call(functools.partial(sum_kernel, peers), out_shape=jax.ShapeD...  17.7 us
  transfers between devices with their start and end apart: 2, of which 0 were waited for; matrix products, arithmetic and copies ran while one was open for 6% of the time, Pallas kernels for 20%

profile of v4, /device:TPU:1, one launch (start us, length us, event | category | flops | bytes accessed | tf_op | source)
XLA Modules:
  0.0 734.9 jit_solution(9089881732575825276)
XLA Ops:
  10.5 3.6 fusion.108
  14.8 101.9 %shard_map.161 = (bf16[9,8,64,512]{3,2,1,0:T(8,128)(2,1)}, bf16[512,2048]{1,0:T(8,128)(2,1)}, bf16[2048,512]{1,0:T(8,128)(2,1)}) custom-call(bf16[9,64,128]{2,1,0:T(8,128)(2,1)} %pad_maximum_fusion.2.small_ref, bf16[512,512]{1,0:T(8,128)(2,1)} %get-tuple-element.114.win_ref, bf16[512,512]{1,0:T(8,128)(2,1)} %get-tuple-element.132.wout_ref), custom_call_target="tpu_custom_call" | custom-call | tf_op jit(solution)/shard_map/pallas_call | solution.py:159
  117.4 4.5 fusion.136
  128.5 14.7 %shard_map.162 = (f32[5,208,512]{2,1,0:T(8,128)}, bf16[5,208,512]{2,1,0:T(8,128)(2,1)}, f32[5,208,128]{2,1,0:T(8,128)}, bf16[5,208,512]{2,1,0:T(8,128)(2,1)}) custom-call(f32[5,208,512]{2,1,0:T(8,128)} %pad.46.stream_ref, bf16[4,512,512]{2,1,0:T(8,128)(2,1)} %get-tuple-element.111.mats_ref, f32[2,512]{1,0:T(2,128)} %squeeze.26.gains_ref, ...), custom_call_target="tpu_custom_call" | custom-call | tf_op jit(solution)/shard_map/pallas_call | solution.py:581
  146.8 6.3 fusion.61
  159.5 118.2 %shard_map.163 = (bf16[8,320,512]{2,1,0:T(8,128)(2,1)}, bf16[8,320,512]{2,1,0:T(8,128)(2,1)}) custom-call(bf16[8,320,512]{2,1,0:T(8,128)(2,1)} %bitcast.150, bf16[512,2048]{1,0:T(8,128)(2,1)} %get-tuple-element.45.win_ref, bf16[2048,512]{1,0:T(8,128)(2,1)} %get-tuple-element.46.wout_ref), custom_call_target="tpu_custom_call" | custom-call | tf_op jit(solution)/shard_map/pallas_call | solution.py:359
  277.8 4.9 fusion.10
  282.6 4.8 fusion.91
  287.4 14.4 %shard_map.164 = (f32[5,208,512]{2,1,0:T(8,128)}, bf16[5,208,512]{2,1,0:T(8,128)(2,1)}, f32[5,208,128]{2,1,0:T(8,128)}, bf16[5,208,512]{2,1,0:T(8,128)(2,1)}) custom-call(f32[5,208,512]{2,1,0:T(8,128)} %bitcast.136, bf16[4,512,512]{2,1,0:T(8,128)(2,1)} %get-tuple-element.110.mats_ref, f32[2,512]{1,0:T(2,128)} %squeeze.28.gains_ref, ...), custom_call_target="tpu_custom_call" | custom-call | tf_op jit(solution)/shard_map/pallas_call | solution.py:581
  303.3 7.6 %fusion.58 = bf16[2560,512]{1,0:T(8,128)(2,1)} fusion(bf16[1040,512]{1,0:T(8,128)(2,1)} %bitcast.184, s32[1040]{0:T(1024)S(1)} %get-tuple-element.100, s32[1040]{0:T(1024)S(1)} %get-tuple-element.99), kind=kOutput, calls=%fused_computation.60 | convolution fusion | flops 2748907520 | bytes 3694720 | tf_op jit(solution)/shard_map/dot_general | solution.py:19
  310.9 87.8 %shard_map.165 = (bf16[8,320,512]{2,1,0:T(8,128)(2,1)}, bf16[8,320,512]{2,1,0:T(8,128)(2,1)}) custom-call(bf16[8,320,512]{2,1,0:T(8,128)(2,1)} %bitcast.151, bf16[512,2048]{1,0:T(8,128)(2,1)} %bitcast.141, bf16[2048,512]{1,0:T(8,128)(2,1)} %bitcast.143), custom_call_target="tpu_custom_call" | custom-call | tf_op jit(solution)/shard_map/pallas_call | solution.py:359
  398.7 4.8 fusion.1
  403.5 4.5 multiply_reduce_fusion.3
  408.1 6.4 fusion
  414.7 7.7 %add_convert_fusion.1 = bf16[2560,512]{1,0:T(8,128)(2,1)} fusion(f32[2560,512]{1,0:T(8,128)} %fusion, s32[1040]{0:T(1024)S(1)} %get-tuple-element.99, f32[1040,512]{1,0:T(8,128)S(1)} %bitcast.135, f32[1040]{0:T(1024)S(1)} %get-tuple-element.96), kind=kOutput, calls=%fused_computation.59 | convolution fusion | flops 2732646400 | bytes 10002560 | tf_op jit(solution)/shard_map/dot_general | solution.py:19
  422.3 89.3 %shard_map.166 = (bf16[8,320,512]{2,1,0:T(8,128)(2,1)}, f32[512,512]{1,0:T(8,128)}, f32[512,512]{1,0:T(8,128)}) custom-call(bf16[8,320,512]{2,1,0:T(8,128)(2,1)} %bitcast.149, bf16[8,320,512]{2,1,0:T(8,128)(2,1)} %get-tuple-element.54.arrived_ref, bf16[512,2048]{1,0:T(8,128)(2,1)} %bitcast.142, bf16[2048,512]{1,0:T(8,128)(2,1)} %bitcast.144), custom_call_target="tpu_custom_call" | custom-call | tf_op jit(solution)/shard_map/pallas_call | solution.py:376
  512.4 6.7 fusion.31.grad_ref
  519.0 29.7 %shard_map.167 = (f32[5,208,512]{2,1,0:T(8,128)}, f32[4,512,128]{2,1,0:T(8,128)}, f32[128,512]{1,0:T(8,128)}, f32[2,512]{1,0:T(2,128)}) custom-call(s32[1]{0:T(128)} %bitcast.29.own_ref, f32[5,208,512]{2,1,0:T(8,128)} %copy-done, f32[5,208,512]{2,1,0:T(8,128)} %fusion.31.grad_ref, bf16[5,208,128]{2,1,0:T(8,128)(2,1)} %bitcast.157, f32[5,208,512]{2,1,0:T(8,128)} %bitcast.137, ...), custom_call_target="tpu_custom_call" | custom-call | tf_op jit(solution)/shard_map/pallas_call | solution.py:600
  548.7 5.7 fusion.6
  554.5 6.0 add_convert_fusion
  562.1 88.8 %shard_map.168 = (bf16[8,320,512]{2,1,0:T(8,128)(2,1)}, f32[512,512]{1,0:T(8,128)}, f32[512,512]{1,0:T(8,128)}) custom-call(bf16[8,320,512]{2,1,0:T(8,128)(2,1)} %bitcast.148, bf16[8,320,512]{2,1,0:T(8,128)(2,1)} %get-tuple-element.58.arrived_ref, bf16[512,2048]{1,0:T(8,128)(2,1)} %get-tuple-element.45.win_ref, bf16[2048,512]{1,0:T(8,128)(2,1)} %get-tuple-element.46.wout_ref), custom_call_target="tpu_custom_call" | custom-call | tf_op jit(solution)/shard_map/pallas_call | solution.py:376
  650.9 6.7 fusion.26.grad_ref
  657.6 29.4 %shard_map.169 = (f32[5,208,512]{2,1,0:T(8,128)}, f32[4,512,128]{2,1,0:T(8,128)}, f32[128,512]{1,0:T(8,128)}, f32[2,512]{1,0:T(2,128)}) custom-call(s32[1]{0:T(128)} %bitcast.29.own_ref, f32[5,208,512]{2,1,0:T(8,128)} %get-tuple-element.57.upstream_ref, f32[5,208,512]{2,1,0:T(8,128)} %fusion.26.grad_ref, bf16[5,208,128]{2,1,0:T(8,128)(2,1)} %bitcast.156, ...), custom_call_target="tpu_custom_call" | custom-call | tf_op jit(solution)/shard_map/pallas_call | solution.py:600
  692.2 17.7 %shard_map.170 = f32[544,128]{1,0:T(8,128)} custom-call(bf16[8,544,128]{2,1,0:T(8,128)(2,1)} %pad_maximum_fusion.rows_ref), custom_call_target="tpu_custom_call" | custom-call | tf_op jit(solution)/shard_map/pallas_call | solution.py:426
  (150 shorter events, 48.1 us)
Async XLA Ops:
  7.2 303.7 %all-gather.5.cloned.1.call-start = ((), (), s32[]{:S(2)}) async-start(), calls=%async_computation | async-start | bytes 2621440 | tf_op jit(solution)/shard_map/all_gather | solution.py:662
  116.7 194.2 %all-gather.7.cloned.1.call-start = ((), (), s32[]{:S(2)}) async-start(), calls=%async_computation.1 | async-start | bytes 2621440 | tf_op jit(solution)/shard_map/all_gather | solution.py:662
  122.9 3.6 copy-start.14
  122.9 3.8 copy-start.13
  143.2 3.6 copy-start.18
  153.2 3.0 copy-start.8
  159.5 255.2 %copy-start = (f32[5,208,512]{2,1,0:T(8,128)}, f32[5,208,512]{2,1,0:T(8,128)S(1)}, u32[]{:S(2)}) copy-start(f32[5,208,512]{2,1,0:T(8,128)S(1)} %pad.53.upstream_ref) | copy-start | bytes 6389764
  277.7 4.9 copy-start.6
  277.7 4.9 copy-start.16
  282.6 4.8 copy-start.3
  398.7 4.9 copy-start.17
  403.5 4.5 copy-start.7
  548.7 5.8 copy-start.1
  554.5 6.1 copy-start.4
  554.5 6.1 copy-start.5
  687.0 3.1 copy-start.15
  687.0 4.0 copy-start.9
  691.1 21.9 %copy-start.2 = (f32[5,208,512]{2,1,0:T(8,128)S(1)}, f32[5,208,512]{2,1,0:T(8,128)}, u32[]{:S(2)}) copy-start(f32[5,208,512]{2,1,0:T(8,128)} %get-tuple-element.48.middle_ref) | copy-start | bytes 6389764
  719.4 4.2 copy-start.11
  720.9 5.4 copy-start.10
  721.1 5.2 copy-start.12
Sparse Core Ops, SparseCore 0:
  116.8 56.5 all-gather.4
  175.0 84.2 all-gather.6

commit v5 on v4

--- a/solution.py
+++ b/solution.py
@@ -66,6 +66,97 @@
     barrier = pltpu.get_barrier_semaphore()
     greet_axis(barrier, "expert", me, peers)
     pl.semaphore_wait(barrier, peers - 1)
+
+
+class Ring:
+    def __init__(self, parts, place, own, sends, arrivals, both=True):
+        self.parts, self.place, self.own = parts, place, own
+        self.sends, self.arrivals = sends, arrivals
+        self.side = lax.axis_index("tensor")
+        self.hops = []
+        for distance in range(1, parts // 2 + 1):
+            if 2 * distance < parts:
+                self.hops += [(distance, 1, None), (distance, -1, None)]
+            elif both:
+                self.hops += [(distance, 1, 0), (distance, -1, 1)]
+            else:
+                self.hops += [(distance, 1, None)]
+
+    def wrap(self, index):
+        return lax.rem(self.side + self.parts + index, self.parts)
+
+    def outgoing(self, number):
+        distance, way, half = self.hops[number]
+        landing = self.place(self.wrap(-way * (distance - 1)), half)
+        source = landing if distance > 1 else self.own(half)
+        return send(
+            source,
+            landing,
+            self.sends(number),
+            self.arrivals(number),
+            "tensor",
+            self.wrap(way),
+        )
+
+    def incoming(self, number):
+        distance, way, half = self.hops[number]
+        landing = self.place(self.wrap(-way * distance), half)
+        return send(
+            landing,
+            landing,
+            self.sends(number),
+            self.arrivals(number),
+            "tensor",
+            self.wrap(way),
+        )
+
+    def stage(self, wanted):
+        for number, (distance, way, _) in enumerate(self.hops):
+            if distance == wanted:
+                for earlier, (before, same, _) in enumerate(self.hops):
+                    if before == distance - 1 and same == way:
+                        self.incoming(earlier).wait_recv()
+                self.outgoing(number).start()
+
+    def finish(self):
+        kept = {(distance, way) for distance, way, _ in self.hops}
+        for number, (distance, way, _) in enumerate(self.hops):
+            self.outgoing(number).wait_send()
+            if (distance + 1, way) not in kept:
+                self.incoming(number).wait_recv()
+
+
+def weight_rings(parts, sources, targets, sends, arrivals):
+    def ring_of(kind):
+        source, target = sources[kind], targets[kind]
+        length = source.shape[1 - kind]
+
+        def cut(ref, start, half):
+            size = length if half is None else length // 2
+            start = start + (0 if half is None else half * size)
+            span = pl.ds(pl.multiple_of(start, size), size)
+            return ref.at[:, span] if kind == 0 else ref.at[span, :]
+
+        return Ring(
+            parts,
+            lambda owner, half: cut(target, owner * length, half),
+            lambda half: cut(source, 0, half),
+            lambda number: sends.at[kind, number],
+            lambda number: arrivals.at[kind, number],
+        )
+
+    return [ring_of(kind) for kind in range(2)]
+
+
+def own_weights(sources, targets, local_sem):
+    side = lax.axis_index("tensor")
+    copies = []
+    for kind in range(2):
+        length = sources[kind].shape[1 - kind]
+        span = pl.ds(pl.multiple_of(side * length, length), length)
+        target = targets[kind].at[:, span] if kind == 0 else targets[kind].at[span, :]
+        copies.append(pltpu.make_async_copy(sources[kind], target, local_sem.at[kind]))
+    return copies
 
 
 def gather_kernel(
@@ -79,6 +170,8 @@
     wout_full,
     side_send,
     side_recv,
+    ring_send,
+    ring_recv,
     chip_send,
     chip_recv,
     twin_send,
@@ -90,7 +183,6 @@
     twin = me + 1 - 2 * lax.rem(me, 2)
     chips = experts // 2
     cols = small_ref.shape[2]
-    width = win_ref.shape[1]
     barrier = pltpu.get_barrier_semaphore()
     greet_axis(barrier, "tensor", side, parts)
     greet(barrier, "expert", twin)
@@ -98,31 +190,26 @@
         greet(barrier, "expert", lax.rem(me + 2 * step, experts))
     pl.semaphore_wait(barrier, parts - 1 + chips)
 
-    def places(index):
-        lanes = pl.ds(pl.multiple_of(index * cols, cols), cols)
-        hidden = pl.ds(pl.multiple_of(index * width, width), width)
-        return (whole.at[:, me, :, lanes], win_full.at[:, hidden], wout_full.at[hidden, :])
-
-    sources = (small_ref, win_ref, wout_ref)
-
-    def side_copy(kind, step, owner, target):
+    def place(index):
+        return whole.at[:, me, :, pl.ds(pl.multiple_of(index * cols, cols), cols)]
+
+    def side_copy(step, owner, target):
         return send(
-            sources[kind],
-            places(owner)[kind],
-            side_send.at[kind, step],
-            side_recv.at[kind, step],
-            "tensor",
-            target,
-        )
-
-    for kind in range(3):
-        for step in range(1, parts):
-            side_copy(kind, step, side, lax.rem(side + step, parts)).start()
-    for kind in range(3):
-        pltpu.make_async_copy(sources[kind], places(side)[kind], local_sem.at[kind]).start()
-    pltpu.make_async_copy(sources[0], places(side)[0], local_sem.at[0]).wait()
+            small_ref, place(owner), side_send.at[step], side_recv.at[step], "tensor", target
+        )
+
     for step in range(1, parts):
-        side_copy(0, step, lax.rem(side + parts - step, parts), side).wait_recv()
+        side_copy(step, side, lax.rem(side + step, parts)).start()
+    rings = weight_rings(parts, (win_ref, wout_ref), (win_full, wout_full), ring_send, ring_recv)
+    for ring in rings:
+        ring.stage(1)
+    copies = own_weights((win_ref, wout_ref), (win_full, wout_full), local_sem)
+    copies.append(pltpu.make_async_copy(small_ref, place(side), local_sem.at[2]))
+    for copy in copies:
+        copy.start()
+    copies[2].wait()
+    for step in range(1, parts):
+        side_copy(step, lax.rem(side + parts - step, parts), side).wait_recv()
 
     def chip_copy(step, owner, target):
         return send_chunk(whole.at[:, owner], whole.at[:, owner], chip_send, chip_recv, step, target)
@@ -133,6 +220,9 @@
     for step in range(1, chips):
         chip_copy(step, me, lax.rem(me + 2 * step, experts)).start()
     twin_copy(0, me).start()
+    for distance in range(2, parts // 2 + 1):
+        for ring in rings:
+            ring.stage(distance)
     for step in range(1, chips):
         owner = lax.rem(me + experts - 2 * step, experts)
         chip_copy(step, owner, owner).wait_recv()
@@ -142,14 +232,12 @@
         twin_copy(step, lax.rem(me + experts - 2 * step, experts)).wait_send()
         if step:
             chip_copy(step, me, lax.rem(me + 2 * step, experts)).wait_send()
-    for kind in range(3):
-        for step in range(1, parts):
-            one = side_copy(kind, step, lax.rem(side + parts - step, parts), side)
-            one.wait_send()
-            if kind:
-                one.wait_recv()
-    for kind in range(1, 3):
-        pltpu.make_async_copy(sources[kind], places(side)[kind], local_sem.at[kind]).wait()
+    for step in range(1, parts):
+        side_copy(step, side, lax.rem(side + step, parts)).wait_send()
+    for ring in rings:
+        ring.finish()
+    for copy in copies[:2]:
+        copy.wait()
 
 
 def gather_start(small, win, wout, experts, parts):
@@ -165,14 +253,17 @@
         ),
         in_specs=whole_in_vmem(3),
         out_specs=tuple(whole_in_vmem(3)),
-        scratch_shapes=[pltpu.SemaphoreType.DMA((3, parts))] * 2
+        scratch_shapes=[pltpu.SemaphoreType.DMA((parts,))] * 2
+        + [pltpu.SemaphoreType.DMA((2, parts))] * 2
         + [pltpu.SemaphoreType.DMA((chips,))] * 4
         + [pltpu.SemaphoreType.DMA((3,))],
         compiler_params=pltpu.CompilerParams(collective_id=3, has_side_effects=True),
     )(small, win, wout)
 
 
-def exchange_chunks(peers, parts, work, out_rows, landed, results, back, sems, sum_up=None):
+def exchange_chunks(
+    peers, parts, work, out_rows, landed, results, back, sems, sum_up=None, rings=()
+):
     out_send, out_recv, back_send, back_recv, side_send, side_recv = sems
     me = lax.axis_index("expert")
     side = lax.axis_index("tensor")
@@ -193,25 +284,41 @@
         return carry
 
     lax.fori_loop(1, peers, start_out, 0)
+    for ring in rings:
+        ring.stage(1)
     landed[me] = out_rows[me]
 
-    def side_copy(shift, step, slab, owner, target):
-        place = back.at[slab, share_of(owner)]
-        return send(
-            place, place, side_send.at[shift, step], side_recv.at[shift, step], "tensor", target
-        )
-
-    def pass_on(step):
+    first = -(-share // 32) * 16
+    distances = range(1, parts // 2 + 1)
+
+    def chunk_ring(step):
         slab = lax.rem(me + step, peers)
 
-        @pl.when(step > 0)
-        def _():
-            send_chunk(
-                results.at[step], back.at[slab, mine], back_send, back_recv, step, slab
-            ).wait_recv()
-
-        for shift in range(1, parts):
-            side_copy(shift, step, slab, side, lax.rem(side + shift, parts)).start()
+        def place(owner, half):
+            start = owner * share + (first if half == 1 else 0)
+            size = share if half is None else (share - first if half else first)
+            return back.at[slab, pl.ds(pl.multiple_of(start, 16), size)]
+
+        return Ring(
+            parts,
+            place,
+            lambda half: place(side, half),
+            lambda number: side_send.at[number, step],
+            lambda number: side_recv.at[number, step],
+            both=first < share,
+        )
+
+    def pass_on(step, distance):
+        if distance == 1:
+            slab = lax.rem(me + step, peers)
+
+            @pl.when(step > 0)
+            def _():
+                send_chunk(
+                    results.at[step], back.at[slab, mine], back_send, back_recv, step, slab
+                ).wait_recv()
+
+        chunk_ring(step).stage(distance)
 
     lag = 2
 
@@ -236,9 +343,19 @@
         def _():
             back[me, mine] = results[0]
 
-        @pl.when(step >= lag)
-        def _():
-            pass_on(step - lag)
+        for distance in distances:
+
+            @pl.when(step >= lag * distance)
+            def _(distance=distance):
+                pass_on(step - lag * distance, distance)
+
+        if rings:
+
+            @pl.when(step == peers // 2)
+            def _():
+                for distance in distances[1:]:
+                    for ring in rings:
+                        ring.stage(distance)
 
         if sum_up is not None:
             sum_up(peer)
@@ -246,11 +363,13 @@
 
     lax.fori_loop(0, peers, one_chunk, 0)
 
-    def pass_last(step, carry):
-        pass_on(step)
-        return carry
-
-    lax.fori_loop(peers - lag, peers, pass_last, 0)
+    for distance in distances:
+
+        def pass_last(step, carry, distance=distance):
+            pass_on(step, distance)
+            return carry
+
+        lax.fori_loop(max(0, peers - lag * distance), peers, pass_last, 0)
 
     def finish(step, carry):
         ahead = lax.rem(me + step, peers)
@@ -264,18 +383,26 @@
                 results.at[step], back.at[me, mine], back_send, back_recv, step, ahead
             ).wait_send()
 
-        for shift in range(1, parts):
-            behind = lax.rem(side + parts - shift, parts)
-            side_copy(shift, step, ahead, side, lax.rem(side + shift, parts)).wait_send()
-            side_copy(shift, step, ahead, behind, behind).wait_recv()
+        chunk_ring(step).finish()
         return carry
 
     lax.fori_loop(0, peers, finish, 0)
-
-
-def forward_kernel(
-    peers, parts, rows_ref, win_ref, wout_ref, landed, back, results, total, *sems
-):
+    for ring in rings:
+        ring.finish()
+
+
+def forward_kernel(peers, parts, follow, *refs):
+    rows_ref, win_ref, wout_ref = refs[:3]
+    sources = refs[3 : 3 + follow]
+    landed, back = refs[3 + follow : 5 + follow]
+    targets = refs[5 + follow : 5 + 2 * follow]
+    results, total, *sems = refs[5 + 2 * follow :]
+    rings, copies = (), ()
+    if follow:
+        rings = weight_rings(parts, sources, targets, sems[6], sems[7])
+        copies = own_weights(sources, targets, sems[8])
+        for copy in copies:
+            copy.start()
     width = win_ref.shape[1] // parts
 
     def work(step, peer, mine):
@@ -292,7 +419,11 @@
             else:
                 results[step] = (total[...] + term).astype(jnp.bfloat16)
 
-    exchange_chunks(peers, parts, work, rows_ref, landed, results, back, sems)
+    exchange_chunks(
+        peers, parts, work, rows_ref, landed, results, back, sems[:6], rings=rings
+    )
+    for copy in copies:
+        copy.wait()
 
 
 def backward_kernel(
@@ -353,21 +484,27 @@
     return [pltpu.SemaphoreType.DMA((peers,))] * 4 + [pltpu.SemaphoreType.DMA((parts, peers))] * 2
 
 
-def experts_forward(rows, win, wout, parts):
+def experts_forward(rows, win, wout, parts, following=()):
     peers, capacity, width = rows.shape
     like = jax.ShapeDtypeStruct(rows.shape, jnp.bfloat16)
+    follow = len(following)
+    wholes = (win, wout)[:follow]
     return pl.pallas_call(
-        functools.partial(forward_kernel, peers, parts),
-        out_shape=(like, like),
-        in_specs=whole_in_vmem(3),
-        out_specs=tuple(whole_in_vmem(2)),
+        functools.partial(forward_kernel, peers, parts, follow),
+        out_shape=(like, like) + tuple(jax.ShapeDtypeStruct(w.shape, w.dtype) for w in wholes),
+        in_specs=whole_in_vmem(3 + follow),
+        out_specs=tuple(whole_in_vmem(2 + follow)),
         scratch_shapes=[
             pltpu.VMEM((peers, capacity // parts, width), jnp.bfloat16),
             pltpu.VMEM((capacity // parts, width), jnp.float32),
         ]
-        + exchange_sems(peers, parts),
-        compiler_params=pltpu.CompilerParams(collective_id=0, has_side_effects=True),
-    )(rows, win, wout)
+        + exchange_sems(peers, parts)
+        + [pltpu.SemaphoreType.DMA((2, parts))] * follow
+        + [pltpu.SemaphoreType.DMA((2,))] * (follow // 2),
+        compiler_params=pltpu.CompilerParams(
+            collective_id=4 if follow else 0, has_side_effects=True
+        ),
+    )(rows, win, wout, *following)
 
 
 def experts_backward(rows, arrived, win, wout, parts):
@@ -680,9 +817,6 @@
         peers_tensor,
     )
     whole = whole.reshape(whole.shape[0], model_width, model_width)
-    later_in, later_out, whole = lax.optimization_barrier(
-        (expert_in[1:, 0], expert_out[1:, 0], whole)
-    )
     small_rows = whole[4 * layers :, :, :head_cols].reshape(-1, experts, block)
     small_rows = small_rows.transpose(1, 0, 2).reshape(experts, -1)
     router_all = small_rows[:, : layers * model_width].reshape(experts, layers, model_width)
@@ -691,9 +825,6 @@
     gains_all = gains_all.reshape(layers, 2, model_width).astype(jnp.float32)
     router_all = jnp.pad(router_all.transpose(1, 2, 0), ((0, 0), (0, 0), (0, -experts % 128)))
     win_full, wout_full = [win_first], [wout_first]
-    for layer_index in range(layers - 1):
-        win_full.append(gather_tensor(later_in[layer_index], 1))
-        wout_full.append(gather_tensor(later_out[layer_index], 0))
     slot_ids = lax.broadcasted_iota(jnp.int32, (1, slots_all), 1)
     stream = spread(inputs, 0)
     stash_list = []
@@ -715,12 +846,22 @@
         pick_second = (target[:, 1:2] == slot_ids).astype(jnp.bfloat16)
         pick_both = pick_first + pick_second
         dispatched = contract_rows(pick_both, normed_two.reshape(tokens_all, model_width))
-        arrived, returned = experts_forward(
+        following = ()
+        if layer_index + 1 < layers:
+            following = (
+                expert_in[layer_index + 1, 0].astype(jnp.bfloat16),
+                expert_out[layer_index + 1, 0].astype(jnp.bfloat16),
+            )
+        arrived, returned, *gathered = experts_forward(
             dispatched.astype(jnp.bfloat16).reshape(experts, spacing, model_width),
             win_full[layer_index],
             wout_full[layer_index],
             peers_tensor,
-        )
+            following,
+        )
+        if gathered:
+            win_full.append(gathered[0])
+            wout_full.append(gathered[1])
         returned = returned.reshape(slots_all, model_width)
         rows_first = jnp.dot(pick_first, returned, preferred_element_type=jnp.float32)
         rows_second = jnp.dot(pick_second, returned, preferred_element_type=jnp.float32)

time: 738 us -> 695 us (0.942)
  Pallas kernels: 592 us -> 560 us
  between operations: 14.8 us -> 1.5 us
    pallas_call x2, Pallas kernels: 178 us -> 162 us  [experts_backward(): pl.pallas_call(functools.partial(backward_kernel, peers, parts), out_shap...]
    pallas_call x1, Pallas kernels: 102 us -> 86.3 us  [gather_start(): pl.pallas_call(functools.partial(gather_kernel, experts, parts), out_shap...]
  transfers between devices with their start and end apart: 2 -> 0, of which waited for: 0 -> 0; matrix products, arithmetic and copies ran while one was open for 6% -> 0% of each run, Pallas kernels for 20% -> 0%
where the time goes in v5:
time: 695 us; the launch traced here: 686 us
  Pallas kernels  560 us (81%)
  matrix products  74.6 us (11%)
  local copies, waits for them, and re-layouts  34.5 us (5%)
  other arithmetic  16 us (2%)
    pallas_call x2, Pallas kernels, experts_forward(): pl.pallas_call(functools.partial(forward_kernel, peers, parts, follow), o...  206 us
    pallas_call x2, Pallas kernels, experts_backward(): pl.pallas_call(functools.partial(backward_kernel, peers, parts), out_shap...  162 us
    pallas_call x1, Pallas kernels, gather_start(): pl.pallas_call(functools.partial(gather_kernel, experts, parts), out_shap...  86.3 us
    pallas_call x2, Pallas kernels, attend_back(): pl.pallas_call(attend_back_kernel, grid=(images,), out_shape=(jax.ShapeDt...  59.1 us
    dot_general x6, matrix products, contract_rows(): lax.dot_general(left_side, right_side, (((0,), (0,)), ((), ())), preferre...  34.7 us
    pallas_call x2, Pallas kernels, attend(): pl.pallas_call(functools.partial(attend_kernel, experts), grid=(images,),...  28.9 us
    pallas_call x1, Pallas kernels, sum_shares(): pl.pallas_call(functools.partial(sum_kernel, peers), out_shape=jax.ShapeD...  17.6 us

profile of v5, /device:TPU:1, one launch (start us, length us, event | category | flops | bytes accessed | tf_op | source)
XLA Modules:
  0.0 686.3 jit_solution(5120391455421220549)
XLA Ops:
  8.2 86.3 %shard_map.161 = (bf16[9,8,64,512]{3,2,1,0:T(8,128)(2,1)}, bf16[512,2048]{1,0:T(8,128)(2,1)}, bf16[2048,512]{1,0:T(8,128)(2,1)}) custom-call(bf16[9,64,128]{2,1,0:T(8,128)(2,1)} %pad_maximum_fusion.2.small_ref, bf16[512,512]{1,0:T(8,128)(2,1)} %get-tuple-element.129.win_ref, bf16[512,512]{1,0:T(8,128)(2,1)} %get-tuple-element.111.wout_ref), custom_call_target="tpu_custom_call" | custom-call | tf_op jit(solution)/shard_map/pallas_call | solution.py:247
  94.6 4.7 fusion.134
  102.0 14.4 %shard_map.162 = (f32[5,208,512]{2,1,0:T(8,128)}, bf16[5,208,512]{2,1,0:T(8,128)(2,1)}, f32[5,208,128]{2,1,0:T(8,128)}, bf16[5,208,512]{2,1,0:T(8,128)(2,1)}) custom-call(f32[5,208,512]{2,1,0:T(8,128)} %pad.46.stream_ref, bf16[4,512,512]{2,1,0:T(8,128)(2,1)} %bitcast.135, f32[2,512]{1,0:T(2,128)} %squeeze.8.gains_ref, ...), custom_call_target="tpu_custom_call" | custom-call | tf_op jit(solution)/shard_map/pallas_call | solution.py:718
  120.2 6.4 fusion.61
  126.5 125.6 %shard_map.163 = (bf16[8,320,512]{2,1,0:T(8,128)(2,1)}, bf16[8,320,512]{2,1,0:T(8,128)(2,1)}, bf16[512,2048]{1,0:T(8,128)(2,1)}, bf16[2048,512]{1,0:T(8,128)(2,1)}) custom-call(bf16[8,320,512]{2,1,0:T(8,128)(2,1)} %bitcast.152, bf16[512,2048]{1,0:T(8,128)(2,1)} %get-tuple-element.43.refs_1_.win_ref, bf16[2048,512]{1,0:T(8,128)(2,1)} %get-tuple-element.44.refs_2_.wout_ref, ...), custom_call_target="tpu_custom_call" | custom-call | tf_op jit(solution)/shard_map/pallas_call | solution.py:492
  252.2 4.8 fusion.10
  257.1 4.8 fusion.91
  262.5 14.4 %shard_map.164 = (f32[5,208,512]{2,1,0:T(8,128)}, bf16[5,208,512]{2,1,0:T(8,128)(2,1)}, f32[5,208,128]{2,1,0:T(8,128)}, bf16[5,208,512]{2,1,0:T(8,128)(2,1)}) custom-call(f32[5,208,512]{2,1,0:T(8,128)} %bitcast.139, bf16[4,512,512]{2,1,0:T(8,128)(2,1)} %bitcast.137, f32[2,512]{1,0:T(2,128)} %squeeze.20.gains_ref, bf16[512,128]{1,0:T(8,128)(2,1)} %get-tuple-element.120.router_ref), custom_call_target="tpu_custom_call" | custom-call | tf_op jit(solution)/shard_map/pallas_call | solution.py:718
  279.4 6.4 fusion.58
  285.8 80.5 %shard_map.165 = (bf16[8,320,512]{2,1,0:T(8,128)(2,1)}, bf16[8,320,512]{2,1,0:T(8,128)(2,1)}) custom-call(bf16[8,320,512]{2,1,0:T(8,128)(2,1)} %bitcast.151, bf16[512,2048]{1,0:T(8,128)(2,1)} %get-tuple-element.49.refs_1_.win_ref, bf16[2048,512]{1,0:T(8,128)(2,1)} %get-tuple-element.50.refs_2_.wout_ref), custom_call_target="tpu_custom_call" | custom-call | tf_op jit(solution)/shard_map/pallas_call | solution.py:492
  366.4 6.3 fusion.1
  376.4 6.8 multiply_reduce_fusion.3
  383.4 3.3 fusion.90
  391.4 4.0 fusion
  395.4 6.2 add_convert_fusion.1
  401.6 81.0 %shard_map.166 = (bf16[8,320,512]{2,1,0:T(8,128)(2,1)}, f32[512,512]{1,0:T(8,128)}, f32[512,512]{1,0:T(8,128)}) custom-call(bf16[8,320,512]{2,1,0:T(8,128)(2,1)} %bitcast.149, bf16[8,320,512]{2,1,0:T(8,128)(2,1)} %get-tuple-element.52.arrived_ref, bf16[512,2048]{1,0:T(8,128)(2,1)} %get-tuple-element.49.refs_1_.win_ref, ...), custom_call_target="tpu_custom_call" | custom-call | tf_op jit(solution)/shard_map/pallas_call | solution.py:513
  482.7 6.7 fusion.31.grad_ref
  490.4 29.6 %shard_map.167 = (f32[5,208,512]{2,1,0:T(8,128)}, f32[4,512,128]{2,1,0:T(8,128)}, f32[128,512]{1,0:T(8,128)}, f32[2,512]{1,0:T(2,128)}) custom-call(s32[1]{0:T(128)} %bitcast.29.own_ref, f32[5,208,512]{2,1,0:T(8,128)} %copy-done, f32[5,208,512]{2,1,0:T(8,128)} %fusion.31.grad_ref, bf16[5,208,128]{2,1,0:T(8,128)(2,1)} %bitcast.158, f32[5,208,512]{2,1,0:T(8,128)} %bitcast.140, ...), custom_call_target="tpu_custom_call" | custom-call | tf_op jit(solution)/shard_map/pallas_call | solution.py:737
  520.0 5.7 fusion.6
  525.8 6.0 add_convert_fusion
  531.8 80.8 %shard_map.168 = (bf16[8,320,512]{2,1,0:T(8,128)(2,1)}, f32[512,512]{1,0:T(8,128)}, f32[512,512]{1,0:T(8,128)}) custom-call(bf16[8,320,512]{2,1,0:T(8,128)(2,1)} %bitcast.150, bf16[8,320,512]{2,1,0:T(8,128)(2,1)} %get-tuple-element.56.arrived_ref, bf16[512,2048]{1,0:T(8,128)(2,1)} %get-tuple-element.43.refs_1_.win_ref, ...), custom_call_target="tpu_custom_call" | custom-call | tf_op jit(solution)/shard_map/pallas_call | solution.py:513
  612.8 6.8 fusion.26.grad_ref
  621.1 29.4 %shard_map.169 = (f32[5,208,512]{2,1,0:T(8,128)}, f32[4,512,128]{2,1,0:T(8,128)}, f32[128,512]{1,0:T(8,128)}, f32[2,512]{1,0:T(2,128)}) custom-call(s32[1]{0:T(128)} %bitcast.29.own_ref, f32[5,208,512]{2,1,0:T(8,128)} %get-tuple-element.55.upstream_ref, f32[5,208,512]{2,1,0:T(8,128)} %fusion.26.grad_ref, bf16[5,208,128]{2,1,0:T(8,128)(2,1)} %bitcast.157, ...), custom_call_target="tpu_custom_call" | custom-call | tf_op jit(solution)/shard_map/pallas_call | solution.py:737
  658.3 17.6 %shard_map.170 = f32[544,128]{1,0:T(8,128)} custom-call(bf16[8,544,128]{2,1,0:T(8,128)(2,1)} %pad_maximum_fusion.rows_ref), custom_call_target="tpu_custom_call" | custom-call | tf_op jit(solution)/shard_map/pallas_call | solution.py:563
  (157 shorter events, 46.2 us)
Async XLA Ops:
  2.4 1.6 copy-start.21
  2.5 1.7 copy-start.18
  2.5 1.7 copy-start.15
  2.5 1.7 copy-start.14
  4.0 2.6 copy-start.7
  100.4 16.0 %copy-start.17 = (s32[2,985]{1,0:T(2,128)S(1)}, s32[2,985]{1,0:T(2,128)}, u32[]{:S(2)}) copy-start(s32[2,985]{1,0:T(2,128)} %param.13) | copy-start | bytes 23644
  101.1 15.6 %copy-start.16 = (s32[2,985,2]{1,2,0:T(2,128)S(1)}, s32[2,985,2]{1,2,0:T(2,128)}, u32[]{:S(2)}) copy-start(s32[2,985,2]{1,2,0:T(2,128)} %param.12) | copy-start | bytes 47284
  116.4 3.8 copy-start.23
  252.2 4.9 copy-start.5
  252.2 4.9 copy-start.22
  257.0 4.8 copy-start.2
  277.0 2.4 copy-start.24
  366.4 6.3 copy-start.8
  374.2 2.2 copy-start.6
  376.2 19.2 %copy-start = (f32[5,208,512]{2,1,0:T(8,128)}, f32[5,208,512]{2,1,0:T(8,128)S(1)}, u32[]{:S(2)}) copy-start(f32[5,208,512]{2,1,0:T(8,128)S(1)} %pad.53.upstream_ref) | copy-start | bytes 6389764
  376.4 6.8 copy-start.13
  520.0 5.8 copy-start.1
  612.7 6.9 copy-start.3
  612.7 6.9 copy-start.4
  652.3 3.8 copy-start.19
  652.3 4.8 copy-start.9
  657.2 24.7 %copy-start.11 = (f32[512,512]{1,0:T(8,128)S(1)}, f32[512,512]{1,0:T(8,128)}, u32[]{:S(2)}) copy-start(f32[512,512]{1,0:T(8,128)} %get-tuple-element.67) | copy-start | bytes 3145732
  675.9 8.7 %copy-start.10 = (f32[512,512]{1,0:T(8,128)S(1)}, f32[512,512]{1,0:T(8,128)}, u32[]{:S(2)}) copy-start(f32[512,512]{1,0:T(8,128)} %get-tuple-element.69) | copy-start | bytes 3145732
  675.9 8.7 %copy-start.12 = (f32[512,512]{1,0:T(8,128)S(1)}, f32[512,512]{1,0:T(8,128)}, u32[]{:S(2)}) copy-start(f32[512,512]{1,0:T(8,128)} %get-tuple-element.68) | copy-start | bytes 3145732
  (1 other events, 1.6 us)

commit v6 on v3

--- a/solution.py
+++ b/solution.py
@@ -33,37 +33,228 @@
     return rows_in * half, slope
 
 
-def meet_peers(me, peers):
-    barrier = pltpu.get_barrier_semaphore()
-
-    def greet(step, carry):
-        pl.semaphore_signal(
-            barrier,
-            inc=1,
-            device_id={"expert": lax.rem(me + step, peers)},
-            device_id_type=pl.DeviceIdType.MESH,
-        )
+def greet(barrier, axis, index):
+    pl.semaphore_signal(
+        barrier, inc=1, device_id={axis: index}, device_id_type=pl.DeviceIdType.MESH
+    )
+
+
+def greet_axis(barrier, axis, me, peers):
+    def one(step, carry):
+        greet(barrier, axis, lax.rem(me + step, peers))
         return carry
 
-    lax.fori_loop(1, peers, greet, 0)
-    pl.semaphore_wait(barrier, peers - 1)
-
-
-def send_chunk(source, landing, sends, arrivals, step, peer):
+    lax.fori_loop(1, peers, one, 0)
+
+
+def send(source, landing, send_sem, recv_sem, axis, index):
     return pltpu.make_async_remote_copy(
         src_ref=source,
         dst_ref=landing,
-        send_sem=sends.at[step],
-        recv_sem=arrivals.at[step],
-        device_id={"expert": peer},
+        send_sem=send_sem,
+        recv_sem=recv_sem,
+        device_id={axis: index},
         device_id_type=pl.DeviceIdType.MESH,
     )
 
 
-def exchange_chunks(peers, work, out_rows, landed, results, back, sems):
+def send_chunk(source, landing, sends, arrivals, step, peer):
+    return send(source, landing, sends.at[step], arrivals.at[step], "expert", peer)
+
+
+def meet_peers(me, peers):
+    barrier = pltpu.get_barrier_semaphore()
+    greet_axis(barrier, "expert", me, peers)
+    pl.semaphore_wait(barrier, peers - 1)
+
+
+class Ring:
+    def __init__(self, parts, place, own, sends, arrivals, both=True):
+        self.parts, self.place, self.own = parts, place, own
+        self.sends, self.arrivals = sends, arrivals
+        self.side = lax.axis_index("tensor")
+        self.hops = []
+        for distance in range(1, parts // 2 + 1):
+            if 2 * distance < parts:
+                self.hops += [(distance, 1, None), (distance, -1, None)]
+            elif both:
+                self.hops += [(distance, 1, 0), (distance, -1, 1)]
+            else:
+                self.hops += [(distance, 1, None)]
+
+    def wrap(self, index):
+        return lax.rem(self.side + self.parts + index, self.parts)
+
+    def outgoing(self, number):
+        distance, way, half = self.hops[number]
+        landing = self.place(self.wrap(-way * (distance - 1)), half)
+        source = landing if distance > 1 else self.own(half)
+        return send(
+            source,
+            landing,
+            self.sends(number),
+            self.arrivals(number),
+            "tensor",
+            self.wrap(way),
+        )
+
+    def incoming(self, number):
+        distance, way, half = self.hops[number]
+        landing = self.place(self.wrap(-way * distance), half)
+        return send(
+            landing,
+            landing,
+            self.sends(number),
+            self.arrivals(number),
+            "tensor",
+            self.wrap(way),
+        )
+
+    def stage(self, wanted):
+        for number, (distance, way, _) in enumerate(self.hops):
+            if distance == wanted:
+                for earlier, (before, same, _) in enumerate(self.hops):
+                    if before == distance - 1 and same == way:
+                        self.incoming(earlier).wait_recv()
+                self.outgoing(number).start()
+
+    def finish(self):
+        kept = {(distance, way) for distance, way, _ in self.hops}
+        for number, (distance, way, _) in enumerate(self.hops):
+            self.outgoing(number).wait_send()
+            if (distance + 1, way) not in kept:
+                self.incoming(number).wait_recv()
+
+
+def weight_ring(parts, kind, source, target, sends, arrivals):
+    length = source.shape[1 - kind]
+
+    def cut(ref, start, half):
+        size = length if half is None else length // 2
+        start = start + (0 if half is None else half * size)
+        span = pl.ds(pl.multiple_of(start, size), size)
+        return ref.at[:, span] if kind == 0 else ref.at[span, :]
+
+    return Ring(
+        parts,
+        lambda owner, half: cut(target, owner * length, half),
+        lambda half: cut(source, 0, half),
+        lambda number: sends.at[number],
+        lambda number: arrivals.at[number],
+    )
+
+
+def own_weight(kind, source, target, local_sem):
+    length = source.shape[1 - kind]
+    span = pl.ds(pl.multiple_of(lax.axis_index("tensor") * length, length), length)
+    place = target.at[:, span] if kind == 0 else target.at[span, :]
+    return pltpu.make_async_copy(source, place, local_sem)
+
+
+def gather_kernel(
+    experts,
+    parts,
+    small_ref,
+    win_ref,
+    whole,
+    win_full,
+    side_send,
+    side_recv,
+    ring_send,
+    ring_recv,
+    chip_send,
+    chip_recv,
+    twin_send,
+    twin_recv,
+    local_sem,
+):
+    me = lax.axis_index("expert")
+    side = lax.axis_index("tensor")
+    twin = me + 1 - 2 * lax.rem(me, 2)
+    chips = experts // 2
+    cols = small_ref.shape[2]
+    barrier = pltpu.get_barrier_semaphore()
+    greet_axis(barrier, "tensor", side, parts)
+    greet(barrier, "expert", twin)
+    for step in range(1, chips):
+        greet(barrier, "expert", lax.rem(me + 2 * step, experts))
+    pl.semaphore_wait(barrier, parts - 1 + chips)
+
+    def place(index):
+        return whole.at[:, me, :, pl.ds(pl.multiple_of(index * cols, cols), cols)]
+
+    def side_copy(step, owner, target):
+        return send(
+            small_ref, place(owner), side_send.at[step], side_recv.at[step], "tensor", target
+        )
+
+    for step in range(1, parts):
+        side_copy(step, side, lax.rem(side + step, parts)).start()
+    ring = weight_ring(parts, 0, win_ref, win_full, ring_send, ring_recv)
+    ring.stage(1)
+    own_win = own_weight(0, win_ref, win_full, local_sem.at[0])
+    own_small = pltpu.make_async_copy(small_ref, place(side), local_sem.at[1])
+    own_win.start()
+    own_small.start()
+    own_small.wait()
+    for step in range(1, parts):
+        side_copy(step, lax.rem(side + parts - step, parts), side).wait_recv()
+
+    def chip_copy(step, owner, target):
+        return send_chunk(whole.at[:, owner], whole.at[:, owner], chip_send, chip_recv, step, target)
+
+    def twin_copy(step, owner):
+        return send_chunk(whole.at[:, owner], whole.at[:, owner], twin_send, twin_recv, step, twin)
+
+    for step in range(1, chips):
+        chip_copy(step, me, lax.rem(me + 2 * step, experts)).start()
+    twin_copy(0, me).start()
+    for distance in range(2, parts // 2 + 1):
+        ring.stage(distance)
+    for step in range(1, chips):
+        owner = lax.rem(me + experts - 2 * step, experts)
+        chip_copy(step, owner, owner).wait_recv()
+        twin_copy(step, owner).start()
+    for step in range(chips):
+        twin_copy(step, lax.rem(twin + experts - 2 * step, experts)).wait_recv()
+        twin_copy(step, lax.rem(me + experts - 2 * step, experts)).wait_send()
+        if step:
+            chip_copy(step, me, lax.rem(me + 2 * step, experts)).wait_send()
+    for step in range(1, parts):
+        side_copy(step, side, lax.rem(side + step, parts)).wait_send()
+    ring.finish()
+    own_win.wait()
+
+
+def gather_start(small, win, experts, parts):
+    count, rows, cols = small.shape
+    depth, width = win.shape
+    chips = experts // 2
+    return pl.pallas_call(
+        functools.partial(gather_kernel, experts, parts),
+        out_shape=(
+            jax.ShapeDtypeStruct((count, experts, rows, cols * parts), jnp.bfloat16),
+            jax.ShapeDtypeStruct((depth, width * parts), jnp.bfloat16),
+        ),
+        in_specs=whole_in_vmem(2),
+        out_specs=tuple(whole_in_vmem(2)),
+        scratch_shapes=[pltpu.SemaphoreType.DMA((parts,))] * 4
+        + [pltpu.SemaphoreType.DMA((chips,))] * 4
+        + [pltpu.SemaphoreType.DMA((2,))],
+        compiler_params=pltpu.CompilerParams(collective_id=3, has_side_effects=True),
+    )(small, win)
+
+
+def exchange_chunks(peers, work, out_rows, landed, results, back, sems, parts=1, rings=()):
     out_send, out_recv, back_send, back_recv = sems
     me = lax.axis_index("expert")
-    meet_peers(me, peers)
+    barrier = pltpu.get_barrier_semaphore()
+    greet_axis(barrier, "expert", me, peers)
+    if rings:
+        greet_axis(barrier, "tensor", lax.axis_index("tensor"), parts)
+    pl.semaphore_wait(barrier, peers - 1 + (parts - 1 if rings else 0))
+    for ring in rings:
+        ring.stage(1)
 
     def start_out(step, carry):
         peer = lax.rem(me + step, peers)
@@ -72,9 +263,21 @@
 
     lax.fori_loop(1, peers, start_out, 0)
     landed[me] = out_rows[me]
+    for distance in range(2, parts // 2 + 1):
+        for ring in rings[:1]:
+            ring.stage(distance)
+    for ring in rings[:1]:
+        ring.finish()
 
     def one_chunk(step, carry):
         peer = lax.rem(me + peers - step, peers)
+        if len(rings) > 1:
+
+            @pl.when(step == peers // 4)
+            def _():
+                for distance in range(2, parts // 2 + 1):
+                    for ring in rings[1:]:
+                        ring.stage(distance)
 
         @pl.when(step > 0)
         def _():
@@ -102,11 +305,27 @@
         return carry
 
     lax.fori_loop(1, peers, finish, 0)
-
-
-def forward_kernel(
-    peers, parts, rows_ref, win_ref, wout_ref, landed, back, results, total, *sems
-):
+    for ring in rings[1:]:
+        ring.finish()
+
+
+def forward_kernel(peers, parts, follow, *refs):
+    rows_ref, win_ref = refs[:2]
+    sources = refs[2 : 3 + follow]
+    landed, back = refs[3 + follow : 5 + follow]
+    targets = refs[5 + follow : 6 + 2 * follow]
+    results, total, *sems = refs[6 + 2 * follow :]
+    wout_ref = targets[0]
+    kinds = (1, 0)[: 1 + follow]
+    local_sem = sems[-1]
+    rings, copies = [], []
+    for order, kind in enumerate(kinds):
+        pair = (sources[order], targets[order])
+        rings.append(weight_ring(parts, kind, *pair, sems[4 + 2 * order], sems[5 + 2 * order]))
+        copies.append(own_weight(kind, *pair, local_sem.at[order]))
+    for copy in copies:
+        copy.start()
+    copies[0].wait()
     width = win_ref.shape[1] // parts
 
     def work(step, peer):
@@ -123,7 +342,11 @@
             else:
                 results[step] = (total[...] + term).astype(jnp.bfloat16)
 
-    exchange_chunks(peers, work, rows_ref, landed, results, back, sems)
+    exchange_chunks(
+        peers, work, rows_ref, landed, results, back, sems[:4], parts=parts, rings=rings
+    )
+    for copy in copies[1:]:
+        copy.wait()
 
 
 def backward_kernel(
@@ -209,7 +432,7 @@
         out_shape=jax.ShapeDtypeStruct(rows.shape[1:], jnp.float32),
         in_specs=whole_in_vmem(1),
         out_specs=whole_in_vmem(1)[0],
-        scratch_shapes=[pltpu.VMEM(rows.shape, rows.dtype)] + exchange_sems(peers)[:2],
+        scratch_shapes=[pltpu.VMEM(rows.shape, rows.dtype)] + [pltpu.SemaphoreType.DMA((peers,))] * 2,
         compiler_params=pltpu.CompilerParams(collective_id=2, has_side_effects=True),
     )(rows)
 
@@ -222,21 +445,28 @@
     return [pltpu.SemaphoreType.DMA((peers,)) for _ in range(4)]
 
 
-def experts_forward(rows, win, wout, parts):
+def experts_forward(rows, win, wout_part, parts, following=()):
     peers, capacity, width = rows.shape
     like = jax.ShapeDtypeStruct(rows.shape, jnp.bfloat16)
+    follow = len(following)
+    wholes = (jax.ShapeDtypeStruct(win.shape[::-1], win.dtype),)
+    wholes += (jax.ShapeDtypeStruct(win.shape, win.dtype),) * follow
     return pl.pallas_call(
-        functools.partial(forward_kernel, peers, parts),
-        out_shape=(like, like),
-        in_specs=whole_in_vmem(3),
-        out_specs=tuple(whole_in_vmem(2)),
+        functools.partial(forward_kernel, peers, parts, follow),
+        out_shape=(like, like) + wholes,
+        in_specs=whole_in_vmem(3 + follow),
+        out_specs=tuple(whole_in_vmem(3 + follow)),
         scratch_shapes=[
             pltpu.VMEM(rows.shape, jnp.bfloat16),
             pltpu.VMEM((capacity, width), jnp.float32),
         ]
-        + exchange_sems(peers),
-        compiler_params=pltpu.CompilerParams(collective_id=0, has_side_effects=True),
-    )(rows, win, wout)
+        + exchange_sems(peers)
+        + [pltpu.SemaphoreType.DMA((parts,))] * (2 + 2 * follow)
+        + [pltpu.SemaphoreType.DMA((2,))],
+        compiler_params=pltpu.CompilerParams(
+            collective_id=4 if follow else 0, has_side_effects=True
+        ),
+    )(rows, win, wout_part, *following)
 
 
 def experts_backward(rows, arrived, win, wout, parts):
@@ -475,9 +705,9 @@
     head_cols = attend_in.shape[3]
     layers = attend_in.shape[0]
     capacity = max(2, (10 * tokens + 4 * experts - 1) // (4 * experts))
+    peers_tensor = lax.axis_size("tensor")
     spacing = -(-capacity // 16) * 16
     slots_all = experts * spacing
-    peers_tensor = lax.axis_size("tensor")
     row_share = attend_in.shape[2]
     gain_share = norm_gains.shape[2]
     image_rows = -(-SEQ // 16) * 16
@@ -487,9 +717,6 @@
         shaped = rows.reshape((images, SEQ) + rows.shape[1:])
         edges = ((0, 0), (0, image_rows - SEQ)) + ((0, 0),) * (rows.ndim - 1)
         return jnp.pad(shaped, edges, constant_values=fill)
-
-    def gather_tensor(rows, axis):
-        return lax.all_gather(rows.astype(jnp.bfloat16), "tensor", axis=axis, tiled=True)
 
     smalls = jnp.concatenate([router.reshape(-1), norm_gains.reshape(-1)])
     block = row_share * head_cols
@@ -502,7 +729,13 @@
             smalls,
         ]
     )
-    whole = lax.all_gather(gather_tensor(packed, 2), "expert", axis=1, tiled=True)
+    whole, win_first = gather_start(
+        packed.astype(jnp.bfloat16),
+        expert_in[0, 0].astype(jnp.bfloat16),
+        experts,
+        peers_tensor,
+    )
+    whole = whole.reshape(whole.shape[0], model_width, model_width)
     small_rows = whole[4 * layers :, :, :head_cols].reshape(-1, experts, block)
     small_rows = small_rows.transpose(1, 0, 2).reshape(experts, -1)
     router_all = small_rows[:, : layers * model_width].reshape(experts, layers, model_width)
@@ -510,8 +743,7 @@
     gains_all = gains_all.reshape(experts, layers, 2, gain_share).transpose(1, 2, 0, 3)
     gains_all = gains_all.reshape(layers, 2, model_width).astype(jnp.float32)
     router_all = jnp.pad(router_all.transpose(1, 2, 0), ((0, 0), (0, 0), (0, -experts % 128)))
-    win_full = [gather_tensor(expert_in[layer_index, 0], 1) for layer_index in range(layers)]
-    wout_full = [gather_tensor(expert_out[layer_index, 0], 0) for layer_index in range(layers)]
+    win_full, wout_full = [win_first], []
     slot_ids = lax.broadcasted_iota(jnp.int32, (1, slots_all), 1)
     stream = spread(inputs, 0)
     stash_list = []
@@ -533,12 +765,18 @@
         pick_second = (target[:, 1:2] == slot_ids).astype(jnp.bfloat16)
         pick_both = pick_first + pick_second
         dispatched = contract_rows(pick_both, normed_two.reshape(tokens_all, model_width))
-        arrived, returned = experts_forward(
+        following = ()
+        if layer_index + 1 < layers:
+            following = (expert_in[layer_index + 1, 0].astype(jnp.bfloat16),)
+        arrived, returned, wout_now, *gathered = experts_forward(
             dispatched.astype(jnp.bfloat16).reshape(experts, spacing, model_width),
             win_full[layer_index],
-            wout_full[layer_index],
+            expert_out[layer_index, 0].astype(jnp.bfloat16),
             peers_tensor,
-        )
+            following,
+        )
+        win_full.extend(gathered)
+        wout_full.append(wout_now)
         returned = returned.reshape(slots_all, model_width)
         rows_first = jnp.dot(pick_first, returned, preferred_element_type=jnp.float32)
         rows_second = jnp.dot(pick_second, returned, preferred_element_type=jnp.float32)

time: 625 us -> 628 us (level)
  Pallas kernels: 371 us -> 492 us
  waiting for transfers between devices: 85.6 us -> 0 us
  blocking collectives: 16 us -> 0 us
  between operations: 14.6 us -> 1.53 us
    pallas_call x2 -> x3, Pallas kernels: 130 us -> 248 us  [the longest x2 194 us: experts_forward(): pl.pallas_call(functools.partial(forward_kernel, peers, parts, follow), o...]
    all_gather x5 -> x0, waiting for transfers between devices: 84.5 us -> none  [the longest x4 59.9 us: gather_tensor(): lax.all_gather(rows.astype(jnp.bfloat16), 'tensor', axis=axis, tiled=True)]
    all_gather x1 -> x0, blocking collectives: 16 us -> none  [gather_tensor(): lax.all_gather(rows.astype(jnp.bfloat16), 'tensor', axis=axis, tiled=True)]
    dot_general x6, matrix products: 41.2 us -> 34.7 us  [contract_rows(): lax.dot_general(left_side, right_side, (((0,), (0,)), ((), ())), preferre...]
  transfers between devices with their start and end apart: 5 -> 0, of which waited for: 3 -> 0; matrix products, arithmetic and copies ran while one was open for 8% -> 0% of each run, Pallas kernels for 15% -> 0%
where the time goes in v6:
time: 628 us; the launch traced here: 619 us
  Pallas kernels  492 us (78%)
  matrix products  74.7 us (12%)
  local copies, waits for them, and re-layouts  34.5 us (5%)
  other arithmetic  16 us (3%)
    pallas_call x2, Pallas kernels, experts_forward(): pl.pallas_call(functools.partial(forward_kernel, peers, parts, follow), o...  194 us
    pallas_call x2, Pallas kernels, experts_backward(): pl.pallas_call(functools.partial(backward_kernel, peers, parts), out_shap...  135 us
    pallas_call x2, Pallas kernels, attend_back(): pl.pallas_call(attend_back_kernel, grid=(images,), out_shape=(jax.ShapeDt...  58.9 us
    pallas_call x1, Pallas kernels, gather_start(): pl.pallas_call(functools.partial(gather_kernel, experts, parts), out_shap...  54.4 us
    dot_general x6, matrix products, contract_rows(): lax.dot_general(left_side, right_side, (((0,), (0,)), ((), ())), preferre...  34.7 us
    pallas_call x2, Pallas kernels, attend(): pl.pallas_call(functools.partial(attend_kernel, experts), grid=(images,),...  29.4 us
    pallas_call x1, Pallas kernels, sum_shares(): pl.pallas_call(functools.partial(sum_kernel, peers), out_shape=jax.ShapeD...  20.9 us
    dot_general x2, matrix products, local(): jnp.dot(pick_both, grad_dispatched, preferred_element_type=jnp.float32)  13.7 us

profile of v6, /device:TPU:1, one launch (start us, length us, event | category | flops | bytes accessed | tf_op | source)
XLA Modules:
  0.0 618.6 jit_solution(8205049287731941837)
XLA Ops:
  8.2 54.4 %shard_map.161 = (bf16[9,8,64,512]{3,2,1,0:T(8,128)(2,1)}, bf16[512,2048]{1,0:T(8,128)(2,1)}) custom-call(bf16[9,64,128]{2,1,0:T(8,128)(2,1)} %pad_maximum_fusion.2.small_ref, bf16[512,512]{1,0:T(8,128)(2,1)} %get-tuple-element.129.win_ref), custom_call_target="tpu_custom_call" | custom-call | tf_op jit(solution)/shard_map/pallas_call | solution.py:233
  62.6 4.7 fusion.134
  70.0 14.4 %shard_map.162 = (f32[5,208,512]{2,1,0:T(8,128)}, bf16[5,208,512]{2,1,0:T(8,128)(2,1)}, f32[5,208,128]{2,1,0:T(8,128)}, bf16[5,208,512]{2,1,0:T(8,128)(2,1)}) custom-call(f32[5,208,512]{2,1,0:T(8,128)} %pad.46.stream_ref, bf16[4,512,512]{2,1,0:T(8,128)(2,1)} %bitcast.135, f32[2,512]{1,0:T(2,128)} %squeeze.8.gains_ref, ...), custom_call_target="tpu_custom_call" | custom-call | tf_op jit(solution)/shard_map/pallas_call | solution.py:641
  88.2 6.4 %fusion.61 = bf16[2560,512]{1,0:T(8,128)(2,1)} fusion(bf16[1040,512]{1,0:T(8,128)(2,1)S(1)} %bitcast.184, s32[1040]{0:T(1024)S(1)} %get-tuple-element.102, s32[1040]{0:T(1024)S(1)} %get-tuple-element.101), kind=kOutput, calls=%fused_computation.61 | convolution fusion | flops 2748907520 | bytes 3694720 | tf_op jit(solution)/shard_map/dot_general | solution.py:19
  94.5 112.3 %shard_map.163 = (bf16[8,320,512]{2,1,0:T(8,128)(2,1)}, bf16[8,320,512]{2,1,0:T(8,128)(2,1)}, bf16[2048,512]{1,0:T(8,128)(2,1)}, bf16[512,2048]{1,0:T(8,128)(2,1)}) custom-call(bf16[8,320,512]{2,1,0:T(8,128)(2,1)} %bitcast.151, bf16[512,2048]{1,0:T(8,128)(2,1)} %get-tuple-element.43.refs_1_.win_ref, bf16[512,512]{1,0:T(8,128)(2,1)} %get-tuple-element.111.refs_2_, ...), custom_call_target="tpu_custom_call" | custom-call | tf_op jit(solution)/shard_map/pallas_call | solution.py:454
  206.9 4.8 fusion.10
  211.8 4.8 fusion.91
  217.2 14.9 %shard_map.164 = (f32[5,208,512]{2,1,0:T(8,128)}, bf16[5,208,512]{2,1,0:T(8,128)(2,1)}, f32[5,208,128]{2,1,0:T(8,128)}, bf16[5,208,512]{2,1,0:T(8,128)(2,1)}) custom-call(f32[5,208,512]{2,1,0:T(8,128)} %bitcast.139, bf16[4,512,512]{2,1,0:T(8,128)(2,1)} %bitcast.137, f32[2,512]{1,0:T(2,128)} %squeeze.20.gains_ref, bf16[512,128]{1,0:T(8,128)(2,1)} %get-tuple-element.120.router_ref), custom_call_target="tpu_custom_call" | custom-call | tf_op jit(solution)/shard_map/pallas_call | solution.py:641
  234.6 6.4 %fusion.58 = bf16[2560,512]{1,0:T(8,128)(2,1)} fusion(bf16[1040,512]{1,0:T(8,128)(2,1)S(1)} %bitcast.185, s32[1040]{0:T(1024)S(1)} %get-tuple-element.98, s32[1040]{0:T(1024)S(1)} %get-tuple-element.97), kind=kOutput, calls=%fused_computation.60 | convolution fusion | flops 2748907520 | bytes 3694720 | tf_op jit(solution)/shard_map/dot_general | solution.py:19
  241.0 81.3 %shard_map.165 = (bf16[8,320,512]{2,1,0:T(8,128)(2,1)}, bf16[8,320,512]{2,1,0:T(8,128)(2,1)}, bf16[2048,512]{1,0:T(8,128)(2,1)}) custom-call(bf16[8,320,512]{2,1,0:T(8,128)(2,1)} %bitcast.152, bf16[512,2048]{1,0:T(8,128)(2,1)} %get-tuple-element.48.refs_1_.win_ref, bf16[512,512]{1,0:T(8,128)(2,1)} %get-tuple-element.110.refs_2_), custom_call_target="tpu_custom_call" | custom-call | tf_op jit(solution)/shard_map/pallas_call | solution.py:454
  322.4 6.3 %fusion.1 = f32[1040,512]{1,0:T(8,128)} fusion(bf16[2560,512]{1,0:T(8,128)(2,1)} %bitcast.178, s32[1040]{0:T(1024)S(1)} %get-tuple-element.98), kind=kOutput, calls=%fused_computation.6 | convolution fusion | flops 2728960000 | bytes 4755520 | tf_op jit(solution)/shard_map/dot_general | solution.py:782
  332.5 6.8 %multiply_reduce_fusion.3 = (f32[1040]{0:T(1024)S(1)}, f32[1040]{0:T(1024)S(1)}, f32[1040,512]{1,0:T(8,128)}) fusion(f32[1040,512]{1,0:T(8,128)S(1)} %bitcast.141, f32[1040,512]{1,0:T(8,128)S(1)} %copy-done.6, bf16[2560,512]{1,0:T(8,128)(2,1)} %bitcast.179, s32[1040]{0:T(1024)S(1)} %get-tuple-element.97), kind=kOutput, calls=%fused_computation.85 | convolution fusion | flops 2731087872 | bytes 9023680 | tf_op jit(solution)/shard_map/dot_general | solution.py:781
  339.5 3.3 fusion.90
  347.4 4.0 fusion
  351.4 6.2 %add_convert_fusion.1 = bf16[2560,512]{1,0:T(8,128)(2,1)} fusion(f32[2560,512]{1,0:T(8,128)S(1)} %fusion, s32[1040]{0:T(1024)S(1)} %get-tuple-element.97, f32[1040,512]{1,0:T(8,128)S(1)} %bitcast.143, f32[1040]{0:T(1024)S(1)} %get-tuple-element.94), kind=kOutput, calls=%fused_computation.59 | convolution fusion | flops 2732646400 | bytes 10002560 | tf_op jit(solution)/shard_map/dot_general | solution.py:19
  357.6 66.2 %shard_map.166 = (bf16[8,320,512]{2,1,0:T(8,128)(2,1)}, f32[512,512]{1,0:T(8,128)}, f32[512,512]{1,0:T(8,128)}) custom-call(bf16[8,320,512]{2,1,0:T(8,128)(2,1)} %bitcast.149, bf16[8,320,512]{2,1,0:T(8,128)(2,1)} %get-tuple-element.50.arrived_ref, bf16[512,2048]{1,0:T(8,128)(2,1)} %get-tuple-element.48.refs_1_.win_ref, ...), custom_call_target="tpu_custom_call" | custom-call | tf_op jit(solution)/shard_map/pallas_call | solution.py:475
  424.0 6.7 %fusion.31.grad_ref = f32[5,208,512]{2,1,0:T(8,128)} fusion(bf16[2560,512,1]{1,0,2:T(8,128)(2,1)} %bitcast.182, s32[5,208]{1,0:T(8,128)S(1)} %eq.244, s32[5,208]{1,0:T(8,128)S(1)} %eq.240), kind=kOutput, calls=%fused_computation.37 | convolution fusion | flops 2747596800 | bytes 4759680 | tf_op jit(solution)/shard_map/dot_general | solution.py:848
  431.6 29.6 %shard_map.167 = (f32[5,208,512]{2,1,0:T(8,128)}, f32[4,512,128]{2,1,0:T(8,128)}, f32[128,512]{1,0:T(8,128)}, f32[2,512]{1,0:T(2,128)}) custom-call(s32[1]{0:T(128)} %bitcast.29.own_ref, f32[5,208,512]{2,1,0:T(8,128)} %copy-done, f32[5,208,512]{2,1,0:T(8,128)} %fusion.31.grad_ref, bf16[5,208,128]{2,1,0:T(8,128)(2,1)} %bitcast.158, f32[5,208,512]{2,1,0:T(8,128)} %bitcast.140, ...), custom_call_target="tpu_custom_call" | custom-call | tf_op jit(solution)/shard_map/pallas_call | solution.py:660
  461.3 5.7 fusion.6
  467.0 6.0 add_convert_fusion
  473.0 68.5 %shard_map.168 = (bf16[8,320,512]{2,1,0:T(8,128)(2,1)}, f32[512,512]{1,0:T(8,128)}, f32[512,512]{1,0:T(8,128)}) custom-call(bf16[8,320,512]{2,1,0:T(8,128)(2,1)} %bitcast.150, bf16[8,320,512]{2,1,0:T(8,128)(2,1)} %get-tuple-element.55.arrived_ref, bf16[512,2048]{1,0:T(8,128)(2,1)} %get-tuple-element.43.refs_1_.win_ref, ...), custom_call_target="tpu_custom_call" | custom-call | tf_op jit(solution)/shard_map/pallas_call | solution.py:475
  541.6 7.0 %fusion.26.grad_ref = f32[5,208,512]{2,1,0:T(8,128)} fusion(bf16[2560,512,1]{1,0,2:T(8,128)(2,1)} %bitcast.183, s32[5,208]{1,0:T(8,128)S(1)} %eq.252, s32[5,208]{1,0:T(8,128)S(1)} %eq.248), kind=kOutput, calls=%fused_computation.34 | convolution fusion | flops 2747596800 | bytes 4759680 | tf_op jit(solution)/shard_map/dot_general | solution.py:848
  550.2 29.3 %shard_map.169 = (f32[5,208,512]{2,1,0:T(8,128)}, f32[4,512,128]{2,1,0:T(8,128)}, f32[128,512]{1,0:T(8,128)}, f32[2,512]{1,0:T(2,128)}) custom-call(s32[1]{0:T(128)} %bitcast.29.own_ref, f32[5,208,512]{2,1,0:T(8,128)} %get-tuple-element.54.upstream_ref, f32[5,208,512]{2,1,0:T(8,128)} %fusion.26.grad_ref, bf16[5,208,128]{2,1,0:T(8,128)(2,1)} %bitcast.157, ...), custom_call_target="tpu_custom_call" | custom-call | tf_op jit(solution)/shard_map/pallas_call | solution.py:660
  587.2 20.9 %shard_map.170 = f32[544,128]{1,0:T(8,128)} custom-call(bf16[8,544,128]{2,1,0:T(8,128)(2,1)} %pad_maximum_fusion.rows_ref), custom_call_target="tpu_custom_call" | custom-call | tf_op jit(solution)/shard_map/pallas_call | solution.py:430
  (157 shorter events, 46.2 us)
Async XLA Ops:
  2.4 1.6 copy-start.21
  2.5 1.7 copy-start.18
  2.5 1.7 copy-start.15
  2.5 1.7 copy-start.14
  4.0 2.6 copy-start.7
  68.4 16.0 %copy-start.17 = (s32[2,985]{1,0:T(2,128)S(1)}, s32[2,985]{1,0:T(2,128)}, u32[]{:S(2)}) copy-start(s32[2,985]{1,0:T(2,128)} %param.13) | copy-start | bytes 23644
  69.1 15.6 %copy-start.16 = (s32[2,985,2]{1,2,0:T(2,128)S(1)}, s32[2,985,2]{1,2,0:T(2,128)}, u32[]{:S(2)}) copy-start(s32[2,985,2]{1,2,0:T(2,128)} %param.12) | copy-start | bytes 47284
  84.4 3.8 copy-start.23
  206.9 4.9 copy-start.5
  206.9 4.9 copy-start.22
  211.7 4.8 copy-start.2
  232.2 2.5 copy-start.24
  322.4 6.3 %copy-start.8 = (f32[985,512]{1,0:T(8,128)S(1)}, f32[985,512]{1,0:T(8,128)}, u32[]{:S(2)}) copy-start(f32[985,512]{1,0:T(8,128)} %param.11) | copy-start | bytes 6051844
  330.2 2.2 copy-start.6
  332.2 19.2 %copy-start = (f32[5,208,512]{2,1,0:T(8,128)}, f32[5,208,512]{2,1,0:T(8,128)S(1)}, u32[]{:S(2)}) copy-start(f32[5,208,512]{2,1,0:T(8,128)S(1)} %pad.53.upstream_ref) | copy-start | bytes 6389764
  332.4 6.8 %copy-start.13 = (f32[5,208,128]{2,1,0:T(8,128)S(1)}, f32[5,208,128]{2,1,0:T(8,128)}, u32[]{:S(2)}) copy-start(f32[5,208,128]{2,1,0:T(8,128)} %get-tuple-element.46) | copy-start | bytes 1597444
  461.3 5.8 copy-start.1
  541.6 7.0 %copy-start.3 = (f32[1040,512]{1,0:T(8,128)S(1)}, f32[1040,512]{1,0:T(8,128)}, u32[]{:S(2)}) copy-start(f32[1040,512]{1,0:T(8,128)} %copy-done.2) | copy-start | bytes 6389764
  541.6 7.0 %copy-start.4 = (f32[1040,512]{1,0:T(8,128)S(1)}, f32[1040,512]{1,0:T(8,128)}, u32[]{:S(2)}) copy-start(f32[1040,512]{1,0:T(8,128)} %get-tuple-element.127) | copy-start | bytes 6389764
  581.2 3.8 copy-start.19
  581.2 4.8 copy-start.9
  586.1 28.0 %copy-start.11 = (f32[512,512]{1,0:T(8,128)S(1)}, f32[512,512]{1,0:T(8,128)}, u32[]{:S(2)}) copy-start(f32[512,512]{1,0:T(8,128)} %get-tuple-element.67) | copy-start | bytes 3145732
  608.2 8.7 %copy-start.10 = (f32[512,512]{1,0:T(8,128)S(1)}, f32[512,512]{1,0:T(8,128)}, u32[]{:S(2)}) copy-start(f32[512,512]{1,0:T(8,128)} %get-tuple-element.69) | copy-start | bytes 3145732
  608.2 8.7 %copy-start.12 = (f32[512,512]{1,0:T(8,128)S(1)}, f32[512,512]{1,0:T(8,128)}, u32[]{:S(2)}) copy-start(f32[512,512]{1,0:T(8,128)} %get-tuple-element.68) | copy-start | bytes 3145732
  (1 other events, 1.6 us)

commit v7 on v6

--- a/solution.py
+++ b/solution.py
@@ -245,7 +245,9 @@
     )(small, win)
 
 
-def exchange_chunks(peers, work, out_rows, landed, results, back, sems, parts=1, rings=()):
+def exchange_chunks(
+    peers, make_rows, work, take_rows, out_rows, landed, results, back, sems, parts=1, rings=()
+):
     out_send, out_recv, back_send, back_recv = sems
     me = lax.axis_index("expert")
     barrier = pltpu.get_barrier_semaphore()
@@ -253,31 +255,36 @@
     if rings:
         greet_axis(barrier, "tensor", lax.axis_index("tensor"), parts)
     pl.semaphore_wait(barrier, peers - 1 + (parts - 1 if rings else 0))
-    for ring in rings:
+    for ring in rings[:1]:
         ring.stage(1)
 
-    def start_out(step, carry):
+    def start_out(step):
         peer = lax.rem(me + step, peers)
         send_chunk(out_rows.at[peer], landed.at[me], out_send, out_recv, step, peer).start()
+
+    def make_out(step, carry):
+        peer = lax.rem(me + step, peers)
+        out_rows[peer] = make_rows(peer)
+
+        @pl.when(step > 1)
+        def _():
+            start_out(step - 1)
+
         return carry
 
-    lax.fori_loop(1, peers, start_out, 0)
-    landed[me] = out_rows[me]
+    lax.fori_loop(1, peers, make_out, 0)
+    landed[me] = make_rows(me)
+    start_out(peers - 1)
     for distance in range(2, parts // 2 + 1):
         for ring in rings[:1]:
             ring.stage(distance)
     for ring in rings[:1]:
         ring.finish()
+    for ring in rings[1:]:
+        ring.stage(1)
 
     def one_chunk(step, carry):
         peer = lax.rem(me + peers - step, peers)
-        if len(rings) > 1:
-
-            @pl.when(step == peers // 4)
-            def _():
-                for distance in range(2, parts // 2 + 1):
-                    for ring in rings[1:]:
-                        ring.stage(distance)
 
         @pl.when(step > 0)
         def _():
@@ -294,14 +301,19 @@
         return carry
 
     lax.fori_loop(0, peers, one_chunk, 0)
+    for distance in range(2, parts // 2 + 1):
+        for ring in rings[1:]:
+            ring.stage(distance)
     back[me] = results[0]
+    take_rows(me)
 
     def finish(step, carry):
         ahead = lax.rem(me + step, peers)
+        last = send_chunk(results.at[step], back.at[ahead], back_send, back_recv, step, ahead)
+        last.wait_recv()
+        take_rows(ahead)
         send_chunk(out_rows.at[ahead], landed.at[me], out_send, out_recv, step, ahead).wait_send()
-        last = send_chunk(results.at[step], back.at[ahead], back_send, back_recv, step, ahead)
         last.wait_send()
-        last.wait_recv()
         return carry
 
     lax.fori_loop(1, peers, finish, 0)
@@ -309,13 +321,23 @@
         ring.finish()
 
 
+def slot_hits(slots, start, shape, axis):
+    return slots == start + lax.broadcasted_iota(jnp.int32, shape, axis)
+
+
+def one_hot(hits):
+    return jnp.where(hits, 1.0, 0.0).astype(jnp.bfloat16)
+
+
 def forward_kernel(peers, parts, follow, *refs):
-    rows_ref, win_ref = refs[:2]
-    sources = refs[2 : 3 + follow]
-    landed, back = refs[3 + follow : 5 + follow]
-    targets = refs[5 + follow : 6 + 2 * follow]
-    results, total, *sems = refs[6 + 2 * follow :]
+    rows_ref, across_ref, down_ref, win_ref = refs[:4]
+    sources = refs[4 : 5 + follow]
+    landed, first, second = refs[5 + follow : 8 + follow]
+    targets = refs[8 + follow : 9 + 2 * follow]
+    out_rows, back, results, total, *sems = refs[9 + 2 * follow :]
     wout_ref = targets[0]
+    spacing = landed.shape[1]
+    tokens = rows_ref.shape[0]
     kinds = (1, 0)[: 1 + follow]
     local_sem = sems[-1]
     rings, copies = [], []
@@ -327,6 +349,15 @@
         copy.start()
     copies[0].wait()
     width = win_ref.shape[1] // parts
+    first[...] = jnp.zeros_like(first)
+    second[...] = jnp.zeros_like(second)
+
+    def make_rows(peer):
+        shape = (spacing, tokens)
+        hits = [slot_hits(across_ref[k : k + 1], peer * spacing, shape, 0) for k in range(2)]
+        return jnp.dot(
+            one_hot(hits[0] | hits[1]), rows_ref[...], preferred_element_type=jnp.float32
+        ).astype(jnp.bfloat16)
 
     def work(step, peer):
         chunk = landed[peer]
@@ -342,8 +373,26 @@
             else:
                 results[step] = (total[...] + term).astype(jnp.bfloat16)
 
+    def take_rows(slab):
+        rows_back = back[slab]
+        for k, kept in enumerate((first, second)):
+            hits = slot_hits(down_ref[:, k : k + 1], slab * spacing, (tokens, spacing), 1)
+            kept[...] += jnp.dot(
+                one_hot(hits), rows_back, preferred_element_type=jnp.float32
+            ).astype(jnp.bfloat16)
+
     exchange_chunks(
-        peers, work, rows_ref, landed, results, back, sems[:4], parts=parts, rings=rings
+        peers,
+        make_rows,
+        work,
+        take_rows,
+        out_rows,
+        landed,
+        results,
+        back,
+        sems[:4],
+        parts=parts,
+        rings=rings,
     )
     for copy in copies[1:]:
         copy.wait()
@@ -352,14 +401,19 @@
 def backward_kernel(
     peers,
     parts,
-    rows_ref,
+    first_ref,
+    second_ref,
+    across_ref,
+    down_ref,
     arrived_ref,
     win_ref,
     wout_ref,
-    back,
+    token_grad,
     win_grad,
     wout_grad,
+    out_rows,
     landed,
+    back,
     results,
     total,
     hidden_all,
@@ -367,9 +421,19 @@
     *sems,
 ):
     width = win_ref.shape[1] // parts
+    spacing = landed.shape[1]
+    tokens = first_ref.shape[0]
     own = lax.axis_index("tensor") * width
     win_grad[...] = jnp.zeros_like(win_grad)
     wout_grad[...] = jnp.zeros_like(wout_grad)
+    token_grad[...] = jnp.zeros_like(token_grad)
+
+    def make_rows(peer):
+        made = 0.0
+        for k, rows_ref in enumerate((first_ref, second_ref)):
+            hits = slot_hits(across_ref[k : k + 1], peer * spacing, (spacing, tokens), 0)
+            made += jnp.dot(one_hot(hits), rows_ref[...], preferred_element_type=jnp.float32)
+        return made.astype(jnp.bfloat16)
 
     def work(step, peer):
         chunk = arrived_ref[peer]
@@ -393,7 +457,14 @@
         wout_grad[...] += contract_rows(hidden_all[:, mine], grad_chunk)
         win_grad[...] += contract_rows(chunk, before_all[:, mine])
 
-    exchange_chunks(peers, work, rows_ref, landed, results, back, sems)
+    def take_rows(slab):
+        shape = (tokens, spacing)
+        hits = [slot_hits(down_ref[:, k : k + 1], slab * spacing, shape, 1) for k in range(2)]
+        token_grad[...] += jnp.dot(
+            one_hot(hits[0] | hits[1]), back[slab], preferred_element_type=jnp.float32
+        )
+
+    exchange_chunks(peers, make_rows, work, take_rows, out_rows, landed, results, back, sems)
 
 
 def sum_kernel(peers, rows_ref, sum_ref, landed, sends, arrivals):
@@ -445,52 +516,49 @@
     return [pltpu.SemaphoreType.DMA((peers,)) for _ in range(4)]
 
 
-def experts_forward(rows, win, wout_part, parts, following=()):
-    peers, capacity, width = rows.shape
-    like = jax.ShapeDtypeStruct(rows.shape, jnp.bfloat16)
+def experts_forward(rows, slots, peers, spacing, win, wout_part, parts, following=()):
+    tokens, width = rows.shape
+    chunks = (peers, spacing, width)
     follow = len(following)
     wholes = (jax.ShapeDtypeStruct(win.shape[::-1], win.dtype),)
     wholes += (jax.ShapeDtypeStruct(win.shape, win.dtype),) * follow
+    outs = tuple(
+        jax.ShapeDtypeStruct(shape, jnp.bfloat16) for shape in (chunks, rows.shape, rows.shape)
+    )
     return pl.pallas_call(
         functools.partial(forward_kernel, peers, parts, follow),
-        out_shape=(like, like) + wholes,
-        in_specs=whole_in_vmem(3 + follow),
-        out_specs=tuple(whole_in_vmem(3 + follow)),
-        scratch_shapes=[
-            pltpu.VMEM(rows.shape, jnp.bfloat16),
-            pltpu.VMEM((capacity, width), jnp.float32),
-        ]
+        out_shape=outs + wholes,
+        in_specs=whole_in_vmem(5 + follow),
+        out_specs=tuple(whole_in_vmem(4 + follow)),
+        scratch_shapes=[pltpu.VMEM(chunks, jnp.bfloat16)] * 3
+        + [pltpu.VMEM((spacing, width), jnp.float32)]
         + exchange_sems(peers)
         + [pltpu.SemaphoreType.DMA((parts,))] * (2 + 2 * follow)
         + [pltpu.SemaphoreType.DMA((2,))],
         compiler_params=pltpu.CompilerParams(
             collective_id=4 if follow else 0, has_side_effects=True
         ),
-    )(rows, win, wout_part, *following)
-
-
-def experts_backward(rows, arrived, win, wout, parts):
-    peers, capacity, width = rows.shape
+    )(rows, slots.T, slots, win, wout_part, *following)
+
+
+def experts_backward(first, second, slots, arrived, win, wout, parts):
+    peers, spacing, width = arrived.shape
     inner = win.shape[1]
     return pl.pallas_call(
         functools.partial(backward_kernel, peers, parts),
         out_shape=(
-            jax.ShapeDtypeStruct(rows.shape, jnp.bfloat16),
+            jax.ShapeDtypeStruct(first.shape, jnp.float32),
             jax.ShapeDtypeStruct((width, inner // parts), jnp.float32),
             jax.ShapeDtypeStruct((inner // parts, width), jnp.float32),
         ),
-        in_specs=whole_in_vmem(4),
+        in_specs=whole_in_vmem(7),
         out_specs=tuple(whole_in_vmem(3)),
-        scratch_shapes=[
-            pltpu.VMEM(rows.shape, jnp.bfloat16),
-            pltpu.VMEM(rows.shape, jnp.bfloat16),
-            pltpu.VMEM((capacity, width), jnp.float32),
-            pltpu.VMEM((capacity, inner), jnp.bfloat16),
-            pltpu.VMEM((capacity, inner), jnp.bfloat16),
-        ]
+        scratch_shapes=[pltpu.VMEM(arrived.shape, jnp.bfloat16)] * 4
+        + [pltpu.VMEM((spacing, width), jnp.float32)]
+        + [pltpu.VMEM((spacing, inner), jnp.bfloat16)] * 2
         + exchange_sems(peers),
         compiler_params=pltpu.CompilerParams(collective_id=1, has_side_effects=True),
-    )(rows, arrived, win, wout)
+    )(first, second, slots.T, slots, arrived, win, wout)
 
 
 def norm_parts(rows_in):
@@ -707,7 +775,6 @@
     capacity = max(2, (10 * tokens + 4 * experts - 1) // (4 * experts))
     peers_tensor = lax.axis_size("tensor")
     spacing = -(-capacity // 16) * 16
-    slots_all = experts * spacing
     row_share = attend_in.shape[2]
     gain_share = norm_gains.shape[2]
     image_rows = -(-SEQ // 16) * 16
@@ -744,7 +811,6 @@
     gains_all = gains_all.reshape(layers, 2, model_width).astype(jnp.float32)
     router_all = jnp.pad(router_all.transpose(1, 2, 0), ((0, 0), (0, 0), (0, -experts % 128)))
     win_full, wout_full = [win_first], []
-    slot_ids = lax.broadcasted_iota(jnp.int32, (1, slots_all), 1)
     stream = spread(inputs, 0)
     stash_list = []
     for layer_index in range(layers):
@@ -761,15 +827,14 @@
         gate_values = jnp.stack(
             [jnp.sum(probs_all * first_f, axis=1), jnp.sum(probs_all * second_f, axis=1)], axis=1
         )
-        pick_first = (target[:, 0:1] == slot_ids).astype(jnp.bfloat16)
-        pick_second = (target[:, 1:2] == slot_ids).astype(jnp.bfloat16)
-        pick_both = pick_first + pick_second
-        dispatched = contract_rows(pick_both, normed_two.reshape(tokens_all, model_width))
         following = ()
         if layer_index + 1 < layers:
             following = (expert_in[layer_index + 1, 0].astype(jnp.bfloat16),)
-        arrived, returned, wout_now, *gathered = experts_forward(
-            dispatched.astype(jnp.bfloat16).reshape(experts, spacing, model_width),
+        arrived, rows_first, rows_second, wout_now, *gathered = experts_forward(
+            normed_two.reshape(tokens_all, model_width),
+            target,
+            experts,
+            spacing,
             win_full[layer_index],
             expert_out[layer_index, 0].astype(jnp.bfloat16),
             peers_tensor,
@@ -777,9 +842,8 @@
         )
         win_full.extend(gathered)
         wout_full.append(wout_now)
-        returned = returned.reshape(slots_all, model_width)
-        rows_first = jnp.dot(pick_first, returned, preferred_element_type=jnp.float32)
-        rows_second = jnp.dot(pick_second, returned, preferred_element_type=jnp.float32)
+        rows_first = rows_first.astype(jnp.float32)
+        rows_second = rows_second.astype(jnp.float32)
         output = (
             middle.reshape(tokens_all, model_width)
             + gate_values[:, 0:1] * rows_first
@@ -797,9 +861,7 @@
                 gate_values,
                 first_f,
                 second_f,
-                pick_first,
-                pick_second,
-                pick_both,
+                target,
                 arrived,
                 rows_first,
                 rows_second,
@@ -821,9 +883,7 @@
             gate_values,
             first_f,
             second_f,
-            pick_first,
-            pick_second,
-            pick_both,
+            target,
             arrived,
             rows_first,
             rows_second,
@@ -832,11 +892,10 @@
         gate_second = jnp.sum(upstream * rows_second, axis=1)
         scaled_first = (gate_values[:, 0:1] * upstream).astype(jnp.bfloat16)
         scaled_second = (gate_values[:, 1:2] * upstream).astype(jnp.bfloat16)
-        grad_slots = (
-            contract_rows(pick_first, scaled_first) + contract_rows(pick_second, scaled_second)
-        ).astype(jnp.bfloat16)
-        grad_dispatched, win_grad, wout_grad = experts_backward(
-            grad_slots.reshape(experts, spacing, model_width),
+        grad_normed, win_grad, wout_grad = experts_backward(
+            scaled_first,
+            scaled_second,
+            target,
             arrived,
             win_full[layer_index],
             wout_full[layer_index],
@@ -844,8 +903,6 @@
         )
         grads_win.append(win_grad)
         grads_wout.append(wout_grad)
-        grad_dispatched = grad_dispatched.reshape(slots_all, model_width)
-        grad_normed = jnp.dot(pick_both, grad_dispatched, preferred_element_type=jnp.float32)
         grad_probs = first_f * gate_first[:, None] + second_f * gate_second[:, None]
         grad_logits = (
             probs_all * (grad_probs - jnp.sum(probs_all * grad_probs, axis=1, keepdims=True))

time: 628 us -> 569 us (0.906)
  matrix products: 74.7 us -> 3.69 us
  other arithmetic: 16 us -> 24.9 us
    dot_general x12 -> x0, matrix products: 71 us -> none  [the longest x6 34.7 us: contract_rows(): lax.dot_general(left_side, right_side, (((0,), (0,)), ((), ())), preferre...]
    pallas_call x2, Pallas kernels: 135 us -> 151 us  [experts_backward(): pl.pallas_call(functools.partial(backward_kernel, peers, parts), out_shap...]
    pallas_call x2, Pallas kernels: 194 us -> 179 us  [experts_forward(): pl.pallas_call(functools.partial(forward_kernel, peers, parts, follow), o...]
where the time goes in v7:
time: 569 us; the launch traced here: 559 us
  Pallas kernels  493 us (87%)
  local copies, waits for them, and re-layouts  36.2 us (6%)
  other arithmetic  24.9 us (4%)
    pallas_call x2, Pallas kernels, experts_forward(): pl.pallas_call(functools.partial(forward_kernel, peers, parts, follow), o...  179 us
    pallas_call x2, Pallas kernels, experts_backward(): pl.pallas_call(functools.partial(backward_kernel, peers, parts), out_shap...  151 us
    pallas_call x2, Pallas kernels, attend_back(): pl.pallas_call(attend_back_kernel, grid=(images,), out_shape=(jax.ShapeDt...  58.5 us
    pallas_call x1, Pallas kernels, gather_start(): pl.pallas_call(functools.partial(gather_kernel, experts, parts), out_shap...  54.5 us
    pallas_call x2, Pallas kernels, attend(): pl.pallas_call(functools.partial(attend_kernel, experts), grid=(images,),...  29.4 us
    pallas_call x1, Pallas kernels, sum_shares(): pl.pallas_call(functools.partial(sum_kernel, peers), out_shape=jax.ShapeD...  20.3 us

profile of v7, /device:TPU:1, one launch (start us, length us, event | category | flops | bytes accessed | tf_op | source)
XLA Modules:
  0.0 559.1 jit_solution(18341829474446632490)
XLA Ops:
  0.6 1.8 reshape.193
  2.5 1.6 pad.46.stream_ref
  5.0 1.7 convert.77
  8.3 54.5 %shard_map.161 = (bf16[9,8,64,512]{3,2,1,0:T(8,128)(2,1)}, bf16[512,2048]{1,0:T(8,128)(2,1)}) custom-call(bf16[9,64,128]{2,1,0:T(8,128)(2,1)} %pad_maximum_fusion.2.small_ref, bf16[512,512]{1,0:T(8,128)(2,1)} %get-tuple-element.147.win_ref), custom_call_target="tpu_custom_call" | custom-call | tf_op jit(solution)/shard_map/pallas_call | solution.py:233
  62.7 4.7 fusion.80
  70.2 14.5 %shard_map.162 = (f32[5,208,512]{2,1,0:T(8,128)}, bf16[5,208,512]{2,1,0:T(8,128)(2,1)}, f32[5,208,128]{2,1,0:T(8,128)}, bf16[5,208,512]{2,1,0:T(8,128)(2,1)}) custom-call(f32[5,208,512]{2,1,0:T(8,128)} %pad.46.stream_ref, bf16[4,512,512]{2,1,0:T(8,128)(2,1)} %bitcast.117, f32[2,512]{1,0:T(2,128)} %squeeze.8.gains_ref, ...), custom_call_target="tpu_custom_call" | custom-call | tf_op jit(solution)/shard_map/pallas_call | solution.py:709
  89.5 92.1 %shard_map.163 = (bf16[8,320,512]{2,1,0:T(8,128)(2,1)}, bf16[1040,512]{1,0:T(8,128)(2,1)}, bf16[1040,512]{1,0:T(8,128)(2,1)}, bf16[2048,512]{1,0:T(8,128)(2,1)}, bf16[512,2048]{1,0:T(8,128)(2,1)}) custom-call(bf16[1040,512]{1,0:T(8,128)(2,1)} %bitcast.136, s32[2,1040]{1,0:T(2,128)} %copy.91.refs_1_.across_ref, s32[1040,2]{1,0:T(8,128)} %copy-done.3, ...), custom_call_target="tpu_custom_call" | custom-call | tf_op jit(solution)/shard_map/pallas_call | solution.py:528
  181.6 3.4 fusion.35
  185.7 14.9 %shard_map.164 = (f32[5,208,512]{2,1,0:T(8,128)}, bf16[5,208,512]{2,1,0:T(8,128)(2,1)}, f32[5,208,128]{2,1,0:T(8,128)}, bf16[5,208,512]{2,1,0:T(8,128)(2,1)}) custom-call(f32[5,208,512]{2,1,0:T(8,128)} %bitcast.114, bf16[4,512,512]{2,1,0:T(8,128)(2,1)} %bitcast.119, f32[2,512]{1,0:T(2,128)} %squeeze.20.gains_ref, bf16[512,128]{1,0:T(8,128)(2,1)} %get-tuple-element.140.router_ref), custom_call_target="tpu_custom_call" | custom-call | tf_op jit(solution)/shard_map/pallas_call | solution.py:709
  201.8 1.6 reshape.212
  203.4 1.8 pad.53.upstream_ref
  211.6 86.5 %shard_map.165 = (bf16[8,320,512]{2,1,0:T(8,128)(2,1)}, bf16[1040,512]{1,0:T(8,128)(2,1)}, bf16[1040,512]{1,0:T(8,128)(2,1)}, bf16[2048,512]{1,0:T(8,128)(2,1)}) custom-call(bf16[1040,512]{1,0:T(8,128)(2,1)} %bitcast.135, s32[2,1040]{1,0:T(2,128)} %copy.96.refs_1_.across_ref, s32[1040,2]{1,0:T(8,128)} %copy-done.2, ...), custom_call_target="tpu_custom_call" | custom-call | tf_op jit(solution)/shard_map/pallas_call | solution.py:528
  298.1 2.2 fusion.40
  300.9 2.0 multiply_convert_fusion.2
  303.1 1.5 reshape.210
  304.6 76.1 %shard_map.166 = (f32[1040,512]{1,0:T(8,128)}, f32[512,512]{1,0:T(8,128)}, f32[512,512]{1,0:T(8,128)}) custom-call(bf16[1040,512]{1,0:T(8,128)(2,1)} %get-tuple-element.129.first_ref, bf16[1040,512]{1,0:T(8,128)(2,1)} %get-tuple-element.128.second_ref, s32[2,1040]{1,0:T(2,128)} %copy.96.refs_1_.across_ref, s32[1040,2]{1,0:T(8,128)} %copy-done.2, ...), custom_call_target="tpu_custom_call" | custom-call | tf_op jit(solution)/shard_map/pallas_call | solution.py:547
  381.7 29.2 %shard_map.167 = (f32[5,208,512]{2,1,0:T(8,128)}, f32[4,512,128]{2,1,0:T(8,128)}, f32[128,512]{1,0:T(8,128)}, f32[2,512]{1,0:T(2,128)}) custom-call(s32[1]{0:T(128)} %bitcast.29.own_ref, f32[5,208,512]{2,1,0:T(8,128)} %copy-done, f32[5,208,512]{2,1,0:T(8,128)} %bitcast.128, bf16[5,208,128]{2,1,0:T(8,128)(2,1)} %bitcast.134, f32[5,208,512]{2,1,0:T(8,128)} %bitcast.115, ...), custom_call_target="tpu_custom_call" | custom-call | tf_op jit(solution)/shard_map/pallas_call | solution.py:728
  411.0 3.3 multiply_convert_fusion
  414.2 75.3 %shard_map.168 = (f32[1040,512]{1,0:T(8,128)}, f32[512,512]{1,0:T(8,128)}, f32[512,512]{1,0:T(8,128)}) custom-call(bf16[1040,512]{1,0:T(8,128)(2,1)} %get-tuple-element.127.first_ref, bf16[1040,512]{1,0:T(8,128)(2,1)} %get-tuple-element.126.second_ref, s32[2,1040]{1,0:T(2,128)} %copy.91.refs_1_.across_ref, s32[1040,2]{1,0:T(8,128)} %copy-done.3, ...), custom_call_target="tpu_custom_call" | custom-call | tf_op jit(solution)/shard_map/pallas_call | solution.py:547
  489.5 1.7 fusion.36
  492.3 29.3 %shard_map.169 = (f32[5,208,512]{2,1,0:T(8,128)}, f32[4,512,128]{2,1,0:T(8,128)}, f32[128,512]{1,0:T(8,128)}, f32[2,512]{1,0:T(2,128)}) custom-call(s32[1]{0:T(128)} %bitcast.29.own_ref, f32[5,208,512]{2,1,0:T(8,128)} %get-tuple-element.58.upstream_ref, f32[5,208,512]{2,1,0:T(8,128)} %bitcast.127, bf16[5,208,128]{2,1,0:T(8,128)(2,1)} %bitcast.133, ...), custom_call_target="tpu_custom_call" | custom-call | tf_op jit(solution)/shard_map/pallas_call | solution.py:728
  521.6 1.7 slice.173
  528.2 20.3 %shard_map.170 = f32[544,128]{1,0:T(8,128)} custom-call(bf16[8,544,128]{2,1,0:T(8,128)(2,1)} %pad_maximum_fusion.rows_ref), custom_call_target="tpu_custom_call" | custom-call | tf_op jit(solution)/shard_map/pallas_call | solution.py:501
  554.5 2.7 maximum_bitcast_fusion
  (152 shorter events, 33.0 us)
Async XLA Ops:
  2.4 1.7 copy-start.24
  2.5 1.7 copy-start.21
  2.5 1.8 copy-start.18
  2.5 1.8 copy-start.17
  4.1 2.6 copy-start.9
  70.2 14.5 %copy-start.20 = (s32[2,985]{1,0:T(2,128)S(1)}, s32[2,985]{1,0:T(2,128)}, u32[]{:S(2)}) copy-start(s32[2,985]{1,0:T(2,128)} %param.13) | copy-start | bytes 23644
  70.2 14.7 %copy-start.19 = (s32[2,985,2]{1,2,0:T(2,128)S(1)}, s32[2,985,2]{1,2,0:T(2,128)}, u32[]{:S(2)}) copy-start(s32[2,985,2]{1,2,0:T(2,128)} %param.12) | copy-start | bytes 47284
  84.6 1.1 copy-start.16
  88.7 0.8 copy-start.3
  89.5 92.1 %copy-start.4 = (f32[5,208,512]{2,1,0:T(8,128)S(1)}, f32[5,208,512]{2,1,0:T(8,128)}, u32[]{:S(2)}) copy-start(f32[5,208,512]{2,1,0:T(8,128)} %get-tuple-element.42.middle_ref) | copy-start | bytes 6389764
  185.7 16.1 %copy-start.10 = (f32[985,512]{1,0:T(8,128)S(1)}, f32[985,512]{1,0:T(8,128)}, u32[]{:S(2)}) copy-start(f32[985,512]{1,0:T(8,128)} %param.11) | copy-start | bytes 6051844
  205.2 95.2 %copy-start = (f32[5,208,512]{2,1,0:T(8,128)}, f32[5,208,512]{2,1,0:T(8,128)S(1)}, u32[]{:S(2)}) copy-start(f32[5,208,512]{2,1,0:T(8,128)S(1)} %pad.53.upstream_ref) | copy-start | bytes 6389764
  298.1 2.3 copy-start.5
  298.1 2.5 copy-start.7
  298.1 2.8 copy-start.8
  414.2 75.3 %copy-start.1 = (f32[5,208,512]{2,1,0:T(8,128)S(1)}, f32[5,208,512]{2,1,0:T(8,128)}, u32[]{:S(2)}) copy-start(f32[5,208,512]{2,1,0:T(8,128)} %get-tuple-element.58.upstream_ref) | copy-start | bytes 6389764
  414.2 75.3 %copy-start.6 = (bf16[1040,512]{1,0:T(8,128)(2,1)S(1)}, bf16[1040,512]{1,0:T(8,128)(2,1)}, u32[]{:S(2)}) copy-start(bf16[1040,512]{1,0:T(8,128)(2,1)} %get-tuple-element.46) | copy-start | bytes 3194884
  523.3 1.6 copy-start.23
  523.3 2.6 copy-start.12
  524.9 1.2 copy-start.22
  524.9 2.1 copy-start.11
  527.1 27.4 %copy-start.14 = (f32[512,512]{1,0:T(8,128)S(1)}, f32[512,512]{1,0:T(8,128)}, u32[]{:S(2)}) copy-start(f32[512,512]{1,0:T(8,128)} %get-tuple-element.71) | copy-start | bytes 3145732
  551.6 5.6 %copy-start.13 = (f32[512,512]{1,0:T(8,128)S(1)}, f32[512,512]{1,0:T(8,128)}, u32[]{:S(2)}) copy-start(f32[512,512]{1,0:T(8,128)} %get-tuple-element.73) | copy-start | bytes 3145732
  551.6 5.6 %copy-start.15 = (f32[512,512]{1,0:T(8,128)S(1)}, f32[512,512]{1,0:T(8,128)}, u32[]{:S(2)}) copy-start(f32[512,512]{1,0:T(8,128)} %get-tuple-element.72) | copy-start | bytes 3145732
  (1 other events, 0.8 us)

commit v8 on v7

--- a/solution.py
+++ b/solution.py
@@ -246,7 +246,18 @@
 
 
 def exchange_chunks(
-    peers, make_rows, work, take_rows, out_rows, landed, results, back, sems, parts=1, rings=()
+    peers,
+    make_rows,
+    work,
+    take_rows,
+    out_rows,
+    landed,
+    results,
+    back,
+    sems,
+    parts=1,
+    rings=(),
+    early=None,
 ):
     out_send, out_recv, back_send, back_recv = sems
     me = lax.axis_index("expert")
@@ -275,15 +286,8 @@
     lax.fori_loop(1, peers, make_out, 0)
     landed[me] = make_rows(me)
     start_out(peers - 1)
-    for distance in range(2, parts // 2 + 1):
-        for ring in rings[:1]:
-            ring.stage(distance)
-    for ring in rings[:1]:
-        ring.finish()
-    for ring in rings[1:]:
-        ring.stage(1)
-
-    def one_chunk(step, carry):
+
+    def await_chunk(step):
         peer = lax.rem(me + peers - step, peers)
 
         @pl.when(step > 0)
@@ -292,6 +296,32 @@
                 out_rows.at[peer], landed.at[peer], out_send, out_recv, step, peer
             ).wait_recv()
 
+        return peer
+
+    if early is not None:
+
+        def early_chunk(step, carry):
+            for distance in range(2, parts // 2 + 1):
+
+                @pl.when(step == (5 * peers) // 8 + distance - 2)
+                def _(distance=distance):
+                    for ring in rings[:1]:
+                        ring.stage(distance)
+
+            early(step, await_chunk(step))
+            return carry
+
+        lax.fori_loop(0, peers, early_chunk, 0)
+    for ring in rings[:1]:
+        ring.finish()
+    for ring in rings[1:]:
+        ring.stage(1)
+
+    def one_chunk(step, carry):
+        if early is None:
+            peer = await_chunk(step)
+        else:
+            peer = lax.rem(me + peers - step, peers)
         work(step, peer)
 
         @pl.when(step > 0)
@@ -334,7 +364,7 @@
     sources = refs[4 : 5 + follow]
     landed, first, second = refs[5 + follow : 8 + follow]
     targets = refs[8 + follow : 9 + 2 * follow]
-    out_rows, back, results, total, *sems = refs[9 + 2 * follow :]
+    out_rows, back, results, hidden_all, *sems = refs[9 + 2 * follow :]
     wout_ref = targets[0]
     spacing = landed.shape[1]
     tokens = rows_ref.shape[0]
@@ -359,19 +389,17 @@
             one_hot(hits[0] | hits[1]), rows_ref[...], preferred_element_type=jnp.float32
         ).astype(jnp.bfloat16)
 
-    def work(step, peer):
+    def early(step, peer):
         chunk = landed[peer]
         for part in range(parts):
             cols = slice(part * width, (part + 1) * width)
             before = jnp.dot(chunk, win_ref[:, cols], preferred_element_type=jnp.float32)
-            hidden = gelu_exact(before).astype(jnp.bfloat16)
-            term = jnp.dot(hidden, wout_ref[cols, :], preferred_element_type=jnp.float32)
-            if part == 0:
-                total[...] = term
-            elif part < parts - 1:
-                total[...] += term
-            else:
-                results[step] = (total[...] + term).astype(jnp.bfloat16)
+            hidden_all[step, :, cols] = gelu_exact(before).astype(jnp.bfloat16)
+
+    def work(step, peer):
+        results[step] = jnp.dot(
+            hidden_all[step], wout_ref[...], preferred_element_type=jnp.float32
+        ).astype(jnp.bfloat16)
 
     def take_rows(slab):
         rows_back = back[slab]
@@ -393,6 +421,7 @@
         sems[:4],
         parts=parts,
         rings=rings,
+        early=early,
     )
     for copy in copies[1:]:
         copy.wait()
@@ -531,7 +560,7 @@
         in_specs=whole_in_vmem(5 + follow),
         out_specs=tuple(whole_in_vmem(4 + follow)),
         scratch_shapes=[pltpu.VMEM(chunks, jnp.bfloat16)] * 3
-        + [pltpu.VMEM((spacing, width), jnp.float32)]
+        + [pltpu.VMEM((peers, spacing, win.shape[1]), jnp.bfloat16)]
         + exchange_sems(peers)
         + [pltpu.SemaphoreType.DMA((parts,))] * (2 + 2 * follow)
         + [pltpu.SemaphoreType.DMA((2,))],

time: 569 us -> 564 us (level)
  no operation moved by 1% of the time
where the time goes in v8:
time: 564 us; the launch traced here: 554 us
  Pallas kernels  488 us (87%)
  local copies, waits for them, and re-layouts  36.2 us (6%)
  other arithmetic  24.9 us (4%)
    pallas_call x2, Pallas kernels, experts_forward(): pl.pallas_call(functools.partial(forward_kernel, peers, parts, follow), o...  175 us
    pallas_call x2, Pallas kernels, experts_backward(): pl.pallas_call(functools.partial(backward_kernel, peers, parts), out_shap...  150 us
    pallas_call x2, Pallas kernels, attend_back(): pl.pallas_call(attend_back_kernel, grid=(images,), out_shape=(jax.ShapeDt...  58.5 us
    pallas_call x1, Pallas kernels, gather_start(): pl.pallas_call(functools.partial(gather_kernel, experts, parts), out_shap...  54.5 us
    pallas_call x2, Pallas kernels, attend(): pl.pallas_call(functools.partial(attend_kernel, experts), grid=(images,),...  29.4 us
    pallas_call x1, Pallas kernels, sum_shares(): pl.pallas_call(functools.partial(sum_kernel, peers), out_shape=jax.ShapeD...  20.7 us

profile of v8, /device:TPU:1, one launch (start us, length us, event | category | flops | bytes accessed | tf_op | source)
XLA Modules:
  0.0 554.5 jit_solution(12086499361815712563)
XLA Ops:
  0.6 1.8 reshape.193
  2.5 1.6 pad.46.stream_ref
  5.0 1.7 convert.77
  8.3 54.5 %shard_map.161 = (bf16[9,8,64,512]{3,2,1,0:T(8,128)(2,1)}, bf16[512,2048]{1,0:T(8,128)(2,1)}) custom-call(bf16[9,64,128]{2,1,0:T(8,128)(2,1)} %pad_maximum_fusion.2.small_ref, bf16[512,512]{1,0:T(8,128)(2,1)} %get-tuple-element.147.win_ref), custom_call_target="tpu_custom_call" | custom-call | tf_op jit(solution)/shard_map/pallas_call | solution.py:233
  62.7 4.7 fusion.80
  70.2 14.5 %shard_map.162 = (f32[5,208,512]{2,1,0:T(8,128)}, bf16[5,208,512]{2,1,0:T(8,128)(2,1)}, f32[5,208,128]{2,1,0:T(8,128)}, bf16[5,208,512]{2,1,0:T(8,128)(2,1)}) custom-call(f32[5,208,512]{2,1,0:T(8,128)} %pad.46.stream_ref, bf16[4,512,512]{2,1,0:T(8,128)(2,1)} %bitcast.117, f32[2,512]{1,0:T(2,128)} %squeeze.8.gains_ref, ...), custom_call_target="tpu_custom_call" | custom-call | tf_op jit(solution)/shard_map/pallas_call | solution.py:738
  89.5 94.8 %shard_map.163 = (bf16[8,320,512]{2,1,0:T(8,128)(2,1)}, bf16[1040,512]{1,0:T(8,128)(2,1)}, bf16[1040,512]{1,0:T(8,128)(2,1)}, bf16[2048,512]{1,0:T(8,128)(2,1)}, bf16[512,2048]{1,0:T(8,128)(2,1)}) custom-call(bf16[1040,512]{1,0:T(8,128)(2,1)} %bitcast.136, s32[2,1040]{1,0:T(2,128)} %copy.91.refs_1_.across_ref, s32[1040,2]{1,0:T(8,128)} %copy-done.3, ...), custom_call_target="tpu_custom_call" | custom-call | tf_op jit(solution)/shard_map/pallas_call | solution.py:557
  184.3 3.4 fusion.35
  188.4 14.9 %shard_map.164 = (f32[5,208,512]{2,1,0:T(8,128)}, bf16[5,208,512]{2,1,0:T(8,128)(2,1)}, f32[5,208,128]{2,1,0:T(8,128)}, bf16[5,208,512]{2,1,0:T(8,128)(2,1)}) custom-call(f32[5,208,512]{2,1,0:T(8,128)} %bitcast.114, bf16[4,512,512]{2,1,0:T(8,128)(2,1)} %bitcast.119, f32[2,512]{1,0:T(2,128)} %squeeze.20.gains_ref, bf16[512,128]{1,0:T(8,128)(2,1)} %get-tuple-element.140.router_ref), custom_call_target="tpu_custom_call" | custom-call | tf_op jit(solution)/shard_map/pallas_call | solution.py:738
  204.5 1.6 reshape.212
  206.1 1.8 pad.53.upstream_ref
  214.3 79.8 %shard_map.165 = (bf16[8,320,512]{2,1,0:T(8,128)(2,1)}, bf16[1040,512]{1,0:T(8,128)(2,1)}, bf16[1040,512]{1,0:T(8,128)(2,1)}, bf16[2048,512]{1,0:T(8,128)(2,1)}) custom-call(bf16[1040,512]{1,0:T(8,128)(2,1)} %bitcast.135, s32[2,1040]{1,0:T(2,128)} %copy.96.refs_1_.across_ref, s32[1040,2]{1,0:T(8,128)} %copy-done.2, ...), custom_call_target="tpu_custom_call" | custom-call | tf_op jit(solution)/shard_map/pallas_call | solution.py:557
  294.1 2.2 fusion.40
  296.9 2.0 multiply_convert_fusion.2
  299.1 1.5 reshape.210
  300.6 75.4 %shard_map.166 = (f32[1040,512]{1,0:T(8,128)}, f32[512,512]{1,0:T(8,128)}, f32[512,512]{1,0:T(8,128)}) custom-call(bf16[1040,512]{1,0:T(8,128)(2,1)} %get-tuple-element.129.first_ref, bf16[1040,512]{1,0:T(8,128)(2,1)} %get-tuple-element.128.second_ref, s32[2,1040]{1,0:T(2,128)} %copy.96.refs_1_.across_ref, s32[1040,2]{1,0:T(8,128)} %copy-done.2, ...), custom_call_target="tpu_custom_call" | custom-call | tf_op jit(solution)/shard_map/pallas_call | solution.py:576
  377.0 29.2 %shard_map.167 = (f32[5,208,512]{2,1,0:T(8,128)}, f32[4,512,128]{2,1,0:T(8,128)}, f32[128,512]{1,0:T(8,128)}, f32[2,512]{1,0:T(2,128)}) custom-call(s32[1]{0:T(128)} %bitcast.29.own_ref, f32[5,208,512]{2,1,0:T(8,128)} %copy-done, f32[5,208,512]{2,1,0:T(8,128)} %bitcast.128, bf16[5,208,128]{2,1,0:T(8,128)(2,1)} %bitcast.134, f32[5,208,512]{2,1,0:T(8,128)} %bitcast.115, ...), custom_call_target="tpu_custom_call" | custom-call | tf_op jit(solution)/shard_map/pallas_call | solution.py:757
  406.2 3.3 multiply_convert_fusion
  409.5 75.0 %shard_map.168 = (f32[1040,512]{1,0:T(8,128)}, f32[512,512]{1,0:T(8,128)}, f32[512,512]{1,0:T(8,128)}) custom-call(bf16[1040,512]{1,0:T(8,128)(2,1)} %get-tuple-element.127.first_ref, bf16[1040,512]{1,0:T(8,128)(2,1)} %get-tuple-element.126.second_ref, s32[2,1040]{1,0:T(2,128)} %copy.91.refs_1_.across_ref, s32[1040,2]{1,0:T(8,128)} %copy-done.3, ...), custom_call_target="tpu_custom_call" | custom-call | tf_op jit(solution)/shard_map/pallas_call | solution.py:576
  484.5 1.7 fusion.36
  487.3 29.2 %shard_map.169 = (f32[5,208,512]{2,1,0:T(8,128)}, f32[4,512,128]{2,1,0:T(8,128)}, f32[128,512]{1,0:T(8,128)}, f32[2,512]{1,0:T(2,128)}) custom-call(s32[1]{0:T(128)} %bitcast.29.own_ref, f32[5,208,512]{2,1,0:T(8,128)} %get-tuple-element.58.upstream_ref, f32[5,208,512]{2,1,0:T(8,128)} %bitcast.127, bf16[5,208,128]{2,1,0:T(8,128)(2,1)} %bitcast.133, ...), custom_call_target="tpu_custom_call" | custom-call | tf_op jit(solution)/shard_map/pallas_call | solution.py:757
  516.5 1.7 slice.173
  523.1 20.7 %shard_map.170 = f32[544,128]{1,0:T(8,128)} custom-call(bf16[8,544,128]{2,1,0:T(8,128)(2,1)} %pad_maximum_fusion.rows_ref), custom_call_target="tpu_custom_call" | custom-call | tf_op jit(solution)/shard_map/pallas_call | solution.py:530
  549.9 2.7 maximum_bitcast_fusion
  (152 shorter events, 33.0 us)
Async XLA Ops:
  2.4 1.7 copy-start.24
  2.5 1.7 copy-start.21
  2.5 1.8 copy-start.18
  2.5 1.8 copy-start.17
  4.1 2.6 copy-start.9
  70.2 14.5 %copy-start.20 = (s32[2,985]{1,0:T(2,128)S(1)}, s32[2,985]{1,0:T(2,128)}, u32[]{:S(2)}) copy-start(s32[2,985]{1,0:T(2,128)} %param.13) | copy-start | bytes 23644
  70.2 14.7 %copy-start.19 = (s32[2,985,2]{1,2,0:T(2,128)S(1)}, s32[2,985,2]{1,2,0:T(2,128)}, u32[]{:S(2)}) copy-start(s32[2,985,2]{1,2,0:T(2,128)} %param.12) | copy-start | bytes 47284
  84.6 1.1 copy-start.16
  88.7 0.8 copy-start.3
  89.5 94.8 %copy-start.4 = (f32[5,208,512]{2,1,0:T(8,128)S(1)}, f32[5,208,512]{2,1,0:T(8,128)}, u32[]{:S(2)}) copy-start(f32[5,208,512]{2,1,0:T(8,128)} %get-tuple-element.42.middle_ref) | copy-start | bytes 6389764
  188.4 16.1 %copy-start.10 = (f32[985,512]{1,0:T(8,128)S(1)}, f32[985,512]{1,0:T(8,128)}, u32[]{:S(2)}) copy-start(f32[985,512]{1,0:T(8,128)} %param.11) | copy-start | bytes 6051844
  207.9 88.5 %copy-start = (f32[5,208,512]{2,1,0:T(8,128)}, f32[5,208,512]{2,1,0:T(8,128)S(1)}, u32[]{:S(2)}) copy-start(f32[5,208,512]{2,1,0:T(8,128)S(1)} %pad.53.upstream_ref) | copy-start | bytes 6389764
  294.1 2.3 copy-start.5
  294.1 2.5 copy-start.7
  294.1 2.8 copy-start.8
  409.5 75.0 %copy-start.1 = (f32[5,208,512]{2,1,0:T(8,128)S(1)}, f32[5,208,512]{2,1,0:T(8,128)}, u32[]{:S(2)}) copy-start(f32[5,208,512]{2,1,0:T(8,128)} %get-tuple-element.58.upstream_ref) | copy-start | bytes 6389764
  409.5 75.0 %copy-start.6 = (bf16[1040,512]{1,0:T(8,128)(2,1)S(1)}, bf16[1040,512]{1,0:T(8,128)(2,1)}, u32[]{:S(2)}) copy-start(bf16[1040,512]{1,0:T(8,128)(2,1)} %get-tuple-element.46) | copy-start | bytes 3194884
  518.3 1.6 copy-start.23
  518.3 2.6 copy-start.12
  519.8 1.2 copy-start.22
  519.8 2.1 copy-start.11
  522.1 27.8 %copy-start.14 = (f32[512,512]{1,0:T(8,128)S(1)}, f32[512,512]{1,0:T(8,128)}, u32[]{:S(2)}) copy-start(f32[512,512]{1,0:T(8,128)} %get-tuple-element.71) | copy-start | bytes 3145732
  547.0 5.6 %copy-start.13 = (f32[512,512]{1,0:T(8,128)S(1)}, f32[512,512]{1,0:T(8,128)}, u32[]{:S(2)}) copy-start(f32[512,512]{1,0:T(8,128)} %get-tuple-element.73) | copy-start | bytes 3145732
  547.0 5.6 %copy-start.15 = (f32[512,512]{1,0:T(8,128)S(1)}, f32[512,512]{1,0:T(8,128)}, u32[]{:S(2)}) copy-start(f32[512,512]{1,0:T(8,128)} %get-tuple-element.72) | copy-start | bytes 3145732
  (1 other events, 0.8 us)

commit v9 on v8

--- a/solution.py
+++ b/solution.py
@@ -349,6 +349,146 @@
     lax.fori_loop(1, peers, finish, 0)
     for ring in rings[1:]:
         ring.finish()
+
+
+def exchange_paired(peers, make_rows, work, take_rows, out_rows, landed, results, back, sems):
+    out_sems, back_sems = sems[:2], sems[2:]
+    me = lax.axis_index("expert")
+    side = lax.axis_index("tensor")
+    parity = lax.rem(side, 2)
+    partner = side + 1 - 2 * parity
+    spacing = landed.shape[1]
+    half = spacing * 2 // 5 // 16 * 16
+    common = spacing - 2 * half
+    barrier = pltpu.get_barrier_semaphore()
+    greet_axis(barrier, "expert", me, peers)
+    greet(barrier, "tensor", partner)
+    pl.semaphore_wait(barrier, peers)
+
+    def piece(ref, index, kind):
+        if kind == 0:
+            return ref.at[index, pl.ds(0, common)]
+        start = common + half * (parity if kind == 1 else 1 - parity)
+        return ref.at[index, pl.ds(pl.multiple_of(start, 16), half)]
+
+    def cross(pair, source, held, target, slab, step, peer):
+        return [
+            send(
+                piece(source, held, kind),
+                piece(target, slab, kind),
+                pair[0].at[kind, step],
+                pair[1].at[kind, step],
+                "expert",
+                peer,
+            )
+            for kind in range(2)
+        ]
+
+    def over(pair, target, slab, step, kind):
+        place = piece(target, slab, kind)
+        return send(place, place, pair[0].at[2, step], pair[1].at[2, step], "tensor", partner)
+
+    def ahead_of(step):
+        return lax.rem(me + step, peers)
+
+    def behind(step):
+        return lax.rem(me + peers - step, peers)
+
+    def out_copies(step, peer):
+        return cross(out_sems, out_rows, peer, landed, me, step, peer)
+
+    def back_copies(step, peer, slab):
+        return cross(back_sems, results, step, back, slab, step, peer)
+
+    def start_out(step):
+        for copy in out_copies(step, ahead_of(step)):
+            copy.start()
+
+    def make_out(step, carry):
+        peer = ahead_of(step)
+        out_rows[peer] = make_rows(peer)
+
+        @pl.when(step > 1)
+        def _():
+            start_out(step - 1)
+
+        return carry
+
+    lax.fori_loop(1, peers, make_out, 0)
+    landed[me] = make_rows(me)
+    start_out(peers - 1)
+
+    def pass_out(step):
+        peer = behind(step)
+        for copy in cross(out_sems, out_rows, peer, landed, peer, step, peer):
+            copy.wait_recv()
+        over(out_sems, landed, peer, step, 1).start()
+
+    def pass_back(step):
+        slab = ahead_of(step)
+        for copy in back_copies(step, slab, slab):
+            copy.wait_recv()
+        over(back_sems, back, slab, step, 1).start()
+
+    lag = 5
+
+    def one_chunk(turn, carry):
+        @pl.when((turn > 0) & (turn < peers))
+        def _():
+            pass_out(turn)
+
+        step = turn - 1
+        peer = behind(step)
+
+        @pl.when(step > 0)
+        def _():
+            over(out_sems, landed, peer, step, 2).wait_recv()
+
+        @pl.when(step >= 0)
+        def _():
+            work(step, peer)
+
+        @pl.when(step > 0)
+        def _():
+            for copy in back_copies(step, peer, me):
+                copy.start()
+
+        @pl.when(turn > lag)
+        def _():
+            pass_back(turn - lag)
+
+        return carry
+
+    lax.fori_loop(0, peers + 1, one_chunk, 0)
+    back[me] = results[0]
+    take_rows(me)
+    passed = max(1, peers - lag + 1)
+
+    def collect(turn, carry):
+        @pl.when((turn >= passed) & (turn < peers))
+        def _():
+            pass_back(turn)
+
+        @pl.when(turn > 1)
+        def _():
+            slab = ahead_of(turn - 1)
+            over(back_sems, back, slab, turn - 1, 2).wait_recv()
+            take_rows(slab)
+
+        return carry
+
+    lax.fori_loop(1, peers + 1, collect, 0)
+
+    def finish(step, carry):
+        slab = ahead_of(step)
+        sent = out_copies(step, slab) + back_copies(step, slab, slab)
+        sent.append(over(out_sems, landed, behind(step), step, 1))
+        sent.append(over(back_sems, back, slab, step, 1))
+        for copy in sent:
+            copy.wait_send()
+        return carry
+
+    lax.fori_loop(1, peers, finish, 0)
 
 
 def slot_hits(slots, start, shape, axis):
@@ -493,7 +633,7 @@
             one_hot(hits[0] | hits[1]), back[slab], preferred_element_type=jnp.float32
         )
 
-    exchange_chunks(peers, make_rows, work, take_rows, out_rows, landed, results, back, sems)
+    exchange_paired(peers, make_rows, work, take_rows, out_rows, landed, results, back, sems)
 
 
 def sum_kernel(peers, rows_ref, sum_ref, landed, sends, arrivals):
@@ -585,7 +725,7 @@
         scratch_shapes=[pltpu.VMEM(arrived.shape, jnp.bfloat16)] * 4
         + [pltpu.VMEM((spacing, width), jnp.float32)]
         + [pltpu.VMEM((spacing, inner), jnp.bfloat16)] * 2
-        + exchange_sems(peers),
+        + [pltpu.SemaphoreType.DMA((3, peers))] * 4,
         compiler_params=pltpu.CompilerParams(collective_id=1, has_side_effects=True),
     )(first, second, slots.T, slots, arrived, win, wout)
 

time: 564 us -> 562 us (level)
    pallas_call x2, Pallas kernels: 150 us -> 144 us  [experts_backward(): pl.pallas_call(functools.partial(backward_kernel, peers, parts), out_shap...]
where the time goes in v9:
time: 562 us; the launch traced here: 552 us
  Pallas kernels  486 us (86%)
  local copies, waits for them, and re-layouts  36.2 us (6%)
  other arithmetic  24.9 us (4%)
    pallas_call x2, Pallas kernels, experts_forward(): pl.pallas_call(functools.partial(forward_kernel, peers, parts, follow), o...  175 us
    pallas_call x2, Pallas kernels, experts_backward(): pl.pallas_call(functools.partial(backward_kernel, peers, parts), out_shap...  144 us
    pallas_call x2, Pallas kernels, attend_back(): pl.pallas_call(attend_back_kernel, grid=(images,), out_shape=(jax.ShapeDt...  58.5 us
    pallas_call x1, Pallas kernels, gather_start(): pl.pallas_call(functools.partial(gather_kernel, experts, parts), out_shap...  54.5 us
    pallas_call x2, Pallas kernels, attend(): pl.pallas_call(functools.partial(attend_kernel, experts), grid=(images,),...  29.4 us
    pallas_call x1, Pallas kernels, sum_shares(): pl.pallas_call(functools.partial(sum_kernel, peers), out_shape=jax.ShapeD...  24.2 us

profile of v9, /device:TPU:1, one launch (start us, length us, event | category | flops | bytes accessed | tf_op | source)
XLA Modules:
  0.0 552.0 jit_solution(11253953128670931336)
XLA Ops:
  0.6 1.8 reshape.193
  2.5 1.6 pad.46.stream_ref
  5.0 1.7 convert.77
  8.3 54.5 %shard_map.161 = (bf16[9,8,64,512]{3,2,1,0:T(8,128)(2,1)}, bf16[512,2048]{1,0:T(8,128)(2,1)}) custom-call(bf16[9,64,128]{2,1,0:T(8,128)(2,1)} %pad_maximum_fusion.2.small_ref, bf16[512,512]{1,0:T(8,128)(2,1)} %get-tuple-element.147.win_ref), custom_call_target="tpu_custom_call" | custom-call | tf_op jit(solution)/shard_map/pallas_call | solution.py:233
  62.7 4.7 fusion.80
  70.2 14.5 %shard_map.162 = (f32[5,208,512]{2,1,0:T(8,128)}, bf16[5,208,512]{2,1,0:T(8,128)(2,1)}, f32[5,208,128]{2,1,0:T(8,128)}, bf16[5,208,512]{2,1,0:T(8,128)(2,1)}) custom-call(f32[5,208,512]{2,1,0:T(8,128)} %pad.46.stream_ref, bf16[4,512,512]{2,1,0:T(8,128)(2,1)} %bitcast.117, f32[2,512]{1,0:T(2,128)} %squeeze.8.gains_ref, ...), custom_call_target="tpu_custom_call" | custom-call | tf_op jit(solution)/shard_map/pallas_call | solution.py:878
  89.5 94.8 %shard_map.163 = (bf16[8,320,512]{2,1,0:T(8,128)(2,1)}, bf16[1040,512]{1,0:T(8,128)(2,1)}, bf16[1040,512]{1,0:T(8,128)(2,1)}, bf16[2048,512]{1,0:T(8,128)(2,1)}, bf16[512,2048]{1,0:T(8,128)(2,1)}) custom-call(bf16[1040,512]{1,0:T(8,128)(2,1)} %bitcast.136, s32[2,1040]{1,0:T(2,128)} %copy.91.refs_1_.across_ref, s32[1040,2]{1,0:T(8,128)} %copy-done.3, ...), custom_call_target="tpu_custom_call" | custom-call | tf_op jit(solution)/shard_map/pallas_call | solution.py:697
  184.3 3.4 fusion.35
  188.4 14.9 %shard_map.164 = (f32[5,208,512]{2,1,0:T(8,128)}, bf16[5,208,512]{2,1,0:T(8,128)(2,1)}, f32[5,208,128]{2,1,0:T(8,128)}, bf16[5,208,512]{2,1,0:T(8,128)(2,1)}) custom-call(f32[5,208,512]{2,1,0:T(8,128)} %bitcast.114, bf16[4,512,512]{2,1,0:T(8,128)(2,1)} %bitcast.119, f32[2,512]{1,0:T(2,128)} %squeeze.20.gains_ref, bf16[512,128]{1,0:T(8,128)(2,1)} %get-tuple-element.140.router_ref), custom_call_target="tpu_custom_call" | custom-call | tf_op jit(solution)/shard_map/pallas_call | solution.py:878
  204.5 1.6 reshape.212
  206.1 1.8 pad.53.upstream_ref
  214.3 79.8 %shard_map.165 = (bf16[8,320,512]{2,1,0:T(8,128)(2,1)}, bf16[1040,512]{1,0:T(8,128)(2,1)}, bf16[1040,512]{1,0:T(8,128)(2,1)}, bf16[2048,512]{1,0:T(8,128)(2,1)}) custom-call(bf16[1040,512]{1,0:T(8,128)(2,1)} %bitcast.135, s32[2,1040]{1,0:T(2,128)} %copy.96.refs_1_.across_ref, s32[1040,2]{1,0:T(8,128)} %copy-done.2, ...), custom_call_target="tpu_custom_call" | custom-call | tf_op jit(solution)/shard_map/pallas_call | solution.py:697
  294.1 2.2 fusion.40
  296.9 2.0 multiply_convert_fusion.2
  299.1 1.5 reshape.210
  300.6 70.5 %shard_map.166 = (f32[1040,512]{1,0:T(8,128)}, f32[512,512]{1,0:T(8,128)}, f32[512,512]{1,0:T(8,128)}) custom-call(bf16[1040,512]{1,0:T(8,128)(2,1)} %get-tuple-element.129.first_ref, bf16[1040,512]{1,0:T(8,128)(2,1)} %get-tuple-element.128.second_ref, s32[2,1040]{1,0:T(2,128)} %copy.96.refs_1_.across_ref, s32[1040,2]{1,0:T(8,128)} %copy-done.2, ...), custom_call_target="tpu_custom_call" | custom-call | tf_op jit(solution)/shard_map/pallas_call | solution.py:716
  372.2 29.3 %shard_map.167 = (f32[5,208,512]{2,1,0:T(8,128)}, f32[4,512,128]{2,1,0:T(8,128)}, f32[128,512]{1,0:T(8,128)}, f32[2,512]{1,0:T(2,128)}) custom-call(s32[1]{0:T(128)} %bitcast.29.own_ref, f32[5,208,512]{2,1,0:T(8,128)} %copy-done, f32[5,208,512]{2,1,0:T(8,128)} %bitcast.128, bf16[5,208,128]{2,1,0:T(8,128)(2,1)} %bitcast.134, f32[5,208,512]{2,1,0:T(8,128)} %bitcast.115, ...), custom_call_target="tpu_custom_call" | custom-call | tf_op jit(solution)/shard_map/pallas_call | solution.py:897
  401.4 3.3 multiply_convert_fusion
  404.7 73.8 %shard_map.168 = (f32[1040,512]{1,0:T(8,128)}, f32[512,512]{1,0:T(8,128)}, f32[512,512]{1,0:T(8,128)}) custom-call(bf16[1040,512]{1,0:T(8,128)(2,1)} %get-tuple-element.127.first_ref, bf16[1040,512]{1,0:T(8,128)(2,1)} %get-tuple-element.126.second_ref, s32[2,1040]{1,0:T(2,128)} %copy.91.refs_1_.across_ref, s32[1040,2]{1,0:T(8,128)} %copy-done.3, ...), custom_call_target="tpu_custom_call" | custom-call | tf_op jit(solution)/shard_map/pallas_call | solution.py:716
  478.5 1.7 fusion.36
  481.3 29.3 %shard_map.169 = (f32[5,208,512]{2,1,0:T(8,128)}, f32[4,512,128]{2,1,0:T(8,128)}, f32[128,512]{1,0:T(8,128)}, f32[2,512]{1,0:T(2,128)}) custom-call(s32[1]{0:T(128)} %bitcast.29.own_ref, f32[5,208,512]{2,1,0:T(8,128)} %get-tuple-element.58.upstream_ref, f32[5,208,512]{2,1,0:T(8,128)} %bitcast.127, bf16[5,208,128]{2,1,0:T(8,128)(2,1)} %bitcast.133, ...), custom_call_target="tpu_custom_call" | custom-call | tf_op jit(solution)/shard_map/pallas_call | solution.py:897
  510.5 1.7 slice.173
  517.2 24.2 %shard_map.170 = f32[544,128]{1,0:T(8,128)} custom-call(bf16[8,544,128]{2,1,0:T(8,128)(2,1)} %pad_maximum_fusion.rows_ref), custom_call_target="tpu_custom_call" | custom-call | tf_op jit(solution)/shard_map/pallas_call | solution.py:670
  547.4 2.7 maximum_bitcast_fusion
  (152 shorter events, 33.0 us)
Async XLA Ops:
  2.4 1.7 copy-start.24
  2.5 1.7 copy-start.21
  2.5 1.8 copy-start.18
  2.5 1.8 copy-start.17
  4.1 2.6 copy-start.9
  70.2 14.5 %copy-start.20 = (s32[2,985]{1,0:T(2,128)S(1)}, s32[2,985]{1,0:T(2,128)}, u32[]{:S(2)}) copy-start(s32[2,985]{1,0:T(2,128)} %param.13) | copy-start | bytes 23644
  70.2 14.7 %copy-start.19 = (s32[2,985,2]{1,2,0:T(2,128)S(1)}, s32[2,985,2]{1,2,0:T(2,128)}, u32[]{:S(2)}) copy-start(s32[2,985,2]{1,2,0:T(2,128)} %param.12) | copy-start | bytes 47284
  84.6 1.1 copy-start.16
  88.7 0.8 copy-start.3
  89.5 94.8 %copy-start.4 = (f32[5,208,512]{2,1,0:T(8,128)S(1)}, f32[5,208,512]{2,1,0:T(8,128)}, u32[]{:S(2)}) copy-start(f32[5,208,512]{2,1,0:T(8,128)} %get-tuple-element.42.middle_ref) | copy-start | bytes 6389764
  188.4 16.1 %copy-start.10 = (f32[985,512]{1,0:T(8,128)S(1)}, f32[985,512]{1,0:T(8,128)}, u32[]{:S(2)}) copy-start(f32[985,512]{1,0:T(8,128)} %param.11) | copy-start | bytes 6051844
  207.9 88.5 %copy-start = (f32[5,208,512]{2,1,0:T(8,128)}, f32[5,208,512]{2,1,0:T(8,128)S(1)}, u32[]{:S(2)}) copy-start(f32[5,208,512]{2,1,0:T(8,128)S(1)} %pad.53.upstream_ref) | copy-start | bytes 6389764
  294.1 2.3 copy-start.5
  294.1 2.5 copy-start.7
  294.1 2.8 copy-start.8
  404.7 73.8 %copy-start.1 = (f32[5,208,512]{2,1,0:T(8,128)S(1)}, f32[5,208,512]{2,1,0:T(8,128)}, u32[]{:S(2)}) copy-start(f32[5,208,512]{2,1,0:T(8,128)} %get-tuple-element.58.upstream_ref) | copy-start | bytes 6389764
  404.7 73.8 %copy-start.6 = (bf16[1040,512]{1,0:T(8,128)(2,1)S(1)}, bf16[1040,512]{1,0:T(8,128)(2,1)}, u32[]{:S(2)}) copy-start(bf16[1040,512]{1,0:T(8,128)(2,1)} %get-tuple-element.46) | copy-start | bytes 3194884
  512.3 1.6 copy-start.23
  512.3 2.6 copy-start.12
  513.8 1.2 copy-start.22
  513.8 2.1 copy-start.11
  516.1 31.3 %copy-start.14 = (f32[512,512]{1,0:T(8,128)S(1)}, f32[512,512]{1,0:T(8,128)}, u32[]{:S(2)}) copy-start(f32[512,512]{1,0:T(8,128)} %get-tuple-element.71) | copy-start | bytes 3145732
  544.5 5.6 %copy-start.13 = (f32[512,512]{1,0:T(8,128)S(1)}, f32[512,512]{1,0:T(8,128)}, u32[]{:S(2)}) copy-start(f32[512,512]{1,0:T(8,128)} %get-tuple-element.73) | copy-start | bytes 3145732
  544.5 5.6 %copy-start.15 = (f32[512,512]{1,0:T(8,128)S(1)}, f32[512,512]{1,0:T(8,128)}, u32[]{:S(2)}) copy-start(f32[512,512]{1,0:T(8,128)} %get-tuple-element.72) | copy-start | bytes 3145732
  (1 other events, 0.8 us)
